TPU v7x, 256 devices: a whole 4x4x8 slice. The times are simulated.
256 devices in a mesh: section: 8 (over z), dom: 32 (over x, y, core).
Axes of the slice: x: 4, y: 4, z: 8, core: 2. Of those that a mesh axis runs over, the one named last changes fastest.
Arguments:
- images: bfloat16 [8, 32, 65536], P('section', None, 'dom'), may hold values from -48 to 48
- weights: bfloat16 [16, 1024, 64, 256], P('section', 'dom'), may hold values from -0.625 to 0.625
- bias: bfloat16 [16, 65536], P('section', 'dom'), may hold values from -12 to 12
- pattern: int32 [16, 1024, 4], P('section'), may hold values from 0 to 1023, as said below
- counts: int32 [16, 1024], P('section', 'dom'), may hold values from 2 to 4, as said below
Outputs:
- scores: bfloat16 [8, 32, 65536], P('section', None, 'dom')
Inputs may be any that keep to these rules, and one draw needn't show every extreme that they name: `pattern`: A partition is the 32 consecutive column blocks of one neuron partition (and the row blocks of the same numbers). In each layer, slot 0 of every column block names a row block of its own partition; all slots of one partition's column blocks that name a row block of another partition name the same block of that partition, and every other partition is named so by slot 1 of some column block. Only the first counts[l, n] slots of a column block are live. In each layer every partition has a column block with all 4 slots live.
All inputs are finite; a program needn't handle non-finite values.
Results may differ from a plain program's by a relative error of at most 0.02.
Values may be sent and summed in bfloat16 or wider, within the bound.
No kernel may reach another device: no remote copies, remote signals or barrier semaphores. Data moves between devices by JAX's collectives and lax.ppermute only.
A program may use at most 128 MiB of HBM per device.

v0:
```python
import math

import jax
import jax.numpy as jnp
from jax import lax
from jax.sharding import PartitionSpec as P


def sent_together(arrays, axis, dim, along):
    widths = [math.prod(a.shape[along:]) for a in arrays]
    both = jnp.concatenate(
        [a.reshape(*a.shape[:along], w) for a, w in zip(arrays, widths)], axis=along
    )
    filled = lax.all_gather(both, axis, axis=dim, tiled=True)
    tiles = jnp.split(filled, [sum(widths[:k]) for k in range(1, len(widths))], axis=along)
    return tuple(
        (b.reshape(*filled.shape[:along], *a.shape[along:]) for a, b in zip(arrays, tiles))
    )


def prepare_tables(weights, pattern, counts, part_count, my_part):
    layer_count = weights.shape[0]
    per_part = weights.shape[1]
    block_size = weights.shape[2]
    slot_count = pattern.shape[2]
    block_table = pattern.reshape(layer_count, part_count, per_part * slot_count)
    owners = block_table // per_part
    wanted = jnp.max(jnp.where(owners == my_part, block_table % per_part, 0), axis=2)
    own_rows = lax.dynamic_slice_in_dim(pattern, my_part * per_part, per_part, 1)
    own_owners = own_rows // per_part
    source = jnp.where(own_owners == my_part, own_rows % per_part, per_part + own_owners)
    live_slots = (jnp.arange(slot_count)[None, None, :] < counts[:, :, None]).astype(weights.dtype)
    masked = (
        weights.reshape(layer_count, per_part, block_size, slot_count, block_size)
        * live_slots[:, :, None, :, None]
    )
    return (wanted, source, masked.reshape(weights.shape))


def apply_layer(current, wanted_row, layer_source, weight_layer, bias_row, part_count):
    image_rows = current.shape[0]
    local_width = current.shape[1]
    per_part = weight_layer.shape[0]
    block_size = weight_layer.shape[1]
    slot_count = layer_source.shape[1]
    blocks = current.reshape(image_rows, per_part, block_size)
    outgoing = jnp.take(blocks, wanted_row, axis=1).reshape(image_rows, part_count * block_size)
    arrived = lax.all_to_all(outgoing, "dom", split_axis=1, concat_axis=1, tiled=True)
    pooled = jnp.concatenate([blocks, arrived.reshape(image_rows, part_count, block_size)], axis=1)
    picked = jnp.take(pooled, layer_source.reshape(-1), axis=1)
    picked = picked.reshape(image_rows, per_part, slot_count * block_size)
    summed = jnp.einsum("bck,cok->bco", picked, weight_layer, preferred_element_type=jnp.float32)
    pre_act = summed.reshape(image_rows, local_width) + bias_row.astype(jnp.float32)[None, :]
    return jnp.clip(pre_act, 0.0, 32.0).astype(jnp.bfloat16)


def shards(images, weights, bias, pattern, counts):
    part_count = lax.axis_size("dom")
    my_part = lax.axis_index("dom")
    all_weights, all_bias = (
        lax.all_gather(weights, "section", axis=0, tiled=True),
        lax.all_gather(bias, "section", axis=0, tiled=True),
    )
    all_pattern, all_counts = sent_together((pattern, counts), "section", 0, 1)
    wanted, source, masked = prepare_tables(
        all_weights, all_pattern, all_counts, part_count, my_part
    )
    total_layers = all_weights.shape[0]

    def layer_turn(layer_idx, current):
        return apply_layer(
            current,
            wanted[layer_idx],
            source[layer_idx],
            masked[layer_idx],
            all_bias[layer_idx],
            part_count,
        )

    finished = lax.fori_loop(0, total_layers, layer_turn, images[0])
    return finished[None, :, :]


def solution(mesh):
    placed = (
        P("section", None, "dom"),
        P("section", "dom", None, None),
        P("section", "dom"),
        P("section", None, None),
        P("section", "dom"),
    )
    return jax.shard_map(
        shards, mesh=mesh, in_specs=placed, out_specs=P("section", None, "dom"), check_vma=False
    )
```

profile of v0, /device:TPU:1, one launch (start us, length us, event | category | flops | bytes accessed | tf_op | source)
XLA Modules:
  0.0 502.9 jit_solution(12406866687621141489)
XLA Ops:
  8.4 24.3 %all-gather = s32[8,2,4128]{2,1,0:T(2,128)S(1)} all-gather(s32[1,2,4128]{2,1,0:T(2,128)S(1)} %add_bitcast_fusion), channel_id=1, replica_groups=mesh['section'=8,'dom'=32] {'section'}, dimensions={0}, use_global_device_ids=true | all-gather | bytes 297216 | tf_op jit(solution)/shard_map/all_gather | solution.py:14
  37.3 22.0 %all-gather.1 = bf16[8,2,2048]{2,1,0:T(2,128)(2,1)S(1)} all-gather(bf16[1,2,2048]{2,1,0:T(2,128)(2,1)S(1)} %bitcast.63), channel_id=1, replica_groups=mesh['section'=8,'dom'=32] {'section'}, dimensions={0}, use_global_device_ids=true | all-gather | bytes 73728 | tf_op jit(solution)/shard_map/all_gather | solution.py:62
  59.3 127.9 %all-gather.4.cloned.1.call-done = bf16[16,32,64,256]{3,2,1,0:T(8,128)(2,1)} async-done(((bf16[2,32,64,256]{3,2,1,0:T(8,128)(2,1)}), bf16[16,32,64,256]{3,2,1,0:T(8,128)(2,1)}) %all-gather.4.cloned.1.call-update) | async-done | bytes 16777232 | tf_op jit(solution)/shard_map/all_gather | solution.py:61
  187.2 13.8 %broadcast_multiply_fusion = bf16[16,32,64,256]{3,2,1,0:T(8,128)(2,1)} fusion(bf16[16,32,64,256]{3,2,1,0:T(8,128)(2,1)} %all-gather.4.cloned.1.call-done, bf16[16,32,256]{2,1,0:T(8,128)(2,1)S(1)} %mul.17), kind=kLoop, calls=%fused_computation.24 | loop fusion | flops 8388608 | bytes 33816576 | tf_op jit(solution)/shard_map/mul | solution.py:34
  201.0 294.4 %while.13 = (s32[]{:T(128)}, bf16[32,2048]{1,0:T(8,128)(2,1)S(1)}, bf16[16,32,64,256]{3,2,1,0:T(8,128)(2,1)}, s32[16,32,4]{2,1,0:T(8,128)S(1)}, s32[16,32]{1,0:T...) while((s32[]{:T(128)}, bf16[32,2048]{1,0:T(8,128)(2,1)S(1)}, bf16[16,32,64,256]{3,2,1,0:T(8,128)(2,1)}, ...), condition=%wide.region_2.3_spmd, body=%wide.region_1.2_spmd.sunk | while | flops 34215328 | bytes 10029897 | solution.py:80
  203.0 7.7 %all-to-all-start = ((bf16[32,2,1024]{2,1,0:T(2,128)(2,1)}), bf16[32,2,1024]{2,1,0:T(2,128)(2,1)S(1)}, u32[]{:S(2)}, u32[]{:S(2)}) async-start(bf16[32,2,1024]{2,1,0:T(2,128)(2,1)} %reshape.172), calls=%async_computation | async-start | bytes 262144 | tf_op jit(solution)/shard_map/while/body/eval_jaxpr/all_to_all | solution.py:48
  211.2 7.1 %all-to-all-done = bf16[32,2,1024]{2,1,0:T(2,128)(2,1)S(1)} async-done(((bf16[32,2,1024]{2,1,0:T(2,128)(2,1)}), bf16[32,2,1024]{2,1,0:T(2,128)(2,1)S(1)}, u32[]{:S(2)}, u32[]{:S(2)}) %all-to-all-start) | async-done | bytes 131104 | tf_op jit(solution)/shard_map/while/body/eval_jaxpr/all_to_all | solution.py:48
  224.8 3.9 all-to-all-start
  229.3 7.2 %all-to-all-done = bf16[32,2,1024]{2,1,0:T(2,128)(2,1)S(1)} async-done(((bf16[32,2,1024]{2,1,0:T(2,128)(2,1)}), bf16[32,2,1024]{2,1,0:T(2,128)(2,1)S(1)}, u32[]{:S(2)}, u32[]{:S(2)}) %all-to-all-start) | async-done | bytes 131104 | tf_op jit(solution)/shard_map/while/body/eval_jaxpr/all_to_all | solution.py:48
  247.5 7.2 %all-to-all-done = bf16[32,2,1024]{2,1,0:T(2,128)(2,1)S(1)} async-done(((bf16[32,2,1024]{2,1,0:T(2,128)(2,1)}), bf16[32,2,1024]{2,1,0:T(2,128)(2,1)S(1)}, u32[]{:S(2)}, u32[]{:S(2)}) %all-to-all-start) | async-done | bytes 131104 | tf_op jit(solution)/shard_map/while/body/eval_jaxpr/all_to_all | solution.py:48
  261.2 3.9 all-to-all-start
  265.6 7.2 %all-to-all-done = bf16[32,2,1024]{2,1,0:T(2,128)(2,1)S(1)} async-done(((bf16[32,2,1024]{2,1,0:T(2,128)(2,1)}), bf16[32,2,1024]{2,1,0:T(2,128)(2,1)S(1)}, u32[]{:S(2)}, u32[]{:S(2)}) %all-to-all-start) | async-done | bytes 131104 | tf_op jit(solution)/shard_map/while/body/eval_jaxpr/all_to_all | solution.py:48
  279.3 3.9 all-to-all-start
  283.8 7.2 %all-to-all-done = bf16[32,2,1024]{2,1,0:T(2,128)(2,1)S(1)} async-done(((bf16[32,2,1024]{2,1,0:T(2,128)(2,1)}), bf16[32,2,1024]{2,1,0:T(2,128)(2,1)S(1)}, u32[]{:S(2)}, u32[]{:S(2)}) %all-to-all-start) | async-done | bytes 131104 | tf_op jit(solution)/shard_map/while/body/eval_jaxpr/all_to_all | solution.py:48
  302.0 7.2 %all-to-all-done = bf16[32,2,1024]{2,1,0:T(2,128)(2,1)S(1)} async-done(((bf16[32,2,1024]{2,1,0:T(2,128)(2,1)}), bf16[32,2,1024]{2,1,0:T(2,128)(2,1)S(1)}, u32[]{:S(2)}, u32[]{:S(2)}) %all-to-all-start) | async-done | bytes 131104 | tf_op jit(solution)/shard_map/while/body/eval_jaxpr/all_to_all | solution.py:48
  315.7 3.9 all-to-all-start
  320.2 7.2 %all-to-all-done = bf16[32,2,1024]{2,1,0:T(2,128)(2,1)S(1)} async-done(((bf16[32,2,1024]{2,1,0:T(2,128)(2,1)}), bf16[32,2,1024]{2,1,0:T(2,128)(2,1)S(1)}, u32[]{:S(2)}, u32[]{:S(2)}) %all-to-all-start) | async-done | bytes 131104 | tf_op jit(solution)/shard_map/while/body/eval_jaxpr/all_to_all | solution.py:48
  333.8 3.9 all-to-all-start
  338.3 7.2 %all-to-all-done = bf16[32,2,1024]{2,1,0:T(2,128)(2,1)S(1)} async-done(((bf16[32,2,1024]{2,1,0:T(2,128)(2,1)}), bf16[32,2,1024]{2,1,0:T(2,128)(2,1)S(1)}, u32[]{:S(2)}, u32[]{:S(2)}) %all-to-all-start) | async-done | bytes 131104 | tf_op jit(solution)/shard_map/while/body/eval_jaxpr/all_to_all | solution.py:48
  356.5 7.2 %all-to-all-done = bf16[32,2,1024]{2,1,0:T(2,128)(2,1)S(1)} async-done(((bf16[32,2,1024]{2,1,0:T(2,128)(2,1)}), bf16[32,2,1024]{2,1,0:T(2,128)(2,1)S(1)}, u32[]{:S(2)}, u32[]{:S(2)}) %all-to-all-start) | async-done | bytes 131104 | tf_op jit(solution)/shard_map/while/body/eval_jaxpr/all_to_all | solution.py:48
  370.2 3.9 all-to-all-start
  374.7 7.2 %all-to-all-done = bf16[32,2,1024]{2,1,0:T(2,128)(2,1)S(1)} async-done(((bf16[32,2,1024]{2,1,0:T(2,128)(2,1)}), bf16[32,2,1024]{2,1,0:T(2,128)(2,1)S(1)}, u32[]{:S(2)}, u32[]{:S(2)}) %all-to-all-start) | async-done | bytes 131104 | tf_op jit(solution)/shard_map/while/body/eval_jaxpr/all_to_all | solution.py:48
  388.4 3.9 all-to-all-start
  392.8 7.2 %all-to-all-done = bf16[32,2,1024]{2,1,0:T(2,128)(2,1)S(1)} async-done(((bf16[32,2,1024]{2,1,0:T(2,128)(2,1)}), bf16[32,2,1024]{2,1,0:T(2,128)(2,1)S(1)}, u32[]{:S(2)}, u32[]{:S(2)}) %all-to-all-start) | async-done | bytes 131104 | tf_op jit(solution)/shard_map/while/body/eval_jaxpr/all_to_all | solution.py:48
  406.5 3.9 all-to-all-start
  411.0 7.2 %all-to-all-done = bf16[32,2,1024]{2,1,0:T(2,128)(2,1)S(1)} async-done(((bf16[32,2,1024]{2,1,0:T(2,128)(2,1)}), bf16[32,2,1024]{2,1,0:T(2,128)(2,1)S(1)}, u32[]{:S(2)}, u32[]{:S(2)}) %all-to-all-start) | async-done | bytes 131104 | tf_op jit(solution)/shard_map/while/body/eval_jaxpr/all_to_all | solution.py:48
  424.7 3.9 all-to-all-start
  429.2 7.2 %all-to-all-done = bf16[32,2,1024]{2,1,0:T(2,128)(2,1)S(1)} async-done(((bf16[32,2,1024]{2,1,0:T(2,128)(2,1)}), bf16[32,2,1024]{2,1,0:T(2,128)(2,1)S(1)}, u32[]{:S(2)}, u32[]{:S(2)}) %all-to-all-start) | async-done | bytes 131104 | tf_op jit(solution)/shard_map/while/body/eval_jaxpr/all_to_all | solution.py:48
  447.4 7.2 %all-to-all-done = bf16[32,2,1024]{2,1,0:T(2,128)(2,1)S(1)} async-done(((bf16[32,2,1024]{2,1,0:T(2,128)(2,1)}), bf16[32,2,1024]{2,1,0:T(2,128)(2,1)S(1)}, u32[]{:S(2)}, u32[]{:S(2)}) %all-to-all-start) | async-done | bytes 131104 | tf_op jit(solution)/shard_map/while/body/eval_jaxpr/all_to_all | solution.py:48
  465.5 7.2 %all-to-all-done = bf16[32,2,1024]{2,1,0:T(2,128)(2,1)S(1)} async-done(((bf16[32,2,1024]{2,1,0:T(2,128)(2,1)}), bf16[32,2,1024]{2,1,0:T(2,128)(2,1)S(1)}, u32[]{:S(2)}, u32[]{:S(2)}) %all-to-all-start) | async-done | bytes 131104 | tf_op jit(solution)/shard_map/while/body/eval_jaxpr/all_to_all | solution.py:48
  479.2 3.9 all-to-all-start
  483.7 7.2 %all-to-all-done = bf16[32,2,1024]{2,1,0:T(2,128)(2,1)S(1)} async-done(((bf16[32,2,1024]{2,1,0:T(2,128)(2,1)}), bf16[32,2,1024]{2,1,0:T(2,128)(2,1)S(1)}, u32[]{:S(2)}, u32[]{:S(2)}) %all-to-all-start) | async-done | bytes 131104 | tf_op jit(solution)/shard_map/while/body/eval_jaxpr/all_to_all | solution.py:48
  (480 shorter events, 136.6 us)
Async XLA Ops:
  6.5 0.8 copy-start.2
  6.5 180.7 %all-gather.4.cloned.1.call-start = ((), (), s32[]{:S(2)}) async-start(), calls=%async_computation.1 | async-start | bytes 18874368 | tf_op jit(solution)/shard_map/all_gather | solution.py:61
  6.5 1.8 copy-start.4
  33.5 3.8 copy-start.3
  59.3 141.7 %copy-start.1 = (bf16[1,32,2048]{2,1,0:T(8,128)(2,1)S(1)}, bf16[1,32,2048]{2,1,0:T(8,128)(2,1)}, u32[]{:S(2)}) copy-start(bf16[1,32,2048]{2,1,0:T(8,128)(2,1)} %param.7) | copy-start | bytes 393220
  203.0 15.4 %all-to-all-start = ((bf16[32,2,1024]{2,1,0:T(2,128)(2,1)}), bf16[32,2,1024]{2,1,0:T(2,128)(2,1)S(1)}, u32[]{:S(2)}, u32[]{:S(2)}) async-start(bf16[32,2,1024]{2,1,0:T(2,128)(2,1)} %reshape.172), calls=%async_computation | async-start | bytes 262144 | tf_op jit(solution)/shard_map/while/body/eval_jaxpr/all_to_all | solution.py:48
  224.8 11.7 %all-to-all-start = ((bf16[32,2,1024]{2,1,0:T(2,128)(2,1)}), bf16[32,2,1024]{2,1,0:T(2,128)(2,1)S(1)}, u32[]{:S(2)}, u32[]{:S(2)}) async-start(bf16[32,2,1024]{2,1,0:T(2,128)(2,1)} %reshape.172), calls=%async_computation | async-start | bytes 262144 | tf_op jit(solution)/shard_map/while/body/eval_jaxpr/all_to_all | solution.py:48
  243.0 11.7 %all-to-all-start = ((bf16[32,2,1024]{2,1,0:T(2,128)(2,1)}), bf16[32,2,1024]{2,1,0:T(2,128)(2,1)S(1)}, u32[]{:S(2)}, u32[]{:S(2)}) async-start(bf16[32,2,1024]{2,1,0:T(2,128)(2,1)} %reshape.172), calls=%async_computation | async-start | bytes 262144 | tf_op jit(solution)/shard_map/while/body/eval_jaxpr/all_to_all | solution.py:48
  261.2 11.7 %all-to-all-start = ((bf16[32,2,1024]{2,1,0:T(2,128)(2,1)}), bf16[32,2,1024]{2,1,0:T(2,128)(2,1)S(1)}, u32[]{:S(2)}, u32[]{:S(2)}) async-start(bf16[32,2,1024]{2,1,0:T(2,128)(2,1)} %reshape.172), calls=%async_computation | async-start | bytes 262144 | tf_op jit(solution)/shard_map/while/body/eval_jaxpr/all_to_all | solution.py:48
  279.3 11.7 %all-to-all-start = ((bf16[32,2,1024]{2,1,0:T(2,128)(2,1)}), bf16[32,2,1024]{2,1,0:T(2,128)(2,1)S(1)}, u32[]{:S(2)}, u32[]{:S(2)}) async-start(bf16[32,2,1024]{2,1,0:T(2,128)(2,1)} %reshape.172), calls=%async_computation | async-start | bytes 262144 | tf_op jit(solution)/shard_map/while/body/eval_jaxpr/all_to_all | solution.py:48
  297.5 11.7 %all-to-all-start = ((bf16[32,2,1024]{2,1,0:T(2,128)(2,1)}), bf16[32,2,1024]{2,1,0:T(2,128)(2,1)S(1)}, u32[]{:S(2)}, u32[]{:S(2)}) async-start(bf16[32,2,1024]{2,1,0:T(2,128)(2,1)} %reshape.172), calls=%async_computation | async-start | bytes 262144 | tf_op jit(solution)/shard_map/while/body/eval_jaxpr/all_to_all | solution.py:48
  315.7 11.7 %all-to-all-start = ((bf16[32,2,1024]{2,1,0:T(2,128)(2,1)}), bf16[32,2,1024]{2,1,0:T(2,128)(2,1)S(1)}, u32[]{:S(2)}, u32[]{:S(2)}) async-start(bf16[32,2,1024]{2,1,0:T(2,128)(2,1)} %reshape.172), calls=%async_computation | async-start | bytes 262144 | tf_op jit(solution)/shard_map/while/body/eval_jaxpr/all_to_all | solution.py:48
  333.8 11.7 %all-to-all-start = ((bf16[32,2,1024]{2,1,0:T(2,128)(2,1)}), bf16[32,2,1024]{2,1,0:T(2,128)(2,1)S(1)}, u32[]{:S(2)}, u32[]{:S(2)}) async-start(bf16[32,2,1024]{2,1,0:T(2,128)(2,1)} %reshape.172), calls=%async_computation | async-start | bytes 262144 | tf_op jit(solution)/shard_map/while/body/eval_jaxpr/all_to_all | solution.py:48
  352.0 11.7 %all-to-all-start = ((bf16[32,2,1024]{2,1,0:T(2,128)(2,1)}), bf16[32,2,1024]{2,1,0:T(2,128)(2,1)S(1)}, u32[]{:S(2)}, u32[]{:S(2)}) async-start(bf16[32,2,1024]{2,1,0:T(2,128)(2,1)} %reshape.172), calls=%async_computation | async-start | bytes 262144 | tf_op jit(solution)/shard_map/while/body/eval_jaxpr/all_to_all | solution.py:48
  370.2 11.7 %all-to-all-start = ((bf16[32,2,1024]{2,1,0:T(2,128)(2,1)}), bf16[32,2,1024]{2,1,0:T(2,128)(2,1)S(1)}, u32[]{:S(2)}, u32[]{:S(2)}) async-start(bf16[32,2,1024]{2,1,0:T(2,128)(2,1)} %reshape.172), calls=%async_computation | async-start | bytes 262144 | tf_op jit(solution)/shard_map/while/body/eval_jaxpr/all_to_all | solution.py:48
  388.4 11.7 %all-to-all-start = ((bf16[32,2,1024]{2,1,0:T(2,128)(2,1)}), bf16[32,2,1024]{2,1,0:T(2,128)(2,1)S(1)}, u32[]{:S(2)}, u32[]{:S(2)}) async-start(bf16[32,2,1024]{2,1,0:T(2,128)(2,1)} %reshape.172), calls=%async_computation | async-start | bytes 262144 | tf_op jit(solution)/shard_map/while/body/eval_jaxpr/all_to_all | solution.py:48
  406.5 11.7 %all-to-all-start = ((bf16[32,2,1024]{2,1,0:T(2,128)(2,1)}), bf16[32,2,1024]{2,1,0:T(2,128)(2,1)S(1)}, u32[]{:S(2)}, u32[]{:S(2)}) async-start(bf16[32,2,1024]{2,1,0:T(2,128)(2,1)} %reshape.172), calls=%async_computation | async-start | bytes 262144 | tf_op jit(solution)/shard_map/while/body/eval_jaxpr/all_to_all | solution.py:48
  424.7 11.7 %all-to-all-start = ((bf16[32,2,1024]{2,1,0:T(2,128)(2,1)}), bf16[32,2,1024]{2,1,0:T(2,128)(2,1)S(1)}, u32[]{:S(2)}, u32[]{:S(2)}) async-start(bf16[32,2,1024]{2,1,0:T(2,128)(2,1)} %reshape.172), calls=%async_computation | async-start | bytes 262144 | tf_op jit(solution)/shard_map/while/body/eval_jaxpr/all_to_all | solution.py:48
  442.9 11.7 %all-to-all-start = ((bf16[32,2,1024]{2,1,0:T(2,128)(2,1)}), bf16[32,2,1024]{2,1,0:T(2,128)(2,1)S(1)}, u32[]{:S(2)}, u32[]{:S(2)}) async-start(bf16[32,2,1024]{2,1,0:T(2,128)(2,1)} %reshape.172), calls=%async_computation | async-start | bytes 262144 | tf_op jit(solution)/shard_map/while/body/eval_jaxpr/all_to_all | solution.py:48
  461.1 11.7 %all-to-all-start = ((bf16[32,2,1024]{2,1,0:T(2,128)(2,1)}), bf16[32,2,1024]{2,1,0:T(2,128)(2,1)S(1)}, u32[]{:S(2)}, u32[]{:S(2)}) async-start(bf16[32,2,1024]{2,1,0:T(2,128)(2,1)} %reshape.172), calls=%async_computation | async-start | bytes 262144 | tf_op jit(solution)/shard_map/while/body/eval_jaxpr/all_to_all | solution.py:48
  479.2 11.7 %all-to-all-start = ((bf16[32,2,1024]{2,1,0:T(2,128)(2,1)}), bf16[32,2,1024]{2,1,0:T(2,128)(2,1)S(1)}, u32[]{:S(2)}, u32[]{:S(2)}) async-start(bf16[32,2,1024]{2,1,0:T(2,128)(2,1)} %reshape.172), calls=%async_computation | async-start | bytes 262144 | tf_op jit(solution)/shard_map/while/body/eval_jaxpr/all_to_all | solution.py:48
  495.4 0.7 copy-start
Sparse Core Ops, SparseCore 0:
  9.1 178.0 all-gather.3
where the time goes:
time: 505 us; the launch traced here: 503 us
  waiting for transfers between devices  244 us (48%)
  local copies, waits for them, and re-layouts  81.4 us (16%)
  starting transfers between devices  66.3 us (13%)
  blocking collectives  46.3 us (9%)
  matrix products  26.9 us (5%)
  other arithmetic  21.9 us (4%)
  between operations  13.5 us (3%)
    all_gather x1, waiting for transfers between devices, shards(): lax.all_gather(weights, 'section', axis=0, tiled=True)  128 us
    all_to_all x16, waiting for transfers between devices, apply_layer(): lax.all_to_all(outgoing, 'dom', split_axis=1, concat_axis=1, tiled=True)  115 us
    all_to_all x16, starting transfers between devices, apply_layer(): lax.all_to_all(outgoing, 'dom', split_axis=1, concat_axis=1, tiled=True)  66.3 us
    gather x48, local copies, waits for them, and re-layouts, apply_layer(): picked = jnp.take(pooled, layer_source.reshape(-1), axis=1)  29.3 us
    dot_general x16, matrix products, apply_layer(): jnp.einsum('bck,cok->bco', picked, weight_layer, preferred_element_type=j...  26.9 us
    all_gather x1, blocking collectives, sent_together(): filled = lax.all_gather(both, axis, axis=dim, tiled=True)  24.3 us
    all_gather x1, blocking collectives, shards(): lax.all_gather(bias, 'section', axis=0, tiled=True)  22 us
    while x32, local copies, waits for them, and re-layouts  17.1 us
  transfers between devices with their start and end apart: 17, of which 17 were waited for; matrix products, arithmetic and copies ran while one was open for 3% of the time, Pallas kernels for 0%

commit v1 on v0

v1 whole, which is shorter than its diff:
```python
import jax
import jax.numpy as jnp
from jax import lax
from jax.experimental import pallas as pl
from jax.experimental.pallas import tpu as pltpu
from jax.sharding import PartitionSpec as P


def tables(bias, pattern, counts, parts, me):
    layers, columns, slots = pattern.shape
    per = columns // parts
    by_part = pattern.reshape(layers, parts, per * slots)
    wanted = jnp.max(jnp.where(by_part // per == me, by_part % per, 0), axis=2)
    own = lax.dynamic_slice_in_dim(pattern, me * per, per, 1)
    owner = own // per
    source = jnp.where(owner == me, own % per, per + owner)
    live = jnp.arange(slots)[None, None, :] < counts[:, :, None]
    source = jnp.where(live, source, per + parts)
    small = jnp.concatenate([source.reshape(layers, per * slots), wanted], axis=1)
    return jnp.concatenate([bias, small.astype(jnp.bfloat16)], axis=1)


def layer_kernel(layer, step, last, table, cur, arrived, bias, weights, *rest):
    if last:
        new, pool, held, sems = rest
    else:
        new, send, pool, held, sems = rest
    blocks, half, lanes = cur.shape
    parts = arrived.shape[0]
    pieces = held.shape[0]
    each = blocks // pieces
    size = lanes // 2
    slots = held.shape[2] // size

    def fetch(g):
        return pltpu.make_async_copy(weights.at[g, step], held.at[g], sems.at[g])

    for g in range(pieces):
        fetch(g).start()
    low = lax.broadcasted_iota(jnp.int32, (half, lanes), 1) < size

    def spread(tile, at):
        t = tile.astype(jnp.float32)
        r = pltpu.roll(t, size, 1)
        pool[at, 0:half, :] = jnp.where(low, t, r).astype(jnp.bfloat16)
        pool[at, half : 2 * half, :] = jnp.where(low, r, t).astype(jnp.bfloat16)

    for b in range(blocks):
        spread(cur[b], b)
    for q in range(parts):
        spread(arrived[q], blocks + q)
    pool[blocks + parts] = jnp.zeros((2 * half, lanes), jnp.bfloat16)
    low2 = lax.broadcasted_iota(jnp.int32, (2 * half, lanes), 1) < size

    def group(g, carry):
        fetch(g).wait()
        for b in range(each):
            n = g * each + b
            pairs = []
            for s in range(0, slots, 2):
                left = pool[table[layer, n * slots + s]]
                right = pool[table[layer, n * slots + s + 1]]
                pairs.append(jnp.where(low2, left, right))
            picked = jnp.concatenate(pairs, axis=1)
            acc = lax.dot_general(
                picked,
                held[g, b * size : (b + 1) * size, :],
                (((1,), (1,)), ((), ())),
                preferred_element_type=jnp.float32,
            )
            tile = jnp.concatenate([acc[0:half], acc[half : 2 * half]], axis=1)
            tile = tile + bias[layer, pl.ds(n, 1), :]
            new[n] = jnp.clip(tile, 0.0, 32.0).astype(jnp.bfloat16)
        return carry

    lax.fori_loop(0, pieces, group, 0)
    if not last:
        for q in range(parts):
            send[q] = new[table[layer + 1, blocks * slots + q]]


def apply_layer(layer, step, last, table, cur, arrived, bias, weights):
    pieces, _, rows, width = weights.shape
    tile = jax.ShapeDtypeStruct(cur.shape, cur.dtype)
    vmem = pl.BlockSpec(memory_space=pltpu.VMEM)
    blocks, half, lanes = cur.shape
    n_out = 1 if last else 2

    def body(*refs):
        layer_kernel(layer, step, last, *refs)

    out = pl.pallas_call(
        body,
        out_shape=[tile] * n_out,
        in_specs=[pl.BlockSpec(memory_space=pltpu.SMEM), vmem, vmem, vmem, pl.BlockSpec(memory_space=pl.ANY)],
        out_specs=[vmem] * n_out,
        scratch_shapes=[
            pltpu.VMEM((blocks + arrived.shape[0] + 1, 2 * half, lanes), jnp.bfloat16),
            pltpu.VMEM((pieces, rows, width), jnp.bfloat16),
            pltpu.SemaphoreType.DMA((pieces,)),
        ],
        name="layer",
    )(table, cur, arrived, bias, weights)
    return out if not last else (out[0], None)


def shards(images, weights, bias, pattern, counts):
    parts = lax.axis_size("dom")
    sections = lax.axis_size("section")
    me = lax.axis_index("dom")
    own_layers, blocks, size, width = weights.shape
    slots = pattern.shape[2]
    total = own_layers * sections
    rows = blocks // sections * size
    table = tables(bias, pattern, counts, parts, me)
    extra = 16
    table = jnp.pad(table, ((0, 0), (0, extra * width - table.shape[1])))
    table = table.reshape(own_layers, 1, extra, width)
    table = jnp.broadcast_to(table, (own_layers, sections, extra, width))
    both = jnp.concatenate([weights.reshape(own_layers, sections, rows, width), table], axis=2)
    scattered = lax.all_to_all(both, "section", split_axis=1, concat_axis=0, tiled=True)
    scattered = scattered.reshape(total, rows + extra, width)
    chunk = 4
    filled = [
        lax.all_gather(scattered[c : c + chunk, :rows], "section", axis=0, tiled=False)
        for c in range(0, total, chunk)
    ]
    flat = scattered[:, rows:].reshape(total, extra * width)
    all_bias = flat[:, : blocks * size].reshape(total, blocks, size).astype(jnp.float32)
    all_bias = jnp.concatenate([all_bias, all_bias], axis=2)
    table = flat[:, blocks * size : blocks * (size + slots) + parts].astype(jnp.int32)

    half = images.shape[1] // 2
    cur = images.reshape(2, half, blocks, size).transpose(2, 1, 0, 3).reshape(blocks, half, 2 * size)
    send = jnp.take(cur, table[0, blocks * slots :], axis=0)
    for layer in range(total):
        arrived = lax.all_to_all(send, "dom", split_axis=0, concat_axis=0, tiled=True)
        cur, send = apply_layer(
            layer, layer % chunk, layer == total - 1, table, cur, arrived, all_bias, filled[layer // chunk]
        )
    out = cur.reshape(blocks, half, 2, size).transpose(2, 1, 0, 3)
    return out.reshape(images.shape)


def solution(mesh):
    placed = (
        P("section", None, "dom"),
        P("section", "dom", None, None),
        P("section", "dom"),
        P("section", None, None),
        P("section", "dom"),
    )
    return jax.shard_map(
        shards, mesh=mesh, in_specs=placed, out_specs=P("section", None, "dom"), check_vma=False
    )
```

time: 505 us -> 402 us (0.80)
  waiting for transfers between devices: 244 us -> 63.3 us
  blocking collectives: 46.3 us -> 213 us
  Pallas kernels: 0 us -> 75.3 us
  local copies, waits for them, and re-layouts: 81.4 us -> 7.35 us
  starting transfers between devices: 66.3 us -> 21 us
  matrix products: 26.9 us -> 0 us
  other arithmetic: 21.9 us -> 5.84 us
    all_to_all x0 -> x13, blocking collectives: none -> 213 us  [the longest x12 152 us: shards(): lax.all_to_all(send, 'dom', split_axis=0, concat_axis=0, tiled=True)]
    all_gather x1 -> x4, waiting for transfers between devices: 128 us -> 31.5 us  [shards(): lax.all_gather(scattered[c:c + chunk, :rows], 'section', axis=0, tiled=Fa...]
    all_to_all x16 -> x4, waiting for transfers between devices: 115 us -> 29.9 us  [shards(): lax.all_to_all(send, 'dom', split_axis=0, concat_axis=0, tiled=True)]
    pallas_call x0 -> x16, Pallas kernels: none -> 75.3 us  [apply_layer(): pl.pallas_call(body, out_shape=[tile] * n_out, in_specs=[pl.BlockSpec(mem...]
    all_gather x2 -> x0, blocking collectives: 46.3 us -> none  [the longest x1 24.3 us: sent_together(): filled = lax.all_gather(both, axis, axis=dim, tiled=True)]
    all_to_all x16 -> x4, starting transfers between devices: 66.3 us -> 20.9 us  [shards(): lax.all_to_all(send, 'dom', split_axis=0, concat_axis=0, tiled=True)]
    gather x64 -> x1, local copies, waits for them, and re-layouts: 38.9 us -> 0.59 us  [shards(): send = jnp.take(cur, table[0, blocks * slots:], axis=0)]
    dot_general x16 -> x0, matrix products: 26.9 us -> none  [apply_layer(): jnp.einsum('bck,cok->bco', picked, weight_layer, preferred_element_type=j...]
  transfers between devices with their start and end apart: 17 -> 8, of which waited for: 17 -> 5; matrix products, arithmetic and copies ran while one was open for 3% -> 1% of each run, Pallas kernels for 0% -> 14%
where the time goes in v1:
time: 402 us; the launch traced here: 400 us
  blocking collectives  213 us (53%)
  Pallas kernels  75.3 us (19%)
  waiting for transfers between devices  63.3 us (16%)
  starting transfers between devices  21 us (5%)
  between operations  13.5 us (3%)
  local copies, waits for them, and re-layouts  7.35 us (2%)
  other arithmetic  5.84 us (1%)
    all_to_all x12, blocking collectives, shards(): lax.all_to_all(send, 'dom', split_axis=0, concat_axis=0, tiled=True)  152 us
    pallas_call x16, Pallas kernels, apply_layer(): pl.pallas_call(body, out_shape=[tile] * n_out, in_specs=[pl.BlockSpec(mem...  75.3 us
    all_to_all x1, blocking collectives, shards(): lax.all_to_all(both, 'section', split_axis=1, concat_axis=0, tiled=True)  61.7 us
    all_gather x4, waiting for transfers between devices, shards(): lax.all_gather(scattered[c:c + chunk, :rows], 'section', axis=0, tiled=Fa...  31.5 us
    all_to_all x4, waiting for transfers between devices, shards(): lax.all_to_all(send, 'dom', split_axis=0, concat_axis=0, tiled=True)  29.9 us
    all_to_all x4, starting transfers between devices, shards(): lax.all_to_all(send, 'dom', split_axis=0, concat_axis=0, tiled=True)  20.9 us
  transfers between devices with their start and end apart: 8, of which 5 were waited for; matrix products, arithmetic and copies ran while one was open for 1% of the time, Pallas kernels for 14%

profile of v1, /device:TPU:1, one launch (start us, length us, event | category | flops | bytes accessed | tf_op | source)
XLA Modules:
  0.0 399.6 jit_solution(5936497580314663484)
XLA Ops:
  11.3 61.7 %all_to_all.95 = bf16[2,8,272,256]{3,2,0,1:T(8,128)(2,1)S(1)} all-to-all(bf16[2,8,272,256]{3,2,0,1:T(8,128)(2,1)S(1)} %copy.21), channel_id=1, replica_groups=mesh['section'=8,'dom'=32] {'section'}, dimensions={1} | all-to-all | bytes 4456448 | tf_op jit(solution)/shard_map/all_to_all | solution.py:121
  78.6 9.1 %all-to-all-start.1 = ((bf16[32,16,128]{2,1,0:T(8,128)(2,1)}), bf16[32,16,128]{2,1,0:T(8,128)(2,1)S(1)}, u32[]{:S(2)}, u32[]{:S(2)}) async-start(bf16[32,16,128]{2,1,0:T(8,128)(2,1)} %broadcast_select_fusion), calls=%async_computation.1 | async-start | bytes 262144 | tf_op jit(solution)/shard_map/all_to_all | solution.py:137
  88.8 6.6 %all-to-all-done.1.refs_2_ = bf16[32,16,128]{2,1,0:T(8,128)(2,1)S(1)} async-done(((bf16[32,16,128]{2,1,0:T(8,128)(2,1)}), bf16[32,16,128]{2,1,0:T(8,128)(2,1)S(1)}, u32[]{:S(2)}, u32[]{:S(2)}) %all-to-all-start.1) | async-done | bytes 131104 | tf_op jit(solution)/shard_map/all_to_all | solution.py:137
  95.4 31.4 %all-gather.9.cloned.1.call-done = bf16[32,256,256]{2,1,0:T(8,128)(2,1)} async-done(((bf16[4,256,256]{2,1,0:T(8,128)(2,1)}), bf16[32,256,256]{2,1,0:T(8,128)(2,1)}) %all-gather.9.cloned.1.call-update) | async-done | bytes 4194320 | tf_op jit(solution)/shard_map/all_gather | solution.py:125
  126.9 4.7 %layer.16 = (bf16[32,16,128]{2,1,0:T(8,128)(2,1)}, bf16[32,16,128]{2,1,0:T(8,128)(2,1)}) custom-call(s32[16,160]{1,0:T(8,128)} %copy-done, bf16[32,16,128]{2,1,0:T(8,128)(2,1)} %copy-done.1, bf16[32,16,128]{2,1,0:T(8,128)(2,1)} %copy-done.2, f32[16,32,128]{2,1,0:T(8,128)} %maximum_convert_fusion.refs_3_, bf16[8,4,256,256]{3,2,1,0:T(8,128)(2,1)} %bitcast.40), custom_call_target="tpu_custom_call" | custom-call | tf_op jit(solution)/shard_map/layer/pallas_call | solution.py:92
  131.6 15.5 %all_to_all.96.refs_2_ = bf16[32,16,128]{2,1,0:T(8,128)(2,1)} all-to-all(bf16[32,16,128]{2,1,0:T(8,128)(2,1)} %get-tuple-element.36), channel_id=1, replica_groups=mesh['section'=8,'dom'=32] {'dom'}, dimensions={0} | all-to-all | bytes 262144 | tf_op jit(solution)/shard_map/all_to_all | solution.py:137
  147.0 4.7 %layer.17 = (bf16[32,16,128]{2,1,0:T(8,128)(2,1)}, bf16[32,16,128]{2,1,0:T(8,128)(2,1)}) custom-call(s32[16,160]{1,0:T(8,128)} %copy-done, bf16[32,16,128]{2,1,0:T(8,128)(2,1)} %get-tuple-element.35.refs_1_, bf16[32,16,128]{2,1,0:T(8,128)(2,1)} %all_to_all.96.refs_2_, f32[16,32,128]{2,1,0:T(8,128)} %maximum_convert_fusion.refs_3_, ...), custom_call_target="tpu_custom_call" | custom-call | tf_op jit(solution)/shard_map/layer/pallas_call | solution.py:92
  151.7 12.4 %all_to_all.97.refs_2_ = bf16[32,16,128]{2,1,0:T(8,128)(2,1)} all-to-all(bf16[32,16,128]{2,1,0:T(8,128)(2,1)} %get-tuple-element.38), channel_id=1, replica_groups=mesh['section'=8,'dom'=32] {'dom'}, dimensions={0} | all-to-all | bytes 262144 | tf_op jit(solution)/shard_map/all_to_all | solution.py:137
  164.1 4.7 %layer.18 = (bf16[32,16,128]{2,1,0:T(8,128)(2,1)}, bf16[32,16,128]{2,1,0:T(8,128)(2,1)}) custom-call(s32[16,160]{1,0:T(8,128)} %copy-done, bf16[32,16,128]{2,1,0:T(8,128)(2,1)} %get-tuple-element.37.refs_1_, bf16[32,16,128]{2,1,0:T(8,128)(2,1)} %all_to_all.97.refs_2_, f32[16,32,128]{2,1,0:T(8,128)} %maximum_convert_fusion.refs_3_, ...), custom_call_target="tpu_custom_call" | custom-call | tf_op jit(solution)/shard_map/layer/pallas_call | solution.py:92
  168.8 12.4 %all_to_all.98.refs_2_ = bf16[32,16,128]{2,1,0:T(8,128)(2,1)} all-to-all(bf16[32,16,128]{2,1,0:T(8,128)(2,1)} %get-tuple-element.40), channel_id=1, replica_groups=mesh['section'=8,'dom'=32] {'dom'}, dimensions={0} | all-to-all | bytes 262144 | tf_op jit(solution)/shard_map/all_to_all | solution.py:137
  189.8 7.8 %all-to-all-done.5.refs_2_ = bf16[32,16,128]{2,1,0:T(8,128)(2,1)S(1)} async-done(((bf16[32,16,128]{2,1,0:T(8,128)(2,1)}), bf16[32,16,128]{2,1,0:T(8,128)(2,1)S(1)}, u32[]{:S(2)}, u32[]{:S(2)}) %all-to-all-start.5) | async-done | bytes 131104 | tf_op jit(solution)/shard_map/all_to_all | solution.py:137
  198.3 4.7 %layer.20 = (bf16[32,16,128]{2,1,0:T(8,128)(2,1)}, bf16[32,16,128]{2,1,0:T(8,128)(2,1)}) custom-call(s32[16,160]{1,0:T(8,128)} %copy-done, bf16[32,16,128]{2,1,0:T(8,128)(2,1)} %get-tuple-element.41.refs_1_, bf16[32,16,128]{2,1,0:T(8,128)(2,1)} %copy-done.3, f32[16,32,128]{2,1,0:T(8,128)} %maximum_convert_fusion.refs_3_, bf16[8,4,256,256]{3,2,1,0:T(8,128)(2,1)} %bitcast.36), custom_call_target="tpu_custom_call" | custom-call | tf_op jit(solution)/shard_map/layer/pallas_call | solution.py:92
  203.0 12.4 %all_to_all.99.refs_2_ = bf16[32,16,128]{2,1,0:T(8,128)(2,1)} all-to-all(bf16[32,16,128]{2,1,0:T(8,128)(2,1)} %get-tuple-element.44), channel_id=1, replica_groups=mesh['section'=8,'dom'=32] {'dom'}, dimensions={0} | all-to-all | bytes 262144 | tf_op jit(solution)/shard_map/all_to_all | solution.py:137
  220.0 12.4 %all_to_all.100.refs_2_ = bf16[32,16,128]{2,1,0:T(8,128)(2,1)} all-to-all(bf16[32,16,128]{2,1,0:T(8,128)(2,1)} %get-tuple-element.46), channel_id=1, replica_groups=mesh['section'=8,'dom'=32] {'dom'}, dimensions={0} | all-to-all | bytes 262144 | tf_op jit(solution)/shard_map/all_to_all | solution.py:137
  232.4 4.7 %layer.22 = (bf16[32,16,128]{2,1,0:T(8,128)(2,1)}, bf16[32,16,128]{2,1,0:T(8,128)(2,1)}) custom-call(s32[16,160]{1,0:T(8,128)} %copy-done, bf16[32,16,128]{2,1,0:T(8,128)(2,1)} %get-tuple-element.45.refs_1_, bf16[32,16,128]{2,1,0:T(8,128)(2,1)} %all_to_all.100.refs_2_, f32[16,32,128]{2,1,0:T(8,128)} %maximum_convert_fusion.refs_3_, ...), custom_call_target="tpu_custom_call" | custom-call | tf_op jit(solution)/shard_map/layer/pallas_call | solution.py:92
  237.1 12.4 %all_to_all.101.refs_2_ = bf16[32,16,128]{2,1,0:T(8,128)(2,1)} all-to-all(bf16[32,16,128]{2,1,0:T(8,128)(2,1)} %get-tuple-element.48), channel_id=1, replica_groups=mesh['section'=8,'dom'=32] {'dom'}, dimensions={0} | all-to-all | bytes 262144 | tf_op jit(solution)/shard_map/all_to_all | solution.py:137
  249.5 4.7 %layer.23 = (bf16[32,16,128]{2,1,0:T(8,128)(2,1)}, bf16[32,16,128]{2,1,0:T(8,128)(2,1)}) custom-call(s32[16,160]{1,0:T(8,128)} %copy-done, bf16[32,16,128]{2,1,0:T(8,128)(2,1)} %get-tuple-element.47.refs_1_, bf16[32,16,128]{2,1,0:T(8,128)(2,1)} %all_to_all.101.refs_2_, f32[16,32,128]{2,1,0:T(8,128)} %maximum_convert_fusion.refs_3_, ...), custom_call_target="tpu_custom_call" | custom-call | tf_op jit(solution)/shard_map/layer/pallas_call | solution.py:92
  258.2 7.8 %all-to-all-done.9.refs_2_ = bf16[32,16,128]{2,1,0:T(8,128)(2,1)S(1)} async-done(((bf16[32,16,128]{2,1,0:T(8,128)(2,1)}), bf16[32,16,128]{2,1,0:T(8,128)(2,1)S(1)}, u32[]{:S(2)}, u32[]{:S(2)}) %all-to-all-start.9) | async-done | bytes 131104 | tf_op jit(solution)/shard_map/all_to_all | solution.py:137
  266.6 4.7 %layer.24 = (bf16[32,16,128]{2,1,0:T(8,128)(2,1)}, bf16[32,16,128]{2,1,0:T(8,128)(2,1)}) custom-call(s32[16,160]{1,0:T(8,128)} %copy-done, bf16[32,16,128]{2,1,0:T(8,128)(2,1)} %get-tuple-element.49.refs_1_, bf16[32,16,128]{2,1,0:T(8,128)(2,1)} %copy-done.4, f32[16,32,128]{2,1,0:T(8,128)} %maximum_convert_fusion.refs_3_, bf16[8,4,256,256]{3,2,1,0:T(8,128)(2,1)} %bitcast.32), custom_call_target="tpu_custom_call" | custom-call | tf_op jit(solution)/shard_map/layer/pallas_call | solution.py:92
  271.3 12.4 %all_to_all.102.refs_2_ = bf16[32,16,128]{2,1,0:T(8,128)(2,1)} all-to-all(bf16[32,16,128]{2,1,0:T(8,128)(2,1)} %get-tuple-element.52), channel_id=1, replica_groups=mesh['section'=8,'dom'=32] {'dom'}, dimensions={0} | all-to-all | bytes 262144 | tf_op jit(solution)/shard_map/all_to_all | solution.py:137
  283.7 4.7 %layer.25 = (bf16[32,16,128]{2,1,0:T(8,128)(2,1)}, bf16[32,16,128]{2,1,0:T(8,128)(2,1)}) custom-call(s32[16,160]{1,0:T(8,128)} %copy-done, bf16[32,16,128]{2,1,0:T(8,128)(2,1)} %get-tuple-element.51.refs_1_, bf16[32,16,128]{2,1,0:T(8,128)(2,1)} %all_to_all.102.refs_2_, f32[16,32,128]{2,1,0:T(8,128)} %maximum_convert_fusion.refs_3_, ...), custom_call_target="tpu_custom_call" | custom-call | tf_op jit(solution)/shard_map/layer/pallas_call | solution.py:92
  288.4 12.4 %all_to_all.103.refs_2_ = bf16[32,16,128]{2,1,0:T(8,128)(2,1)} all-to-all(bf16[32,16,128]{2,1,0:T(8,128)(2,1)} %get-tuple-element.54), channel_id=1, replica_groups=mesh['section'=8,'dom'=32] {'dom'}, dimensions={0} | all-to-all | bytes 262144 | tf_op jit(solution)/shard_map/all_to_all | solution.py:137
  300.8 4.7 %layer.26 = (bf16[32,16,128]{2,1,0:T(8,128)(2,1)}, bf16[32,16,128]{2,1,0:T(8,128)(2,1)}) custom-call(s32[16,160]{1,0:T(8,128)} %copy-done, bf16[32,16,128]{2,1,0:T(8,128)(2,1)} %get-tuple-element.53.refs_1_, bf16[32,16,128]{2,1,0:T(8,128)(2,1)} %all_to_all.103.refs_2_, f32[16,32,128]{2,1,0:T(8,128)} %maximum_convert_fusion.refs_3_, ...), custom_call_target="tpu_custom_call" | custom-call | tf_op jit(solution)/shard_map/layer/pallas_call | solution.py:92
  305.5 12.4 %all_to_all.104.refs_2_ = bf16[32,16,128]{2,1,0:T(8,128)(2,1)} all-to-all(bf16[32,16,128]{2,1,0:T(8,128)(2,1)} %get-tuple-element.56), channel_id=1, replica_groups=mesh['section'=8,'dom'=32] {'dom'}, dimensions={0} | all-to-all | bytes 262144 | tf_op jit(solution)/shard_map/all_to_all | solution.py:137
  317.9 4.7 %layer.27 = (bf16[32,16,128]{2,1,0:T(8,128)(2,1)}, bf16[32,16,128]{2,1,0:T(8,128)(2,1)}) custom-call(s32[16,160]{1,0:T(8,128)} %copy-done, bf16[32,16,128]{2,1,0:T(8,128)(2,1)} %get-tuple-element.55.refs_1_, bf16[32,16,128]{2,1,0:T(8,128)(2,1)} %all_to_all.104.refs_2_, f32[16,32,128]{2,1,0:T(8,128)} %maximum_convert_fusion.refs_3_, ...), custom_call_target="tpu_custom_call" | custom-call | tf_op jit(solution)/shard_map/layer/pallas_call | solution.py:92
  326.6 7.8 %all-to-all-done.13.refs_2_ = bf16[32,16,128]{2,1,0:T(8,128)(2,1)S(1)} async-done(((bf16[32,16,128]{2,1,0:T(8,128)(2,1)}), bf16[32,16,128]{2,1,0:T(8,128)(2,1)S(1)}, u32[]{:S(2)}, u32[]{:S(2)}) %all-to-all-start.13) | async-done | bytes 131104 | tf_op jit(solution)/shard_map/all_to_all | solution.py:137
  335.0 4.7 %layer.28 = (bf16[32,16,128]{2,1,0:T(8,128)(2,1)}, bf16[32,16,128]{2,1,0:T(8,128)(2,1)}) custom-call(s32[16,160]{1,0:T(8,128)} %copy-done, bf16[32,16,128]{2,1,0:T(8,128)(2,1)} %get-tuple-element.57.refs_1_, bf16[32,16,128]{2,1,0:T(8,128)(2,1)} %copy-done.5, f32[16,32,128]{2,1,0:T(8,128)} %maximum_convert_fusion.refs_3_, bf16[8,4,256,256]{3,2,1,0:T(8,128)(2,1)} %bitcast.28), custom_call_target="tpu_custom_call" | custom-call | tf_op jit(solution)/shard_map/layer/pallas_call | solution.py:92
  339.7 12.4 %all_to_all.105.refs_2_ = bf16[32,16,128]{2,1,0:T(8,128)(2,1)} all-to-all(bf16[32,16,128]{2,1,0:T(8,128)(2,1)} %get-tuple-element.60), channel_id=1, replica_groups=mesh['section'=8,'dom'=32] {'dom'}, dimensions={0} | all-to-all | bytes 262144 | tf_op jit(solution)/shard_map/all_to_all | solution.py:137
  352.1 4.7 %layer.29 = (bf16[32,16,128]{2,1,0:T(8,128)(2,1)}, bf16[32,16,128]{2,1,0:T(8,128)(2,1)}) custom-call(s32[16,160]{1,0:T(8,128)} %copy-done, bf16[32,16,128]{2,1,0:T(8,128)(2,1)} %get-tuple-element.59.refs_1_, bf16[32,16,128]{2,1,0:T(8,128)(2,1)} %all_to_all.105.refs_2_, f32[16,32,128]{2,1,0:T(8,128)} %maximum_convert_fusion.refs_3_, ...), custom_call_target="tpu_custom_call" | custom-call | tf_op jit(solution)/shard_map/layer/pallas_call | solution.py:92
  356.8 12.4 %all_to_all.106.refs_2_ = bf16[32,16,128]{2,1,0:T(8,128)(2,1)} all-to-all(bf16[32,16,128]{2,1,0:T(8,128)(2,1)} %get-tuple-element.62), channel_id=1, replica_groups=mesh['section'=8,'dom'=32] {'dom'}, dimensions={0} | all-to-all | bytes 262144 | tf_op jit(solution)/shard_map/all_to_all | solution.py:137
  369.2 4.7 %layer.30 = (bf16[32,16,128]{2,1,0:T(8,128)(2,1)}, bf16[32,16,128]{2,1,0:T(8,128)(2,1)}) custom-call(s32[16,160]{1,0:T(8,128)} %copy-done, bf16[32,16,128]{2,1,0:T(8,128)(2,1)} %get-tuple-element.61.refs_1_, bf16[32,16,128]{2,1,0:T(8,128)(2,1)} %all_to_all.106.refs_2_, f32[16,32,128]{2,1,0:T(8,128)} %maximum_convert_fusion.refs_3_, ...), custom_call_target="tpu_custom_call" | custom-call | tf_op jit(solution)/shard_map/layer/pallas_call | solution.py:92
  373.9 12.4 %all_to_all.107.refs_2_ = bf16[32,16,128]{2,1,0:T(8,128)(2,1)} all-to-all(bf16[32,16,128]{2,1,0:T(8,128)(2,1)} %get-tuple-element.64), channel_id=1, replica_groups=mesh['section'=8,'dom'=32] {'dom'}, dimensions={0} | all-to-all | bytes 262144 | tf_op jit(solution)/shard_map/all_to_all | solution.py:137
  (61 shorter events, 41.0 us)
Async XLA Ops:
  6.5 120.3 %all-gather.9.cloned.1.call-start = ((), (), s32[]{:S(2)}) async-start(), calls=%async_computation.17 | async-start | bytes 4718592 | tf_op jit(solution)/shard_map/all_gather | solution.py:125
  73.0 3.4 copy-start.6
  74.4 115.5 %all-gather.11.cloned.1.call-start = ((), (), s32[]{:S(2)}) async-start(), calls=%async_computation.18 | async-start | bytes 4718592 | tf_op jit(solution)/shard_map/all_gather | solution.py:125
  75.1 183.0 %all-gather.13.cloned.1.call-start = ((), (), s32[]{:S(2)}) async-start(), calls=%async_computation.19 | async-start | bytes 4718592 | tf_op jit(solution)/shard_map/all_gather | solution.py:125
  75.9 250.7 %all-gather.15.cloned.1.call-start = ((), (), s32[]{:S(2)}) async-start(), calls=%async_computation.20 | async-start | bytes 4718592 | tf_op jit(solution)/shard_map/all_gather | solution.py:125
  77.1 49.7 %copy-start.1 = (bf16[32,16,128]{2,1,0:T(8,128)(2,1)}, bf16[32,16,128]{2,1,0:T(8,128)(2,1)S(1)}, u32[]{:S(2)}) copy-start(bf16[32,16,128]{2,1,0:T(8,128)(2,1)S(1)} %reshape.73.refs_1_) | copy-start | bytes 393220
  77.2 49.6 %copy-start = (s32[16,160]{1,0:T(8,128)}, s32[16,160]{1,0:T(8,128)S(1)}, u32[]{:S(2)}) copy-start(s32[16,160]{1,0:T(8,128)S(1)} %slice_convert_fusion.refs_0_) | copy-start | bytes 30724
  78.6 16.8 %all-to-all-start.1 = ((bf16[32,16,128]{2,1,0:T(8,128)(2,1)}), bf16[32,16,128]{2,1,0:T(8,128)(2,1)S(1)}, u32[]{:S(2)}, u32[]{:S(2)}) async-start(bf16[32,16,128]{2,1,0:T(8,128)(2,1)} %broadcast_select_fusion), calls=%async_computation.1 | async-start | bytes 262144 | tf_op jit(solution)/shard_map/all_to_all | solution.py:137
  95.4 31.4 %copy-start.2 = (bf16[32,16,128]{2,1,0:T(8,128)(2,1)}, bf16[32,16,128]{2,1,0:T(8,128)(2,1)S(1)}, u32[]{:S(2)}) copy-start(bf16[32,16,128]{2,1,0:T(8,128)(2,1)S(1)} %all-to-all-done.1.refs_2_) | copy-start | bytes 393220
  185.9 11.7 %all-to-all-start.5 = ((bf16[32,16,128]{2,1,0:T(8,128)(2,1)}), bf16[32,16,128]{2,1,0:T(8,128)(2,1)S(1)}, u32[]{:S(2)}, u32[]{:S(2)}) async-start(bf16[32,16,128]{2,1,0:T(8,128)(2,1)} %get-tuple-element.42), calls=%async_computation.5 | async-start | bytes 262144 | tf_op jit(solution)/shard_map/all_to_all | solution.py:137
  197.6 0.7 copy-start.3
  254.2 11.7 %all-to-all-start.9 = ((bf16[32,16,128]{2,1,0:T(8,128)(2,1)}), bf16[32,16,128]{2,1,0:T(8,128)(2,1)S(1)}, u32[]{:S(2)}, u32[]{:S(2)}) async-start(bf16[32,16,128]{2,1,0:T(8,128)(2,1)} %get-tuple-element.50), calls=%async_computation.9 | async-start | bytes 262144 | tf_op jit(solution)/shard_map/all_to_all | solution.py:137
  265.9 0.7 copy-start.4
  322.6 11.7 %all-to-all-start.13 = ((bf16[32,16,128]{2,1,0:T(8,128)(2,1)}), bf16[32,16,128]{2,1,0:T(8,128)(2,1)S(1)}, u32[]{:S(2)}, u32[]{:S(2)}) async-start(bf16[32,16,128]{2,1,0:T(8,128)(2,1)} %get-tuple-element.58), calls=%async_computation.13 | async-start | bytes 262144 | tf_op jit(solution)/shard_map/all_to_all | solution.py:137
  334.3 0.6 copy-start.5
Sparse Core Ops, SparseCore 0:
  74.5 52.2 all-gather.8
  128.6 53.3 all-gather.10
  183.8 53.3 all-gather.12
  238.8 53.3 all-gather.14

commit v2 on v1

--- a/solution.py
+++ b/solution.py
@@ -20,23 +20,15 @@
     return jnp.concatenate([bias, small.astype(jnp.bfloat16)], axis=1)
 
 
-def layer_kernel(layer, step, last, table, cur, arrived, bias, weights, *rest):
+def layer_kernel(layer, last, table, cur, arrived, bias, weights, *rest):
     if last:
-        new, pool, held, sems = rest
+        new, pool = rest
     else:
-        new, send, pool, held, sems = rest
+        new, send, pool = rest
     blocks, half, lanes = cur.shape
     parts = arrived.shape[0]
-    pieces = held.shape[0]
-    each = blocks // pieces
     size = lanes // 2
-    slots = held.shape[2] // size
-
-    def fetch(g):
-        return pltpu.make_async_copy(weights.at[g, step], held.at[g], sems.at[g])
-
-    for g in range(pieces):
-        fetch(g).start()
+    slots = weights.shape[2] // size
     low = lax.broadcasted_iota(jnp.int32, (half, lanes), 1) < size
 
     def spread(tile, at):
@@ -52,55 +44,52 @@
     pool[blocks + parts] = jnp.zeros((2 * half, lanes), jnp.bfloat16)
     low2 = lax.broadcasted_iota(jnp.int32, (2 * half, lanes), 1) < size
 
-    def group(g, carry):
-        fetch(g).wait()
-        for b in range(each):
-            n = g * each + b
-            pairs = []
-            for s in range(0, slots, 2):
-                left = pool[table[layer, n * slots + s]]
-                right = pool[table[layer, n * slots + s + 1]]
-                pairs.append(jnp.where(low2, left, right))
-            picked = jnp.concatenate(pairs, axis=1)
-            acc = lax.dot_general(
-                picked,
-                held[g, b * size : (b + 1) * size, :],
-                (((1,), (1,)), ((), ())),
-                preferred_element_type=jnp.float32,
-            )
-            tile = jnp.concatenate([acc[0:half], acc[half : 2 * half]], axis=1)
-            tile = tile + bias[layer, pl.ds(n, 1), :]
-            new[n] = jnp.clip(tile, 0.0, 32.0).astype(jnp.bfloat16)
+    def column(n, carry):
+        pairs = []
+        for s in range(0, slots, 2):
+            left = pool[table[layer, n * slots + s]]
+            right = pool[table[layer, n * slots + s + 1]]
+            pairs.append(jnp.where(low2, left, right))
+        acc = lax.dot_general(
+            jnp.concatenate(pairs, axis=1),
+            weights[n],
+            (((1,), (1,)), ((), ())),
+            preferred_element_type=jnp.float32,
+        )
+        tile = jnp.concatenate([acc[0:half], acc[half : 2 * half]], axis=1)
+        tile = tile + bias[layer, pl.ds(n, 1), :]
+        new[n] = jnp.clip(tile, 0.0, 32.0).astype(jnp.bfloat16)
         return carry
 
-    lax.fori_loop(0, pieces, group, 0)
+    lax.fori_loop(0, blocks, column, 0, unroll=16)
     if not last:
         for q in range(parts):
             send[q] = new[table[layer + 1, blocks * slots + q]]
 
 
-def apply_layer(layer, step, last, table, cur, arrived, bias, weights):
-    pieces, _, rows, width = weights.shape
-    tile = jax.ShapeDtypeStruct(cur.shape, cur.dtype)
+def on_chip(x):
+    return pltpu.with_memory_space_constraint(x, pltpu.VMEM)
+
+
+def apply_layer(layer, last, table, cur, arrived, bias, weights):
+    tile = pltpu.VMEM(cur.shape, cur.dtype)
     vmem = pl.BlockSpec(memory_space=pltpu.VMEM)
     blocks, half, lanes = cur.shape
     n_out = 1 if last else 2
 
     def body(*refs):
-        layer_kernel(layer, step, last, *refs)
+        layer_kernel(layer, last, *refs)
 
     out = pl.pallas_call(
         body,
         out_shape=[tile] * n_out,
-        in_specs=[pl.BlockSpec(memory_space=pltpu.SMEM), vmem, vmem, vmem, pl.BlockSpec(memory_space=pl.ANY)],
+        in_specs=[pl.BlockSpec(memory_space=pltpu.SMEM), vmem, vmem, vmem, vmem],
         out_specs=[vmem] * n_out,
         scratch_shapes=[
             pltpu.VMEM((blocks + arrived.shape[0] + 1, 2 * half, lanes), jnp.bfloat16),
-            pltpu.VMEM((pieces, rows, width), jnp.bfloat16),
-            pltpu.SemaphoreType.DMA((pieces,)),
         ],
         name="layer",
-    )(table, cur, arrived, bias, weights)
+    )(table, on_chip(cur), on_chip(arrived), on_chip(bias), on_chip(weights))
     return out if not last else (out[0], None)
 
 
@@ -135,9 +124,8 @@
     send = jnp.take(cur, table[0, blocks * slots :], axis=0)
     for layer in range(total):
         arrived = lax.all_to_all(send, "dom", split_axis=0, concat_axis=0, tiled=True)
-        cur, send = apply_layer(
-            layer, layer % chunk, layer == total - 1, table, cur, arrived, all_bias, filled[layer // chunk]
-        )
+        held = filled[layer // chunk][:, layer % chunk].reshape(blocks, size, width)
+        cur, send = apply_layer(layer, layer == total - 1, table, cur, arrived, all_bias, held)
     out = cur.reshape(blocks, half, 2, size).transpose(2, 1, 0, 3)
     return out.reshape(images.shape)
 

time: 402 us -> 356 us (0.89)
  Pallas kernels: 75.3 us -> 31 us
  local copies, waits for them, and re-layouts: 7.35 us -> 29.7 us
  blocking collectives: 213 us -> 201 us
  waiting for transfers between devices: 63.3 us -> 52.4 us
    pallas_call x16, Pallas kernels: 75.3 us -> 31 us  [apply_layer(): pl.pallas_call(body, out_shape=[tile] * n_out, in_specs=[pl.BlockSpec(mem...]
    all_to_all x4, waiting for transfers between devices: 29.9 us -> 11.7 us  [shards(): lax.all_to_all(send, 'dom', split_axis=0, concat_axis=0, tiled=True)]
    slice x0 -> x4, local copies, waits for them, and re-layouts: none -> 15.5 us  [shards(): held = filled[layer // chunk][:, layer % chunk].reshape(blocks, size, width)]
    all_to_all x12, blocking collectives: 152 us -> 139 us  [shards(): lax.all_to_all(send, 'dom', split_axis=0, concat_axis=0, tiled=True)]
    unnamed x16 -> x22, local copies, waits for them, and re-layouts: 2.02 us -> 9.91 us
    all_gather x4, waiting for transfers between devices: 31.5 us -> 38.8 us  [shards(): lax.all_gather(scattered[c:c + chunk, :rows], 'section', axis=0, tiled=Fa...]
  transfers between devices with their start and end apart: 8 -> 8, of which waited for: 5 -> 4; matrix products, arithmetic and copies ran while one was open for 1% -> 5% of each run, Pallas kernels for 14% -> 7%
where the time goes in v2:
time: 356 us; the launch traced here: 353 us
  blocking collectives  201 us (56%)
  waiting for transfers between devices  52.4 us (15%)
  Pallas kernels  31 us (9%)
  local copies, waits for them, and re-layouts  29.7 us (8%)
  starting transfers between devices  21 us (6%)
  between operations  13.5 us (4%)
  other arithmetic  5.15 us (1%)
    all_to_all x12, blocking collectives, shards(): lax.all_to_all(send, 'dom', split_axis=0, concat_axis=0, tiled=True)  139 us
    all_to_all x1, blocking collectives, shards(): lax.all_to_all(both, 'section', split_axis=1, concat_axis=0, tiled=True)  61.7 us
    all_gather x4, waiting for transfers between devices, shards(): lax.all_gather(scattered[c:c + chunk, :rows], 'section', axis=0, tiled=Fa...  38.8 us
    pallas_call x16, Pallas kernels, apply_layer(): pl.pallas_call(body, out_shape=[tile] * n_out, in_specs=[pl.BlockSpec(mem...  31 us
    all_to_all x4, starting transfers between devices, shards(): lax.all_to_all(send, 'dom', split_axis=0, concat_axis=0, tiled=True)  20.9 us
    slice x4, local copies, waits for them, and re-layouts, shards(): held = filled[layer // chunk][:, layer % chunk].reshape(blocks, size, width)  15.5 us
    all_to_all x4, waiting for transfers between devices, shards(): lax.all_to_all(send, 'dom', split_axis=0, concat_axis=0, tiled=True)  11.7 us
    unnamed x22, local copies, waits for them, and re-layouts  9.91 us
  transfers between devices with their start and end apart: 8, of which 4 were waited for; matrix products, arithmetic and copies ran while one was open for 5% of the time, Pallas kernels for 7%

profile of v2, /device:TPU:1, one launch (start us, length us, event | category | flops | bytes accessed | tf_op | source)
XLA Modules:
  0.0 353.2 jit_solution(11401809411496086215)
XLA Ops:
  11.2 61.7 %all_to_all.95 = bf16[2,8,272,256]{3,2,0,1:T(8,128)(2,1)S(1)} all-to-all(bf16[2,8,272,256]{3,2,0,1:T(8,128)(2,1)S(1)} %pad_maximum_fusion), channel_id=1, replica_groups=mesh['section'=8,'dom'=32] {'section'}, dimensions={1} | all-to-all | bytes 4456448 | tf_op jit(solution)/shard_map/all_to_all | solution.py:110
  78.5 9.1 %all-to-all-start.1 = ((bf16[32,16,128]{2,1,0:T(8,128)(2,1)}), bf16[32,16,128]{2,1,0:T(8,128)(2,1)S(1)}, u32[]{:S(2)}, u32[]{:S(2)}) async-start(bf16[32,16,128]{2,1,0:T(8,128)(2,1)} %broadcast_select_fusion), calls=%async_computation.1 | async-start | bytes 262144 | tf_op jit(solution)/shard_map/all_to_all | solution.py:126
  87.9 38.8 %all-gather.9.cloned.1.call-done = bf16[32,256,256]{2,1,0:T(8,128)(2,1)} async-done(((bf16[4,256,256]{2,1,0:T(8,128)(2,1)}), bf16[32,256,256]{2,1,0:T(8,128)(2,1)}) %all-gather.9.cloned.1.call-update) | async-done | bytes 4194320 | tf_op jit(solution)/shard_map/all_gather | solution.py:114
  126.7 3.9 %fusion.17 = (bf16[8,1,256,256]{3,2,1,0:T(8,128)(2,1)S(1)}, bf16[8,1,256,256]{3,2,1,0:T(8,128)(2,1)}, bf16[8,1,256,256]{3,2,1,0:T(8,128)(2,1)}, bf16[8,1,256,256]{3,2,1,0:T(8,128)(2,1)S(1)}) fusion(bf16[8,4,256,256]{3,2,1,0:T(8,128)(2,1)} %bitcast.95), kind=kLoop, calls=%fused_computation.42 | loop fusion | bytes 8388608 | tf_op jit(solution)/shard_map/slice | solution.py:127
  132.4 15.2 %all_to_all.96.refs_2_ = bf16[32,16,128]{2,1,0:T(8,128)(2,1)S(1)} all-to-all(bf16[32,16,128]{2,1,0:T(8,128)(2,1)S(1)} %get-tuple-element.36), channel_id=1, replica_groups=mesh['section'=8,'dom'=32] {'dom'}, dimensions={0} | all-to-all | bytes 262144 | tf_op jit(solution)/shard_map/all_to_all | solution.py:126
  150.6 11.2 %all_to_all.97.refs_2_ = bf16[32,16,128]{2,1,0:T(8,128)(2,1)S(1)} all-to-all(bf16[32,16,128]{2,1,0:T(8,128)(2,1)S(1)} %get-tuple-element.38), channel_id=1, replica_groups=mesh['section'=8,'dom'=32] {'dom'}, dimensions={0} | all-to-all | bytes 262144 | tf_op jit(solution)/shard_map/all_to_all | solution.py:126
  164.9 11.3 %all_to_all.98.refs_2_ = bf16[32,16,128]{2,1,0:T(8,128)(2,1)S(1)} all-to-all(bf16[32,16,128]{2,1,0:T(8,128)(2,1)S(1)} %get-tuple-element.40), channel_id=1, replica_groups=mesh['section'=8,'dom'=32] {'dom'}, dimensions={0} | all-to-all | bytes 262144 | tf_op jit(solution)/shard_map/all_to_all | solution.py:126
  176.1 2.5 layer.19
  178.6 3.9 %all-to-all-start.5 = ((bf16[32,16,128]{2,1,0:T(8,128)(2,1)}), bf16[32,16,128]{2,1,0:T(8,128)(2,1)S(1)}, u32[]{:S(2)}, u32[]{:S(2)}) async-start(bf16[32,16,128]{2,1,0:T(8,128)(2,1)} %get-tuple-element.42), calls=%async_computation.5 | async-start | bytes 262144 | tf_op jit(solution)/shard_map/all_to_all | solution.py:126
  182.5 3.8 %fusion.16 = (bf16[8,1,256,256]{3,2,1,0:T(8,128)(2,1)S(1)}, bf16[8,1,256,256]{3,2,1,0:T(8,128)(2,1)}, bf16[8,1,256,256]{3,2,1,0:T(8,128)(2,1)}, bf16[8,1,256,256]{3,2,1,0:T(8,128)(2,1)S(1)}) fusion(bf16[8,4,256,256]{3,2,1,0:T(8,128)(2,1)} %bitcast.94), kind=kLoop, calls=%fused_computation.41 | loop fusion | bytes 8388608 | tf_op jit(solution)/shard_map/slice | solution.py:127
  186.4 3.9 %all-to-all-done.5.refs_2_ = bf16[32,16,128]{2,1,0:T(8,128)(2,1)S(1)} async-done(((bf16[32,16,128]{2,1,0:T(8,128)(2,1)}), bf16[32,16,128]{2,1,0:T(8,128)(2,1)S(1)}, u32[]{:S(2)}, u32[]{:S(2)}) %all-to-all-start.5) | async-done | bytes 131104 | tf_op jit(solution)/shard_map/all_to_all | solution.py:126
  192.1 11.2 %all_to_all.99.refs_2_ = bf16[32,16,128]{2,1,0:T(8,128)(2,1)S(1)} all-to-all(bf16[32,16,128]{2,1,0:T(8,128)(2,1)S(1)} %get-tuple-element.44), channel_id=1, replica_groups=mesh['section'=8,'dom'=32] {'dom'}, dimensions={0} | all-to-all | bytes 262144 | tf_op jit(solution)/shard_map/all_to_all | solution.py:126
  206.4 11.2 %all_to_all.100.refs_2_ = bf16[32,16,128]{2,1,0:T(8,128)(2,1)S(1)} all-to-all(bf16[32,16,128]{2,1,0:T(8,128)(2,1)S(1)} %get-tuple-element.46), channel_id=1, replica_groups=mesh['section'=8,'dom'=32] {'dom'}, dimensions={0} | all-to-all | bytes 262144 | tf_op jit(solution)/shard_map/all_to_all | solution.py:126
  220.7 11.2 %all_to_all.101.refs_2_ = bf16[32,16,128]{2,1,0:T(8,128)(2,1)S(1)} all-to-all(bf16[32,16,128]{2,1,0:T(8,128)(2,1)S(1)} %get-tuple-element.48), channel_id=1, replica_groups=mesh['section'=8,'dom'=32] {'dom'}, dimensions={0} | all-to-all | bytes 262144 | tf_op jit(solution)/shard_map/all_to_all | solution.py:126
  231.9 2.5 layer.23
  234.4 3.9 %all-to-all-start.9 = ((bf16[32,16,128]{2,1,0:T(8,128)(2,1)}), bf16[32,16,128]{2,1,0:T(8,128)(2,1)S(1)}, u32[]{:S(2)}, u32[]{:S(2)}) async-start(bf16[32,16,128]{2,1,0:T(8,128)(2,1)} %get-tuple-element.50), calls=%async_computation.9 | async-start | bytes 262144 | tf_op jit(solution)/shard_map/all_to_all | solution.py:126
  238.3 3.9 %fusion.15 = (bf16[8,1,256,256]{3,2,1,0:T(8,128)(2,1)S(1)}, bf16[8,1,256,256]{3,2,1,0:T(8,128)(2,1)}, bf16[8,1,256,256]{3,2,1,0:T(8,128)(2,1)}, bf16[8,1,256,256]{3,2,1,0:T(8,128)(2,1)S(1)}) fusion(bf16[8,4,256,256]{3,2,1,0:T(8,128)(2,1)} %bitcast.93), kind=kLoop, calls=%fused_computation.40 | loop fusion | bytes 8388608 | tf_op jit(solution)/shard_map/slice | solution.py:127
  242.2 3.9 %all-to-all-done.9.refs_2_ = bf16[32,16,128]{2,1,0:T(8,128)(2,1)S(1)} async-done(((bf16[32,16,128]{2,1,0:T(8,128)(2,1)}), bf16[32,16,128]{2,1,0:T(8,128)(2,1)S(1)}, u32[]{:S(2)}, u32[]{:S(2)}) %all-to-all-start.9) | async-done | bytes 131104 | tf_op jit(solution)/shard_map/all_to_all | solution.py:126
  247.9 11.2 %all_to_all.102.refs_2_ = bf16[32,16,128]{2,1,0:T(8,128)(2,1)S(1)} all-to-all(bf16[32,16,128]{2,1,0:T(8,128)(2,1)S(1)} %get-tuple-element.52), channel_id=1, replica_groups=mesh['section'=8,'dom'=32] {'dom'}, dimensions={0} | all-to-all | bytes 262144 | tf_op jit(solution)/shard_map/all_to_all | solution.py:126
  260.4 1.8 layer.25
  262.2 11.2 %all_to_all.103.refs_2_ = bf16[32,16,128]{2,1,0:T(8,128)(2,1)S(1)} all-to-all(bf16[32,16,128]{2,1,0:T(8,128)(2,1)S(1)} %get-tuple-element.54), channel_id=1, replica_groups=mesh['section'=8,'dom'=32] {'dom'}, dimensions={0} | all-to-all | bytes 262144 | tf_op jit(solution)/shard_map/all_to_all | solution.py:126
  274.7 1.8 layer.26
  276.5 11.3 %all_to_all.104.refs_2_ = bf16[32,16,128]{2,1,0:T(8,128)(2,1)S(1)} all-to-all(bf16[32,16,128]{2,1,0:T(8,128)(2,1)S(1)} %get-tuple-element.56), channel_id=1, replica_groups=mesh['section'=8,'dom'=32] {'dom'}, dimensions={0} | all-to-all | bytes 262144 | tf_op jit(solution)/shard_map/all_to_all | solution.py:126
  287.8 2.5 layer.27
  290.3 3.9 %all-to-all-start.13 = ((bf16[32,16,128]{2,1,0:T(8,128)(2,1)}), bf16[32,16,128]{2,1,0:T(8,128)(2,1)S(1)}, u32[]{:S(2)}, u32[]{:S(2)}) async-start(bf16[32,16,128]{2,1,0:T(8,128)(2,1)} %get-tuple-element.58), calls=%async_computation.13 | async-start | bytes 262144 | tf_op jit(solution)/shard_map/all_to_all | solution.py:126
  294.2 3.9 %fusion.14 = (bf16[8,1,256,256]{3,2,1,0:T(8,128)(2,1)S(1)}, bf16[8,1,256,256]{3,2,1,0:T(8,128)(2,1)}, bf16[8,1,256,256]{3,2,1,0:T(8,128)(2,1)}, bf16[8,1,256,256]{3,2,1,0:T(8,128)(2,1)S(1)}) fusion(bf16[8,4,256,256]{3,2,1,0:T(8,128)(2,1)} %bitcast.92), kind=kLoop, calls=%fused_computation.39 | loop fusion | bytes 8388608 | tf_op jit(solution)/shard_map/slice | solution.py:127
  298.1 3.8 %all-to-all-done.13.refs_2_ = bf16[32,16,128]{2,1,0:T(8,128)(2,1)S(1)} async-done(((bf16[32,16,128]{2,1,0:T(8,128)(2,1)}), bf16[32,16,128]{2,1,0:T(8,128)(2,1)S(1)}, u32[]{:S(2)}, u32[]{:S(2)}) %all-to-all-start.13) | async-done | bytes 131104 | tf_op jit(solution)/shard_map/all_to_all | solution.py:126
  302.0 1.8 layer.28
  303.8 11.2 %all_to_all.105.refs_2_ = bf16[32,16,128]{2,1,0:T(8,128)(2,1)S(1)} all-to-all(bf16[32,16,128]{2,1,0:T(8,128)(2,1)S(1)} %get-tuple-element.60), channel_id=1, replica_groups=mesh['section'=8,'dom'=32] {'dom'}, dimensions={0} | all-to-all | bytes 262144 | tf_op jit(solution)/shard_map/all_to_all | solution.py:126
  316.3 1.8 layer.29
  318.1 11.2 %all_to_all.106.refs_2_ = bf16[32,16,128]{2,1,0:T(8,128)(2,1)S(1)} all-to-all(bf16[32,16,128]{2,1,0:T(8,128)(2,1)S(1)} %get-tuple-element.62), channel_id=1, replica_groups=mesh['section'=8,'dom'=32] {'dom'}, dimensions={0} | all-to-all | bytes 262144 | tf_op jit(solution)/shard_map/all_to_all | solution.py:126
  332.4 11.2 %all_to_all.107.refs_2_ = bf16[32,16,128]{2,1,0:T(8,128)(2,1)S(1)} all-to-all(bf16[32,16,128]{2,1,0:T(8,128)(2,1)S(1)} %get-tuple-element.64), channel_id=1, replica_groups=mesh['section'=8,'dom'=32] {'dom'}, dimensions={0} | all-to-all | bytes 262144 | tf_op jit(solution)/shard_map/all_to_all | solution.py:126
  (70 shorter events, 37.6 us)
Async XLA Ops:
  6.5 120.2 %all-gather.9.cloned.1.call-start = ((), (), s32[]{:S(2)}) async-start(), calls=%async_computation.17 | async-start | bytes 4718592 | tf_op jit(solution)/shard_map/all_gather | solution.py:114
  72.9 3.4 copy-start.9
  74.2 108.3 %all-gather.11.cloned.1.call-start = ((), (), s32[]{:S(2)}) async-start(), calls=%async_computation.18 | async-start | bytes 4718592 | tf_op jit(solution)/shard_map/all_gather | solution.py:114
  75.0 163.3 %all-gather.13.cloned.1.call-start = ((), (), s32[]{:S(2)}) async-start(), calls=%async_computation.19 | async-start | bytes 4718592 | tf_op jit(solution)/shard_map/all_gather | solution.py:114
  75.7 218.5 %all-gather.15.cloned.1.call-start = ((), (), s32[]{:S(2)}) async-start(), calls=%async_computation.20 | async-start | bytes 4718592 | tf_op jit(solution)/shard_map/all_gather | solution.py:114
  77.1 53.5 %copy-start.8 = (s32[16,160]{1,0:T(8,128)}, s32[16,160]{1,0:T(8,128)S(1)}, u32[]{:S(2)}) copy-start(s32[16,160]{1,0:T(8,128)S(1)} %slice_convert_fusion.refs_0_) | copy-start | bytes 30724
  78.5 52.1 %all-to-all-start.1 = ((bf16[32,16,128]{2,1,0:T(8,128)(2,1)}), bf16[32,16,128]{2,1,0:T(8,128)(2,1)S(1)}, u32[]{:S(2)}, u32[]{:S(2)}) async-start(bf16[32,16,128]{2,1,0:T(8,128)(2,1)} %broadcast_select_fusion), calls=%async_computation.1 | async-start | bytes 262144 | tf_op jit(solution)/shard_map/all_to_all | solution.py:126
  147.5 1.2 copy-start.7
  161.8 1.2 copy-start.3
  178.6 11.7 %all-to-all-start.5 = ((bf16[32,16,128]{2,1,0:T(8,128)(2,1)}), bf16[32,16,128]{2,1,0:T(8,128)(2,1)S(1)}, u32[]{:S(2)}, u32[]{:S(2)}) async-start(bf16[32,16,128]{2,1,0:T(8,128)(2,1)} %get-tuple-element.42), calls=%async_computation.5 | async-start | bytes 262144 | tf_op jit(solution)/shard_map/all_to_all | solution.py:126
  203.3 1.2 copy-start.4
  217.6 1.2 copy-start
  234.4 11.7 %all-to-all-start.9 = ((bf16[32,16,128]{2,1,0:T(8,128)(2,1)}), bf16[32,16,128]{2,1,0:T(8,128)(2,1)S(1)}, u32[]{:S(2)}, u32[]{:S(2)}) async-start(bf16[32,16,128]{2,1,0:T(8,128)(2,1)} %get-tuple-element.50), calls=%async_computation.9 | async-start | bytes 262144 | tf_op jit(solution)/shard_map/all_to_all | solution.py:126
  259.1 1.2 copy-start.5
  273.4 1.2 copy-start.1
  290.3 11.7 %all-to-all-start.13 = ((bf16[32,16,128]{2,1,0:T(8,128)(2,1)}), bf16[32,16,128]{2,1,0:T(8,128)(2,1)S(1)}, u32[]{:S(2)}, u32[]{:S(2)}) async-start(bf16[32,16,128]{2,1,0:T(8,128)(2,1)} %get-tuple-element.58), calls=%async_computation.13 | async-start | bytes 262144 | tf_op jit(solution)/shard_map/all_to_all | solution.py:126
  315.1 1.2 copy-start.6
  329.4 1.2 copy-start.2
Sparse Core Ops, SparseCore 0:
  74.3 52.2 all-gather.8
  128.5 53.3 all-gather.10
  183.7 53.3 all-gather.12
  238.7 53.3 all-gather.14

commit v3 on v2

--- a/solution.py
+++ b/solution.py
@@ -20,7 +20,7 @@
     return jnp.concatenate([bias, small.astype(jnp.bfloat16)], axis=1)
 
 
-def layer_kernel(layer, last, table, cur, arrived, bias, weights, *rest):
+def layer_kernel(layer, step, last, table, cur, arrived, bias, weights, *rest):
     if last:
         new, pool = rest
     else:
@@ -28,7 +28,8 @@
     blocks, half, lanes = cur.shape
     parts = arrived.shape[0]
     size = lanes // 2
-    slots = weights.shape[2] // size
+    slots = weights.shape[3] // size
+    each = blocks // weights.shape[0]
     low = lax.broadcasted_iota(jnp.int32, (half, lanes), 1) < size
 
     def spread(tile, at):
@@ -52,7 +53,7 @@
             pairs.append(jnp.where(low2, left, right))
         acc = lax.dot_general(
             jnp.concatenate(pairs, axis=1),
-            weights[n],
+            weights[n // each, step, pl.ds(pl.multiple_of(n % each * size, size), size), :],
             (((1,), (1,)), ((), ())),
             preferred_element_type=jnp.float32,
         )
@@ -71,14 +72,14 @@
     return pltpu.with_memory_space_constraint(x, pltpu.VMEM)
 
 
-def apply_layer(layer, last, table, cur, arrived, bias, weights):
+def apply_layer(layer, step, last, table, cur, arrived, bias, weights):
     tile = pltpu.VMEM(cur.shape, cur.dtype)
     vmem = pl.BlockSpec(memory_space=pltpu.VMEM)
     blocks, half, lanes = cur.shape
     n_out = 1 if last else 2
 
     def body(*refs):
-        layer_kernel(layer, last, *refs)
+        layer_kernel(layer, step, last, *refs)
 
     out = pl.pallas_call(
         body,
@@ -88,6 +89,7 @@
         scratch_shapes=[
             pltpu.VMEM((blocks + arrived.shape[0] + 1, 2 * half, lanes), jnp.bfloat16),
         ],
+        compiler_params=pltpu.CompilerParams(vmem_limit_bytes=4 * 1024 * 1024),
         name="layer",
     )(table, on_chip(cur), on_chip(arrived), on_chip(bias), on_chip(weights))
     return out if not last else (out[0], None)
@@ -102,19 +104,15 @@
     total = own_layers * sections
     rows = blocks // sections * size
     table = tables(bias, pattern, counts, parts, me)
-    extra = 16
-    table = jnp.pad(table, ((0, 0), (0, extra * width - table.shape[1])))
-    table = table.reshape(own_layers, 1, extra, width)
-    table = jnp.broadcast_to(table, (own_layers, sections, extra, width))
-    both = jnp.concatenate([weights.reshape(own_layers, sections, rows, width), table], axis=2)
-    scattered = lax.all_to_all(both, "section", split_axis=1, concat_axis=0, tiled=True)
-    scattered = scattered.reshape(total, rows + extra, width)
+    flat = lax.all_gather(jnp.pad(table, ((0, 0), (0, -table.shape[1] % 1024))), "section", axis=0, tiled=True)
+    split = weights.reshape(own_layers, sections, rows, width)
+    scattered = lax.all_to_all(split, "section", split_axis=1, concat_axis=0, tiled=True)
+    scattered = scattered.reshape(total, rows, width)
     chunk = 4
     filled = [
-        lax.all_gather(scattered[c : c + chunk, :rows], "section", axis=0, tiled=False)
+        lax.all_gather(scattered[c : c + chunk], "section", axis=0, tiled=False)
         for c in range(0, total, chunk)
     ]
-    flat = scattered[:, rows:].reshape(total, extra * width)
     all_bias = flat[:, : blocks * size].reshape(total, blocks, size).astype(jnp.float32)
     all_bias = jnp.concatenate([all_bias, all_bias], axis=2)
     table = flat[:, blocks * size : blocks * (size + slots) + parts].astype(jnp.int32)
@@ -124,8 +122,9 @@
     send = jnp.take(cur, table[0, blocks * slots :], axis=0)
     for layer in range(total):
         arrived = lax.all_to_all(send, "dom", split_axis=0, concat_axis=0, tiled=True)
-        held = filled[layer // chunk][:, layer % chunk].reshape(blocks, size, width)
-        cur, send = apply_layer(layer, layer == total - 1, table, cur, arrived, all_bias, held)
+        cur, send = apply_layer(
+            layer, layer % chunk, layer == total - 1, table, cur, arrived, all_bias, filled[layer // chunk]
+        )
     out = cur.reshape(blocks, half, 2, size).transpose(2, 1, 0, 3)
     return out.reshape(images.shape)
 

time: 356 us -> 345 us (0.969)
  blocking collectives: 201 us -> 218 us
  local copies, waits for them, and re-layouts: 29.7 us -> 14.8 us
  waiting for transfers between devices: 52.4 us -> 38.6 us
  starting transfers between devices: 21 us -> 26.2 us
  other arithmetic: 5.15 us -> 1.23 us
    all_gather x4, waiting for transfers between devices: 38.8 us -> 13.5 us  [shards(): lax.all_gather(scattered[c:c + chunk], 'section', axis=0, tiled=False)]
    all_gather x0 -> x1, blocking collectives: none -> 20.3 us  [shards(): lax.all_gather(jnp.pad(table, ((0, 0), (0, -table.shape[1] % 1024))), 'se...]
    slice x6 -> x1, local copies, waits for them, and re-layouts: 16.8 us -> 1.38 us  [shards(): scattered[c:c + chunk]]
    all_to_all x4, waiting for transfers between devices: 11.7 us -> 23.2 us  [shards(): lax.all_to_all(send, 'dom', split_axis=0, concat_axis=0, tiled=True)]
    all_to_all x4, starting transfers between devices: 20.9 us -> 26.1 us  [shards(): lax.all_to_all(send, 'dom', split_axis=0, concat_axis=0, tiled=True)]
    unnamed x22 -> x23, local copies, waits for them, and re-layouts: 9.91 us -> 8.82 us
  transfers between devices with their start and end apart: 8 -> 8, of which waited for: 4 -> 8; matrix products, arithmetic and copies ran while one was open for 5% -> 1% of each run, Pallas kernels for 7% -> 7%
where the time goes in v3:
time: 345 us; the launch traced here: 344 us
  blocking collectives  218 us (63%)
  waiting for transfers between devices  38.6 us (11%)
  Pallas kernels  32.2 us (9%)
  starting transfers between devices  26.2 us (8%)
  local copies, waits for them, and re-layouts  14.8 us (4%)
  between operations  13.4 us (4%)
    all_to_all x12, blocking collectives, shards(): lax.all_to_all(send, 'dom', split_axis=0, concat_axis=0, tiled=True)  139 us
    all_to_all x1, blocking collectives, shards(): lax.all_to_all(split, 'section', split_axis=1, concat_axis=0, tiled=True)  58.6 us
    pallas_call x16, Pallas kernels, apply_layer(): pl.pallas_call(body, out_shape=[tile] * n_out, in_specs=[pl.BlockSpec(mem...  32.2 us
    all_to_all x4, starting transfers between devices, shards(): lax.all_to_all(send, 'dom', split_axis=0, concat_axis=0, tiled=True)  26.1 us
    all_to_all x4, waiting for transfers between devices, shards(): lax.all_to_all(send, 'dom', split_axis=0, concat_axis=0, tiled=True)  23.2 us
    all_gather x1, blocking collectives, shards(): lax.all_gather(jnp.pad(table, ((0, 0), (0, -table.shape[1] % 1024))), 'se...  20.3 us
    all_gather x4, waiting for transfers between devices, shards(): lax.all_gather(scattered[c:c + chunk], 'section', axis=0, tiled=False)  13.5 us
    unnamed x23, local copies, waits for them, and re-layouts  8.82 us
  transfers between devices with their start and end apart: 8, of which 8 were waited for; matrix products, arithmetic and copies ran while one was open for 1% of the time, Pallas kernels for 7%

profile of v3, /device:TPU:1, one launch (start us, length us, event | category | flops | bytes accessed | tf_op | source)
XLA Modules:
  0.0 344.3 jit_solution(2653742250011480337)
XLA Ops:
  8.3 58.6 %all_to_all.95 = bf16[2,8,256,256]{3,2,0,1:T(8,128)(2,1)S(1)} all-to-all(bf16[2,8,256,256]{3,2,0,1:T(8,128)(2,1)S(1)} %copy.19), channel_id=1, replica_groups=mesh['section'=8,'dom'=32] {'section'}, dimensions={1} | all-to-all | bytes 4194304 | tf_op jit(solution)/shard_map/all_to_all | solution.py:109
  71.1 20.3 %all-gather = bf16[8,2,3072]{2,1,0:T(2,128)(2,1)S(1)} all-gather(bf16[1,2,3072]{2,1,0:T(2,128)(2,1)S(1)} %fusion.9), channel_id=1, replica_groups=mesh['section'=8,'dom'=32] {'section'}, dimensions={0}, use_global_device_ids=true | all-gather | bytes 110592 | tf_op jit(solution)/shard_map/all_gather | solution.py:107
  93.6 14.3 %all-to-all-start = ((bf16[32,16,128]{2,1,0:T(8,128)(2,1)}), bf16[32,16,128]{2,1,0:T(8,128)(2,1)S(1)}, u32[]{:S(2)}, u32[]{:S(2)}) async-start(bf16[32,16,128]{2,1,0:T(8,128)(2,1)} %broadcast_select_fusion), calls=%async_computation | async-start | bytes 262144 | tf_op jit(solution)/shard_map/all_to_all | solution.py:124
  108.2 7.4 %all-to-all-done.refs_2_ = bf16[32,16,128]{2,1,0:T(8,128)(2,1)S(1)} async-done(((bf16[32,16,128]{2,1,0:T(8,128)(2,1)}), bf16[32,16,128]{2,1,0:T(8,128)(2,1)S(1)}, u32[]{:S(2)}, u32[]{:S(2)}) %all-to-all-start) | async-done | bytes 131104 | tf_op jit(solution)/shard_map/all_to_all | solution.py:124
  115.6 6.0 %all-gather.6.cloned.1.call-done.refs_4_ = bf16[8,4,256,256]{3,2,1,0:T(8,128)(2,1)} async-done(((bf16[1,4,256,256]{3,2,1,0:T(8,128)(2,1)}), bf16[8,4,256,256]{3,2,1,0:T(8,128)(2,1)}) %all-gather.6.cloned.1.call-update) | async-done | bytes 4194320 | tf_op jit(solution)/shard_map/all_gather | solution.py:113
  121.6 2.2 copy-done.6
  125.6 15.2 %all_to_all.96.refs_2_ = bf16[32,16,128]{2,1,0:T(8,128)(2,1)S(1)} all-to-all(bf16[32,16,128]{2,1,0:T(8,128)(2,1)S(1)} %get-tuple-element.36), channel_id=1, replica_groups=mesh['section'=8,'dom'=32] {'dom'}, dimensions={0} | all-to-all | bytes 262144 | tf_op jit(solution)/shard_map/all_to_all | solution.py:124
  142.7 11.2 %all_to_all.97.refs_2_ = bf16[32,16,128]{2,1,0:T(8,128)(2,1)S(1)} all-to-all(bf16[32,16,128]{2,1,0:T(8,128)(2,1)S(1)} %get-tuple-element.38), channel_id=1, replica_groups=mesh['section'=8,'dom'=32] {'dom'}, dimensions={0} | all-to-all | bytes 262144 | tf_op jit(solution)/shard_map/all_to_all | solution.py:124
  155.8 11.2 %all_to_all.98.refs_2_ = bf16[32,16,128]{2,1,0:T(8,128)(2,1)S(1)} all-to-all(bf16[32,16,128]{2,1,0:T(8,128)(2,1)S(1)} %get-tuple-element.40), channel_id=1, replica_groups=mesh['section'=8,'dom'=32] {'dom'}, dimensions={0} | all-to-all | bytes 262144 | tf_op jit(solution)/shard_map/all_to_all | solution.py:124
  167.1 2.5 layer.19
  169.6 3.9 %all-to-all-start.5 = ((bf16[32,16,128]{2,1,0:T(8,128)(2,1)}), bf16[32,16,128]{2,1,0:T(8,128)(2,1)S(1)}, u32[]{:S(2)}, u32[]{:S(2)}) async-start(bf16[32,16,128]{2,1,0:T(8,128)(2,1)} %get-tuple-element.42), calls=%async_computation.5 | async-start | bytes 262144 | tf_op jit(solution)/shard_map/all_to_all | solution.py:124
  173.5 3.2 all-gather.8.cloned.1.call-done.refs_4_
  176.8 4.6 %all-to-all-done.5.refs_2_ = bf16[32,16,128]{2,1,0:T(8,128)(2,1)S(1)} async-done(((bf16[32,16,128]{2,1,0:T(8,128)(2,1)}), bf16[32,16,128]{2,1,0:T(8,128)(2,1)S(1)}, u32[]{:S(2)}, u32[]{:S(2)}) %all-to-all-start.5) | async-done | bytes 131104 | tf_op jit(solution)/shard_map/all_to_all | solution.py:124
  181.3 2.2 copy-done.4
  185.4 11.2 %all_to_all.99.refs_2_ = bf16[32,16,128]{2,1,0:T(8,128)(2,1)S(1)} all-to-all(bf16[32,16,128]{2,1,0:T(8,128)(2,1)S(1)} %get-tuple-element.44), channel_id=1, replica_groups=mesh['section'=8,'dom'=32] {'dom'}, dimensions={0} | all-to-all | bytes 262144 | tf_op jit(solution)/shard_map/all_to_all | solution.py:124
  198.5 11.2 %all_to_all.100.refs_2_ = bf16[32,16,128]{2,1,0:T(8,128)(2,1)S(1)} all-to-all(bf16[32,16,128]{2,1,0:T(8,128)(2,1)S(1)} %get-tuple-element.46), channel_id=1, replica_groups=mesh['section'=8,'dom'=32] {'dom'}, dimensions={0} | all-to-all | bytes 262144 | tf_op jit(solution)/shard_map/all_to_all | solution.py:124
  211.7 11.2 %all_to_all.101.refs_2_ = bf16[32,16,128]{2,1,0:T(8,128)(2,1)S(1)} all-to-all(bf16[32,16,128]{2,1,0:T(8,128)(2,1)S(1)} %get-tuple-element.48), channel_id=1, replica_groups=mesh['section'=8,'dom'=32] {'dom'}, dimensions={0} | all-to-all | bytes 262144 | tf_op jit(solution)/shard_map/all_to_all | solution.py:124
  222.9 2.5 layer.23
  225.4 3.9 %all-to-all-start.9 = ((bf16[32,16,128]{2,1,0:T(8,128)(2,1)}), bf16[32,16,128]{2,1,0:T(8,128)(2,1)S(1)}, u32[]{:S(2)}, u32[]{:S(2)}) async-start(bf16[32,16,128]{2,1,0:T(8,128)(2,1)} %get-tuple-element.50), calls=%async_computation.9 | async-start | bytes 262144 | tf_op jit(solution)/shard_map/all_to_all | solution.py:124
  229.4 2.6 all-gather.10.cloned.1.call-done.refs_4_
  231.9 5.2 %all-to-all-done.9.refs_2_ = bf16[32,16,128]{2,1,0:T(8,128)(2,1)S(1)} async-done(((bf16[32,16,128]{2,1,0:T(8,128)(2,1)}), bf16[32,16,128]{2,1,0:T(8,128)(2,1)S(1)}, u32[]{:S(2)}, u32[]{:S(2)}) %all-to-all-start.9) | async-done | bytes 131104 | tf_op jit(solution)/shard_map/all_to_all | solution.py:124
  237.1 2.2 copy-done.2
  241.2 11.2 %all_to_all.102.refs_2_ = bf16[32,16,128]{2,1,0:T(8,128)(2,1)S(1)} all-to-all(bf16[32,16,128]{2,1,0:T(8,128)(2,1)S(1)} %get-tuple-element.52), channel_id=1, replica_groups=mesh['section'=8,'dom'=32] {'dom'}, dimensions={0} | all-to-all | bytes 262144 | tf_op jit(solution)/shard_map/all_to_all | solution.py:124
  254.4 11.2 %all_to_all.103.refs_2_ = bf16[32,16,128]{2,1,0:T(8,128)(2,1)S(1)} all-to-all(bf16[32,16,128]{2,1,0:T(8,128)(2,1)S(1)} %get-tuple-element.54), channel_id=1, replica_groups=mesh['section'=8,'dom'=32] {'dom'}, dimensions={0} | all-to-all | bytes 262144 | tf_op jit(solution)/shard_map/all_to_all | solution.py:124
  267.5 11.2 %all_to_all.104.refs_2_ = bf16[32,16,128]{2,1,0:T(8,128)(2,1)S(1)} all-to-all(bf16[32,16,128]{2,1,0:T(8,128)(2,1)S(1)} %get-tuple-element.56), channel_id=1, replica_groups=mesh['section'=8,'dom'=32] {'dom'}, dimensions={0} | all-to-all | bytes 262144 | tf_op jit(solution)/shard_map/all_to_all | solution.py:124
  278.8 2.6 layer.27
  281.4 3.9 %all-to-all-start.13 = ((bf16[32,16,128]{2,1,0:T(8,128)(2,1)}), bf16[32,16,128]{2,1,0:T(8,128)(2,1)S(1)}, u32[]{:S(2)}, u32[]{:S(2)}) async-start(bf16[32,16,128]{2,1,0:T(8,128)(2,1)} %get-tuple-element.58), calls=%async_computation.13 | async-start | bytes 262144 | tf_op jit(solution)/shard_map/all_to_all | solution.py:124
  287.0 6.1 %all-to-all-done.13.refs_2_ = bf16[32,16,128]{2,1,0:T(8,128)(2,1)S(1)} async-done(((bf16[32,16,128]{2,1,0:T(8,128)(2,1)}), bf16[32,16,128]{2,1,0:T(8,128)(2,1)S(1)}, u32[]{:S(2)}, u32[]{:S(2)}) %all-to-all-start.13) | async-done | bytes 131104 | tf_op jit(solution)/shard_map/all_to_all | solution.py:124
  293.1 2.2 copy-done
  297.2 11.3 %all_to_all.105.refs_2_ = bf16[32,16,128]{2,1,0:T(8,128)(2,1)S(1)} all-to-all(bf16[32,16,128]{2,1,0:T(8,128)(2,1)S(1)} %get-tuple-element.60), channel_id=1, replica_groups=mesh['section'=8,'dom'=32] {'dom'}, dimensions={0} | all-to-all | bytes 262144 | tf_op jit(solution)/shard_map/all_to_all | solution.py:124
  310.3 11.2 %all_to_all.106.refs_2_ = bf16[32,16,128]{2,1,0:T(8,128)(2,1)S(1)} all-to-all(bf16[32,16,128]{2,1,0:T(8,128)(2,1)S(1)} %get-tuple-element.62), channel_id=1, replica_groups=mesh['section'=8,'dom'=32] {'dom'}, dimensions={0} | all-to-all | bytes 262144 | tf_op jit(solution)/shard_map/all_to_all | solution.py:124
  323.5 11.2 %all_to_all.107.refs_2_ = bf16[32,16,128]{2,1,0:T(8,128)(2,1)S(1)} all-to-all(bf16[32,16,128]{2,1,0:T(8,128)(2,1)S(1)} %get-tuple-element.64), channel_id=1, replica_groups=mesh['section'=8,'dom'=32] {'dom'}, dimensions={0} | all-to-all | bytes 262144 | tf_op jit(solution)/shard_map/all_to_all | solution.py:124
  (66 shorter events, 35.6 us)
Async XLA Ops:
  6.5 115.1 %all-gather.6.cloned.1.call-start = ((), (), s32[]{:S(2)}) async-start(), calls=%async_computation.17 | async-start | bytes 4718592 | tf_op jit(solution)/shard_map/all_gather | solution.py:113
  66.9 3.5 %copy-start.8 = (s32[2,1024,4]{1,2,0:T(4,128)S(1)}, s32[2,1024,4]{1,2,0:T(4,128)}, u32[]{:S(2)}) copy-start(s32[2,1024,4]{1,2,0:T(4,128)} %param.8) | copy-start | bytes 98308
  66.9 3.5 %copy-start.10 = (s32[2,32]{1,0:T(2,128)S(1)}, s32[2,32]{1,0:T(2,128)}, u32[]{:S(2)}) copy-start(s32[2,32]{1,0:T(2,128)} %param.9) | copy-start | bytes 772
  66.9 4.1 %copy-start.9 = (bf16[2,2048]{1,0:T(2,128)(2,1)S(1)}, bf16[2,2048]{1,0:T(2,128)(2,1)}, u32[]{:S(2)}) copy-start(bf16[2,2048]{1,0:T(2,128)(2,1)} %param.7) | copy-start | bytes 24580
  66.9 24.6 %copy-start.7 = (bf16[1,32,2048]{2,1,0:T(8,128)(2,1)S(1)}, bf16[1,32,2048]{2,1,0:T(8,128)(2,1)}, u32[]{:S(2)}) copy-start(bf16[1,32,2048]{2,1,0:T(8,128)(2,1)} %param.5) | copy-start | bytes 393220
  68.3 108.4 %all-gather.8.cloned.1.call-start = ((), (), s32[]{:S(2)}) async-start(), calls=%async_computation.18 | async-start | bytes 4718592 | tf_op jit(solution)/shard_map/all_gather | solution.py:113
  69.1 162.9 %all-gather.10.cloned.1.call-start = ((), (), s32[]{:S(2)}) async-start(), calls=%async_computation.19 | async-start | bytes 4718592 | tf_op jit(solution)/shard_map/all_gather | solution.py:113
  69.8 217.2 %all-gather.12.cloned.1.call-start = ((), (), s32[]{:S(2)}) async-start(), calls=%async_computation.20 | async-start | bytes 4718592 | tf_op jit(solution)/shard_map/all_gather | solution.py:113
  93.6 22.0 %all-to-all-start = ((bf16[32,16,128]{2,1,0:T(8,128)(2,1)}), bf16[32,16,128]{2,1,0:T(8,128)(2,1)S(1)}, u32[]{:S(2)}, u32[]{:S(2)}) async-start(bf16[32,16,128]{2,1,0:T(8,128)(2,1)} %broadcast_select_fusion), calls=%async_computation | async-start | bytes 262144 | tf_op jit(solution)/shard_map/all_to_all | solution.py:124
  121.6 2.2 copy-start.6
  169.6 11.7 %all-to-all-start.5 = ((bf16[32,16,128]{2,1,0:T(8,128)(2,1)}), bf16[32,16,128]{2,1,0:T(8,128)(2,1)S(1)}, u32[]{:S(2)}, u32[]{:S(2)}) async-start(bf16[32,16,128]{2,1,0:T(8,128)(2,1)} %get-tuple-element.42), calls=%async_computation.5 | async-start | bytes 262144 | tf_op jit(solution)/shard_map/all_to_all | solution.py:124
  181.3 2.2 copy-start.4
  183.5 13.1 %copy-start.5 = (bf16[8,4,256,256]{3,2,1,0:T(8,128)(2,1)S(1)}, bf16[8,4,256,256]{3,2,1,0:T(8,128)(2,1)}, u32[]{:S(2)}) copy-start(bf16[8,4,256,256]{3,2,1,0:T(8,128)(2,1)} %all-gather.8.cloned.1.call-done.refs_4_) | copy-start | bytes 12582916
  225.4 11.7 %all-to-all-start.9 = ((bf16[32,16,128]{2,1,0:T(8,128)(2,1)}), bf16[32,16,128]{2,1,0:T(8,128)(2,1)S(1)}, u32[]{:S(2)}, u32[]{:S(2)}) async-start(bf16[32,16,128]{2,1,0:T(8,128)(2,1)} %get-tuple-element.50), calls=%async_computation.9 | async-start | bytes 262144 | tf_op jit(solution)/shard_map/all_to_all | solution.py:124
  237.1 2.2 copy-start.2
  239.3 13.1 %copy-start.3 = (bf16[8,4,256,256]{3,2,1,0:T(8,128)(2,1)S(1)}, bf16[8,4,256,256]{3,2,1,0:T(8,128)(2,1)}, u32[]{:S(2)}) copy-start(bf16[8,4,256,256]{3,2,1,0:T(8,128)(2,1)} %all-gather.10.cloned.1.call-done.refs_4_) | copy-start | bytes 12582916
  281.4 11.7 %all-to-all-start.13 = ((bf16[32,16,128]{2,1,0:T(8,128)(2,1)}), bf16[32,16,128]{2,1,0:T(8,128)(2,1)S(1)}, u32[]{:S(2)}, u32[]{:S(2)}) async-start(bf16[32,16,128]{2,1,0:T(8,128)(2,1)} %get-tuple-element.58), calls=%async_computation.13 | async-start | bytes 262144 | tf_op jit(solution)/shard_map/all_to_all | solution.py:124
  293.1 2.2 copy-start
  295.2 13.2 %copy-start.1 = (bf16[8,4,256,256]{3,2,1,0:T(8,128)(2,1)S(1)}, bf16[8,4,256,256]{3,2,1,0:T(8,128)(2,1)}, u32[]{:S(2)}) copy-start(bf16[8,4,256,256]{3,2,1,0:T(8,128)(2,1)} %all-gather.12.cloned.1.call-done.refs_4_) | copy-start | bytes 12582916
Sparse Core Ops, SparseCore 0:
  68.4 53.1 all-gather.5
  123.4 53.3 all-gather.7
  178.6 53.3 all-gather.9
  233.6 53.3 all-gather.11

commit v4 on v3

--- a/solution.py
+++ b/solution.py
@@ -20,16 +20,17 @@
     return jnp.concatenate([bias, small.astype(jnp.bfloat16)], axis=1)
 
 
-def layer_kernel(layer, step, last, table, cur, arrived, bias, weights, *rest):
-    if last:
+def layer_kernel(layer, step, follow, unroll, table, cur, arrived, bias, weights, *rest):
+    if follow is None:
         new, pool = rest
     else:
         new, send, pool = rest
     blocks, half, lanes = cur.shape
     parts = arrived.shape[0]
     size = lanes // 2
-    slots = weights.shape[3] // size
+    slots = weights.shape[2] // size
     each = blocks // weights.shape[0]
+    base = step * each * size
     low = lax.broadcasted_iota(jnp.int32, (half, lanes), 1) < size
 
     def spread(tile, at):
@@ -53,7 +54,7 @@
             pairs.append(jnp.where(low2, left, right))
         acc = lax.dot_general(
             jnp.concatenate(pairs, axis=1),
-            weights[n // each, step, pl.ds(pl.multiple_of(n % each * size, size), size), :],
+            weights[n // each, pl.ds(pl.multiple_of(base + n % each * size, size), size), :],
             (((1,), (1,)), ((), ())),
             preferred_element_type=jnp.float32,
         )
@@ -62,24 +63,24 @@
         new[n] = jnp.clip(tile, 0.0, 32.0).astype(jnp.bfloat16)
         return carry
 
-    lax.fori_loop(0, blocks, column, 0, unroll=16)
-    if not last:
+    lax.fori_loop(0, blocks, column, 0, unroll=unroll)
+    if follow is not None:
         for q in range(parts):
-            send[q] = new[table[layer + 1, blocks * slots + q]]
+            send[q] = new[table[follow, blocks * slots + q]]
 
 
 def on_chip(x):
     return pltpu.with_memory_space_constraint(x, pltpu.VMEM)
 
 
-def apply_layer(layer, step, last, table, cur, arrived, bias, weights):
+def apply_layer(layer, step, follow, unroll, table, cur, arrived, bias, weights):
     tile = pltpu.VMEM(cur.shape, cur.dtype)
     vmem = pl.BlockSpec(memory_space=pltpu.VMEM)
     blocks, half, lanes = cur.shape
-    n_out = 1 if last else 2
+    n_out = 1 if follow is None else 2
 
     def body(*refs):
-        layer_kernel(layer, step, last, *refs)
+        layer_kernel(layer, step, follow, unroll, *refs)
 
     out = pl.pallas_call(
         body,
@@ -89,41 +90,131 @@
         scratch_shapes=[
             pltpu.VMEM((blocks + arrived.shape[0] + 1, 2 * half, lanes), jnp.bfloat16),
         ],
-        compiler_params=pltpu.CompilerParams(vmem_limit_bytes=4 * 1024 * 1024),
+        compiler_params=pltpu.CompilerParams(vmem_limit_bytes=(3 + half // 16) * 1024 * 1024),
         name="layer",
     )(table, on_chip(cur), on_chip(arrived), on_chip(bias), on_chip(weights))
-    return out if not last else (out[0], None)
+    return out if follow is not None else (out[0], None)
+
+
+def split_table(flat, blocks, size, slots, parts):
+    rows = flat.shape[0]
+    bias = flat[:, : blocks * size].reshape(rows, blocks, size).astype(jnp.float32)
+    words = flat[:, blocks * size : blocks * (size + slots) + parts].astype(jnp.int32)
+    return jnp.concatenate([bias, bias], axis=2), words
+
+
+def exchange(send):
+    return lax.all_to_all(send, "dom", split_axis=0, concat_axis=0, tiled=True)
+
+
+def place_kernel(here, *refs):
+    count = len(refs) - 4
+    pieces, held, stage, take, give = refs[:count], *refs[count:]
+    sources = [lax.rem(here[0] + count - d, count) for d in range(count)]
+    ins = [pltpu.make_async_copy(pieces[d], stage.at[d], take.at[d]) for d in range(count)]
+    outs = [pltpu.make_async_copy(stage.at[d], held.at[sources[d]], give.at[d]) for d in range(count)]
+    for copy in ins:
+        copy.start()
+    for copy, onward in zip(ins, outs):
+        copy.wait()
+        onward.start()
+    for onward in outs:
+        onward.wait()
+
+
+def place(here, pieces):
+    count = len(pieces)
+    shape = (count, *pieces[0].shape)
+    hbm = pl.BlockSpec(memory_space=pl.ANY)
+    return pl.pallas_call(
+        place_kernel,
+        out_shape=jax.ShapeDtypeStruct(shape, pieces[0].dtype),
+        in_specs=[pl.BlockSpec(memory_space=pltpu.SMEM)] + [hbm] * count,
+        out_specs=hbm,
+        scratch_shapes=[
+            pltpu.VMEM(shape, pieces[0].dtype),
+            pltpu.SemaphoreType.DMA((count,)),
+            pltpu.SemaphoreType.DMA((count,)),
+        ],
+        compiler_params=pltpu.CompilerParams(vmem_limit_bytes=4 * 1024 * 1024),
+        name="place",
+    )(here.reshape(1), *pieces)
 
 
 def shards(images, weights, bias, pattern, counts):
     parts = lax.axis_size("dom")
     sections = lax.axis_size("section")
     me = lax.axis_index("dom")
+    here = lax.axis_index("section")
     own_layers, blocks, size, width = weights.shape
     slots = pattern.shape[2]
     total = own_layers * sections
     rows = blocks // sections * size
+    half = images.shape[1] // 2
+    words = blocks * slots
+    pair = [(0, 1), (1, 0)]
+    early = 2 * own_layers
+    even = here % 2 == 0
+
+    cur = images.reshape(2, half, blocks, size).transpose(2, 1, 0, 3).reshape(blocks, half, 2 * size)
+    shares = [cur]
+    for k in range(1, sections // 2):
+        shares.append(lax.ppermute(cur, "section", [(2 * k, 0), (2 * k + 1, 1)]))
     table = tables(bias, pattern, counts, parts, me)
-    flat = lax.all_gather(jnp.pad(table, ((0, 0), (0, -table.shape[1] % 1024))), "section", axis=0, tiled=True)
+    table = jnp.pad(table, ((0, 0), (0, -table.shape[1] % 1024)))
+    other = lax.ppermute(table, "section", pair)
+    partner = []
+    for k in range(own_layers):
+        partner.append(lax.ppermute(weights[k], "section", pair))
+
     split = weights.reshape(own_layers, sections, rows, width)
-    scattered = lax.all_to_all(split, "section", split_axis=1, concat_axis=0, tiled=True)
-    scattered = scattered.reshape(total, rows, width)
+    pieces = [lax.dynamic_index_in_dim(split, here, 1, keepdims=False)]
+    for d in range(1, sections):
+        piece = lax.dynamic_index_in_dim(split, (here + d) % sections, 1, keepdims=False)
+        pairs = [(s, (s + d) % sections) for s in range(2, sections)]
+        pieces.append(lax.ppermute(piece, "section", pairs))
+    both = jnp.concatenate([jnp.where(even, table, other), jnp.where(even, other, table)], axis=0)
+    pair_bias, pair_words = split_table(both, blocks, size, slots, parts)
+
+    def mine(layer):
+        k = layer % own_layers
+        ours = even if layer < own_layers else jnp.logical_not(even)
+        return jnp.where(ours, weights[k], partner[k]).reshape(1, blocks * size, width)
+
+
+    cur = jnp.concatenate(shares, axis=1)
+    send = jnp.take(cur, pair_words[0, words:], axis=0)
     chunk = 4
-    filled = [
-        lax.all_gather(scattered[c : c + chunk], "section", axis=0, tiled=False)
-        for c in range(0, total, chunk)
-    ]
-    all_bias = flat[:, : blocks * size].reshape(total, blocks, size).astype(jnp.float32)
-    all_bias = jnp.concatenate([all_bias, all_bias], axis=2)
-    table = flat[:, blocks * size : blocks * (size + slots) + parts].astype(jnp.int32)
-
-    half = images.shape[1] // 2
-    cur = images.reshape(2, half, blocks, size).transpose(2, 1, 0, 3).reshape(blocks, half, 2 * size)
-    send = jnp.take(cur, table[0, blocks * slots :], axis=0)
-    for layer in range(total):
-        arrived = lax.all_to_all(send, "dom", split_axis=0, concat_axis=0, tiled=True)
+    for layer in range(early):
+        arrived = exchange(send)
+        if layer == 1:
+            arrived, pieces, partner[1] = lax.optimization_barrier((arrived, pieces, partner[1]))
+            held = place(here, pieces).reshape(total * rows, width)
+            filled = {}
+            for c in range(early, total, chunk):
+                part = held[c * rows : (c + chunk) * rows]
+                if c == early:
+                    lines = table.reshape(-1, width)
+                    lines = jnp.pad(lines, ((0, -lines.shape[0] % 16), (0, 0)))
+                    part = jnp.concatenate([part, lines], axis=0)
+                filled[c] = lax.all_gather(part, "section", axis=0, tiled=False)
+        follow = layer + 1 if layer + 1 < early else None
+        cur, send = apply_layer(layer, 0, follow, 4, pair_words, cur, arrived, pair_bias, mine(layer))
+
+    ready = cur.reshape(blocks, sections // 2, half, 2 * size)
+    back = jnp.zeros_like(ready[:, 0])
+    for k in range(1, sections // 2):
+        back = back + lax.ppermute(ready[:, k], "section", [(0, 2 * k), (1, 2 * k + 1)])
+    cur = jnp.where(here < 2, ready[:, 0], back)
+
+    flat = filled[early][:, chunk * rows : chunk * rows + table.size // width].reshape(total, -1)
+    all_bias, table = split_table(flat, blocks, size, slots, parts)
+    send = jnp.take(cur, table[early, words:], axis=0)
+    for layer in range(early, total):
+        step = (layer - early) % chunk
+        follow = layer + 1 if layer + 1 < total else None
         cur, send = apply_layer(
-            layer, layer % chunk, layer == total - 1, table, cur, arrived, all_bias, filled[layer // chunk]
+            layer, step, follow, 16, table, cur, exchange(send), all_bias, filled[layer - step]
         )
     out = cur.reshape(blocks, half, 2, size).transpose(2, 1, 0, 3)
     return out.reshape(images.shape)

time: 345 us -> 375 us (1.087)
  blocking collectives: 218 us -> 135 us
  waiting for transfers between devices: 38.6 us -> 104 us
  starting transfers between devices: 26.2 us -> 55.2 us
  Pallas kernels: 32.2 us -> 39.4 us
  other arithmetic: 1.23 us -> 6.62 us
  local copies, waits for them, and re-layouts: 14.8 us -> 19.6 us
    ppermute x0 -> x16, waiting for transfers between devices: none -> 69.6 us  [the longest x7 43.4 us: shards(): pieces.append(lax.ppermute(piece, 'section', pairs))]
    all_to_all x13 -> x11, blocking collectives: 197 us -> 135 us  [exchange(): return lax.all_to_all(send, 'dom', split_axis=0, concat_axis=0, tiled=True)]
    ppermute x0 -> x16, starting transfers between devices: none -> 27.5 us  [the longest x7 9.11 us: shards(): pieces.append(lax.ppermute(piece, 'section', pairs))]
    all_gather x1 -> x0, blocking collectives: 20.3 us -> none  [shards(): lax.all_gather(jnp.pad(table, ((0, 0), (0, -table.shape[1] % 1024))), 'se...]
    all_gather x4 -> x3, waiting for transfers between devices: 13.5 us -> 0.06 us  [shards(): filled[c] = lax.all_gather(part, 'section', axis=0, tiled=False)]
    all_to_all x4 -> x5, waiting for transfers between devices: 23.2 us -> 32.6 us  [exchange(): return lax.all_to_all(send, 'dom', split_axis=0, concat_axis=0, tiled=True)]
    pallas_call x16, Pallas kernels: 32.2 us -> 38 us  [apply_layer(): pl.pallas_call(body, out_shape=[tile] * n_out, in_specs=[pl.BlockSpec(mem...]
    squeeze x0 -> x3, local copies, waits for them, and re-layouts: none -> 4.47 us  [the longest x1 3.14 us: shards(): partner.append(lax.ppermute(weights[k], 'section', pair))]
  transfers between devices with their start and end apart: 8 -> 24, of which waited for: 8 -> 11; matrix products, arithmetic and copies ran while one was open for 1% -> 4% of each run, Pallas kernels for 7% -> 8%
where the time goes in v4:
time: 375 us; the launch traced here: 374 us
  blocking collectives  135 us (36%)
  waiting for transfers between devices  104 us (28%)
  starting transfers between devices  55.2 us (15%)
  Pallas kernels  39.4 us (11%)
  local copies, waits for them, and re-layouts  19.6 us (5%)
  between operations  13.9 us (4%)
  other arithmetic  6.62 us (2%)
    all_to_all x11, blocking collectives, exchange(): return lax.all_to_all(send, 'dom', split_axis=0, concat_axis=0, tiled=True)  135 us
    ppermute x7, waiting for transfers between devices, shards(): pieces.append(lax.ppermute(piece, 'section', pairs))  43.4 us
    pallas_call x16, Pallas kernels, apply_layer(): pl.pallas_call(body, out_shape=[tile] * n_out, in_specs=[pl.BlockSpec(mem...  38 us
    all_to_all x5, waiting for transfers between devices, exchange(): return lax.all_to_all(send, 'dom', split_axis=0, concat_axis=0, tiled=True)  32.6 us
    all_to_all x5, starting transfers between devices, exchange(): return lax.all_to_all(send, 'dom', split_axis=0, concat_axis=0, tiled=True)  27.6 us
    ppermute x1, waiting for transfers between devices, shards(): other = lax.ppermute(table, 'section', pair)  20.8 us
    ppermute x7, starting transfers between devices, shards(): pieces.append(lax.ppermute(piece, 'section', pairs))  9.11 us
    ppermute x2, starting transfers between devices, shards(): partner.append(lax.ppermute(weights[k], 'section', pair))  8.58 us
  transfers between devices with their start and end apart: 24, of which 11 were waited for; matrix products, arithmetic and copies ran while one was open for 4% of the time, Pallas kernels for 8%

profile of v4, /device:TPU:1, one launch (start us, length us, event | category | flops | bytes accessed | tf_op | source)
XLA Modules:
  0.0 373.6 jit_solution(586730679712501765)
XLA Ops:
  12.2 3.1 slice_bitcast_fusion
  15.4 4.4 %collective-permute-start.4 = (bf16[32,64,256]{2,1,0:T(8,128)(2,1)}, bf16[32,64,256]{2,1,0:T(8,128)(2,1)}, u32[]{:S(2)}, u32[]{:S(2)}) collective-permute-start(bf16[32,64,256]{2,1,0:T(8,128)(2,1)} %get-tuple-element.89), channel_id=1, source_target_pairs={{0,32},{32,0},{1,33},{33,1},{2,34},{34,2},{3,35},{35,3},{4,36},{36... | collective-permute-start | bytes 3145736 | tf_op jit(solution)/shard_map/ppermute | solution.py:168
  23.8 20.8 %collective-permute-done = bf16[2,3072]{1,0:T(2,128)(2,1)S(1)} collective-permute-done((bf16[2,3072]{1,0:T(2,128)(2,1)S(1)}, bf16[2,3072]{1,0:T(2,128)(2,1)S(1)}, u32[]{:S(2)}, u32[]{:S(2)}) %collective-permute-start) | collective-permute-done | bytes 12320 | tf_op jit(solution)/shard_map/ppermute | solution.py:165
  48.7 4.2 %collective-permute-start.12 = (bf16[32,64,256]{2,1,0:T(8,128)(2,1)}, bf16[32,64,256]{2,1,0:T(8,128)(2,1)}, u32[]{:S(2)}, u32[]{:S(2)}) collective-permute-start(bf16[32,64,256]{2,1,0:T(8,128)(2,1)} %get-tuple-element.88), channel_id=1, source_target_pairs={{0,32},{32,0},{1,33},{33,1},{2,34},{34,2},{3,35},{35,3},{4,36},{36... | collective-permute-start | bytes 3145736 | tf_op jit(solution)/shard_map/ppermute | solution.py:168
  54.5 8.8 %all-to-all-start = ((bf16[32,64,128]{2,1,0:T(8,128)(2,1)}), bf16[32,64,128]{2,1,0:T(8,128)(2,1)S(1)}, u32[]{:S(2)}, u32[]{:S(2)}) async-start(bf16[32,64,128]{2,1,0:T(8,128)(2,1)} %broadcast_select_fusion.4), calls=%async_computation | async-start | bytes 1048576 | tf_op jit(solution)/shard_map/all_to_all | solution.py:107
  65.3 9.7 %all-to-all-done.refs_2_ = bf16[32,64,128]{2,1,0:T(8,128)(2,1)S(1)} async-done(((bf16[32,64,128]{2,1,0:T(8,128)(2,1)}), bf16[32,64,128]{2,1,0:T(8,128)(2,1)S(1)}, u32[]{:S(2)}, u32[]{:S(2)}) %all-to-all-start) | async-done | bytes 524320 | tf_op jit(solution)/shard_map/all_to_all | solution.py:107
  74.9 3.4 layer.16
  80.0 3.7 all-to-all-start.1
  89.0 11.7 %collective-permute-done.6.refs_2_ = bf16[2,256,256]{2,1,0:T(8,128)(2,1)S(1)} collective-permute-done((bf16[2,256,256]{2,1,0:T(8,128)(2,1)}, bf16[2,256,256]{2,1,0:T(8,128)(2,1)S(1)}, u32[]{:S(2)}, u32[]{:S(2)}) %collective-permute-start.6) | collective-permute-done | bytes 262176 | tf_op jit(solution)/shard_map/ppermute | solution.py:175
  100.7 13.3 %collective-permute-done.7.refs_3_ = bf16[2,256,256]{2,1,0:T(8,128)(2,1)S(1)} collective-permute-done((bf16[2,256,256]{2,1,0:T(8,128)(2,1)}, bf16[2,256,256]{2,1,0:T(8,128)(2,1)S(1)}, u32[]{:S(2)}, u32[]{:S(2)}) %collective-permute-start.7) | collective-permute-done | bytes 262176 | tf_op jit(solution)/shard_map/ppermute | solution.py:175
  114.0 18.4 %collective-permute-done.8.refs_4_ = bf16[2,256,256]{2,1,0:T(8,128)(2,1)S(1)} collective-permute-done((bf16[2,256,256]{2,1,0:T(8,128)(2,1)}, bf16[2,256,256]{2,1,0:T(8,128)(2,1)S(1)}, u32[]{:S(2)}, u32[]{:S(2)}) %collective-permute-start.8) | collective-permute-done | bytes 262176 | tf_op jit(solution)/shard_map/ppermute | solution.py:175
  139.0 3.5 layer.17
  142.6 19.1 %all_to_all.80.refs_2_ = bf16[32,64,128]{2,1,0:T(8,128)(2,1)S(1)} all-to-all(bf16[32,64,128]{2,1,0:T(8,128)(2,1)S(1)} %get-tuple-element.56), channel_id=1, replica_groups=mesh['section'=8,'dom'=32] {'dom'}, dimensions={0} | all-to-all | bytes 1048576 | tf_op jit(solution)/shard_map/all_to_all | solution.py:107
  161.6 3.5 layer.18
  165.2 15.0 %all_to_all.81.refs_2_ = bf16[32,64,128]{2,1,0:T(8,128)(2,1)S(1)} all-to-all(bf16[32,64,128]{2,1,0:T(8,128)(2,1)S(1)} %get-tuple-element.58), channel_id=1, replica_groups=mesh['section'=8,'dom'=32] {'dom'}, dimensions={0} | all-to-all | bytes 1048576 | tf_op jit(solution)/shard_map/all_to_all | solution.py:107
  180.2 3.5 layer.19
  188.3 2.8 collective-permute-done.14
  195.5 7.3 %all-to-all-start.4 = ((bf16[32,16,128]{2,1,0:T(8,128)(2,1)}), bf16[32,16,128]{2,1,0:T(8,128)(2,1)S(1)}, u32[]{:S(2)}, u32[]{:S(2)}) async-start(bf16[32,16,128]{2,1,0:T(8,128)(2,1)} %broadcast_select_fusion.5), calls=%async_computation.4 | async-start | bytes 262144 | tf_op jit(solution)/shard_map/all_to_all | solution.py:107
  203.1 7.4 %all-to-all-done.4.refs_2_ = bf16[32,16,128]{2,1,0:T(8,128)(2,1)S(1)} async-done(((bf16[32,16,128]{2,1,0:T(8,128)(2,1)}), bf16[32,16,128]{2,1,0:T(8,128)(2,1)S(1)}, u32[]{:S(2)}, u32[]{:S(2)}) %all-to-all-start.4) | async-done | bytes 131104 | tf_op jit(solution)/shard_map/all_to_all | solution.py:107
  214.7 11.2 %all_to_all.82.refs_2_ = bf16[32,16,128]{2,1,0:T(8,128)(2,1)S(1)} all-to-all(bf16[32,16,128]{2,1,0:T(8,128)(2,1)S(1)} %get-tuple-element.60), channel_id=1, replica_groups=mesh['section'=8,'dom'=32] {'dom'}, dimensions={0} | all-to-all | bytes 262144 | tf_op jit(solution)/shard_map/all_to_all | solution.py:107
  227.8 11.2 %all_to_all.83.refs_2_ = bf16[32,16,128]{2,1,0:T(8,128)(2,1)S(1)} all-to-all(bf16[32,16,128]{2,1,0:T(8,128)(2,1)S(1)} %get-tuple-element.62), channel_id=1, replica_groups=mesh['section'=8,'dom'=32] {'dom'}, dimensions={0} | all-to-all | bytes 262144 | tf_op jit(solution)/shard_map/all_to_all | solution.py:107
  240.9 11.2 %all_to_all.84.refs_2_ = bf16[32,16,128]{2,1,0:T(8,128)(2,1)S(1)} all-to-all(bf16[32,16,128]{2,1,0:T(8,128)(2,1)S(1)} %get-tuple-element.64), channel_id=1, replica_groups=mesh['section'=8,'dom'=32] {'dom'}, dimensions={0} | all-to-all | bytes 262144 | tf_op jit(solution)/shard_map/all_to_all | solution.py:107
  254.7 3.9 %all-to-all-start.8 = ((bf16[32,16,128]{2,1,0:T(8,128)(2,1)}), bf16[32,16,128]{2,1,0:T(8,128)(2,1)S(1)}, u32[]{:S(2)}, u32[]{:S(2)}) async-start(bf16[32,16,128]{2,1,0:T(8,128)(2,1)} %get-tuple-element.66), calls=%async_computation.8 | async-start | bytes 262144 | tf_op jit(solution)/shard_map/all_to_all | solution.py:107
  258.6 7.8 %all-to-all-done.8.refs_2_ = bf16[32,16,128]{2,1,0:T(8,128)(2,1)S(1)} async-done(((bf16[32,16,128]{2,1,0:T(8,128)(2,1)}), bf16[32,16,128]{2,1,0:T(8,128)(2,1)S(1)}, u32[]{:S(2)}, u32[]{:S(2)}) %all-to-all-start.8) | async-done | bytes 131104 | tf_op jit(solution)/shard_map/all_to_all | solution.py:107
  270.5 11.2 %all_to_all.85.refs_2_ = bf16[32,16,128]{2,1,0:T(8,128)(2,1)S(1)} all-to-all(bf16[32,16,128]{2,1,0:T(8,128)(2,1)S(1)} %get-tuple-element.68), channel_id=1, replica_groups=mesh['section'=8,'dom'=32] {'dom'}, dimensions={0} | all-to-all | bytes 262144 | tf_op jit(solution)/shard_map/all_to_all | solution.py:107
  283.6 11.2 %all_to_all.86.refs_2_ = bf16[32,16,128]{2,1,0:T(8,128)(2,1)S(1)} all-to-all(bf16[32,16,128]{2,1,0:T(8,128)(2,1)S(1)} %get-tuple-element.70), channel_id=1, replica_groups=mesh['section'=8,'dom'=32] {'dom'}, dimensions={0} | all-to-all | bytes 262144 | tf_op jit(solution)/shard_map/all_to_all | solution.py:107
  296.8 11.2 %all_to_all.87.refs_2_ = bf16[32,16,128]{2,1,0:T(8,128)(2,1)S(1)} all-to-all(bf16[32,16,128]{2,1,0:T(8,128)(2,1)S(1)} %get-tuple-element.72), channel_id=1, replica_groups=mesh['section'=8,'dom'=32] {'dom'}, dimensions={0} | all-to-all | bytes 262144 | tf_op jit(solution)/shard_map/all_to_all | solution.py:107
  310.6 3.9 %all-to-all-start.12 = ((bf16[32,16,128]{2,1,0:T(8,128)(2,1)}), bf16[32,16,128]{2,1,0:T(8,128)(2,1)S(1)}, u32[]{:S(2)}, u32[]{:S(2)}) async-start(bf16[32,16,128]{2,1,0:T(8,128)(2,1)} %get-tuple-element.74), calls=%async_computation.12 | async-start | bytes 262144 | tf_op jit(solution)/shard_map/all_to_all | solution.py:107
  314.6 7.8 %all-to-all-done.12.refs_2_ = bf16[32,16,128]{2,1,0:T(8,128)(2,1)S(1)} async-done(((bf16[32,16,128]{2,1,0:T(8,128)(2,1)}), bf16[32,16,128]{2,1,0:T(8,128)(2,1)S(1)}, u32[]{:S(2)}, u32[]{:S(2)}) %all-to-all-start.12) | async-done | bytes 131104 | tf_op jit(solution)/shard_map/all_to_all | solution.py:107
  326.4 11.2 %all_to_all.88.refs_2_ = bf16[32,16,128]{2,1,0:T(8,128)(2,1)S(1)} all-to-all(bf16[32,16,128]{2,1,0:T(8,128)(2,1)S(1)} %get-tuple-element.76), channel_id=1, replica_groups=mesh['section'=8,'dom'=32] {'dom'}, dimensions={0} | all-to-all | bytes 262144 | tf_op jit(solution)/shard_map/all_to_all | solution.py:107
  339.6 11.2 %all_to_all.89.refs_2_ = bf16[32,16,128]{2,1,0:T(8,128)(2,1)S(1)} all-to-all(bf16[32,16,128]{2,1,0:T(8,128)(2,1)S(1)} %get-tuple-element.78), channel_id=1, replica_groups=mesh['section'=8,'dom'=32] {'dom'}, dimensions={0} | all-to-all | bytes 262144 | tf_op jit(solution)/shard_map/all_to_all | solution.py:107
  352.7 11.2 %all_to_all.90.refs_2_ = bf16[32,16,128]{2,1,0:T(8,128)(2,1)S(1)} all-to-all(bf16[32,16,128]{2,1,0:T(8,128)(2,1)S(1)} %get-tuple-element.80), channel_id=1, replica_groups=mesh['section'=8,'dom'=32] {'dom'}, dimensions={0} | all-to-all | bytes 262144 | tf_op jit(solution)/shard_map/all_to_all | solution.py:107
  (115 shorter events, 71.6 us)
Async XLA Ops:
  8.1 11.6 %copy-start.7 = (s32[2,1024,4]{1,2,0:T(4,128)S(1)}, s32[2,1024,4]{1,2,0:T(4,128)}, u32[]{:S(2)}) copy-start(s32[2,1024,4]{1,2,0:T(4,128)} %param.8) | copy-start | bytes 98308
  8.2 11.7 %copy-start.9 = (s32[2,32]{1,0:T(2,128)S(1)}, s32[2,32]{1,0:T(2,128)}, u32[]{:S(2)}) copy-start(s32[2,32]{1,0:T(2,128)} %param.9) | copy-start | bytes 772
  8.2 12.2 %copy-start.8 = (bf16[2,2048]{1,0:T(2,128)(2,1)S(1)}, bf16[2,2048]{1,0:T(2,128)(2,1)}, u32[]{:S(2)}) copy-start(bf16[2,2048]{1,0:T(2,128)(2,1)} %param.7) | copy-start | bytes 24580
  8.2 14.3 %copy-start.6 = (bf16[2,32,64,256]{3,2,1,0:T(8,128)(2,1)S(1)}, bf16[2,32,64,256]{3,2,1,0:T(8,128)(2,1)}, u32[]{:S(2)}) copy-start(bf16[2,32,64,256]{3,2,1,0:T(8,128)(2,1)} %param.6) | copy-start | bytes 6291460
  8.2 37.8 %collective-permute-start.1 = (bf16[32,16,128]{2,1,0:T(8,128)(2,1)S(1)}, bf16[32,16,128]{2,1,0:T(8,128)(2,1)S(1)}, u32[]{:S(2)}, u32[]{:S(2)}) collective-permute-start(bf16[32,16,128]{2,1,0:T(8,128)(2,1)S(1)} %reshape.129), channel_id=1, source_target_pairs={{64,0},{96,32},{65,1},{97,33},{66,2},{98,34},{67,3},{99,35},{68,4}... | collective-permute-start | bytes 393224 | tf_op jit(solution)/shard_map/ppermute | solution.py:162
  9.6 37.8 %collective-permute-start.2 = (bf16[32,16,128]{2,1,0:T(8,128)(2,1)S(1)}, bf16[32,16,128]{2,1,0:T(8,128)(2,1)S(1)}, u32[]{:S(2)}, u32[]{:S(2)}) collective-permute-start(bf16[32,16,128]{2,1,0:T(8,128)(2,1)S(1)} %reshape.129), channel_id=1, source_target_pairs={{128,0},{160,32},{129,1},{161,33},{130,2},{162,34},{131,3},{163,35... | collective-permute-start | bytes 393224 | tf_op jit(solution)/shard_map/ppermute | solution.py:162
  10.9 37.8 %collective-permute-start.3 = (bf16[32,16,128]{2,1,0:T(8,128)(2,1)S(1)}, bf16[32,16,128]{2,1,0:T(8,128)(2,1)S(1)}, u32[]{:S(2)}, u32[]{:S(2)}) collective-permute-start(bf16[32,16,128]{2,1,0:T(8,128)(2,1)S(1)} %reshape.129), channel_id=1, source_target_pairs={{192,0},{224,32},{193,1},{225,33},{194,2},{226,34},{195,3},{227,35... | collective-permute-start | bytes 393224 | tf_op jit(solution)/shard_map/ppermute | solution.py:162
  15.4 48.2 %collective-permute-start.4 = (bf16[32,64,256]{2,1,0:T(8,128)(2,1)}, bf16[32,64,256]{2,1,0:T(8,128)(2,1)}, u32[]{:S(2)}, u32[]{:S(2)}) collective-permute-start(bf16[32,64,256]{2,1,0:T(8,128)(2,1)} %get-tuple-element.89), channel_id=1, source_target_pairs={{0,32},{32,0},{1,33},{33,1},{2,34},{34,2},{3,35},{35,3},{4,36},{36... | collective-permute-start | bytes 3145736 | tf_op jit(solution)/shard_map/ppermute | solution.py:168
  20.4 24.2 %collective-permute-start = (bf16[2,3072]{1,0:T(2,128)(2,1)S(1)}, bf16[2,3072]{1,0:T(2,128)(2,1)S(1)}, u32[]{:S(2)}, u32[]{:S(2)}) collective-permute-start(bf16[2,3072]{1,0:T(2,128)(2,1)S(1)} %fusion.11), channel_id=1, source_target_pairs={{0,32},{32,0},{1,33},{33,1},{2,34},{34,2},{3,35},{35,3},{4,36},{36... | collective-permute-start | bytes 36872 | tf_op jit(solution)/shard_map/ppermute | solution.py:165
  44.6 40.4 %collective-permute-start.10 = (bf16[2,256,256]{2,1,0:T(8,128)(2,1)}, bf16[2,256,256]{2,1,0:T(8,128)(2,1)}, u32[]{:S(2)}, u32[]{:S(2)}) collective-permute-start(bf16[2,256,256]{2,1,0:T(8,128)(2,1)} %get-tuple-element.91), channel_id=1, source_target_pairs={{64,0},{96,32},{128,64},{160,96},{192,128},{224,160},{65,1},{97,33... | collective-permute-start | bytes 786440 | tf_op jit(solution)/shard_map/ppermute | solution.py:175
  46.0 40.4 %collective-permute-start.11 = (bf16[2,256,256]{2,1,0:T(8,128)(2,1)}, bf16[2,256,256]{2,1,0:T(8,128)(2,1)}, u32[]{:S(2)}, u32[]{:S(2)}) collective-permute-start(bf16[2,256,256]{2,1,0:T(8,128)(2,1)} %get-tuple-element.90), channel_id=1, source_target_pairs={{64,32},{96,64},{128,96},{160,128},{192,160},{224,192},{65,33},{97... | collective-permute-start | bytes 786440 | tf_op jit(solution)/shard_map/ppermute | solution.py:175
  47.4 40.3 %collective-permute-start.5 = (bf16[2,256,256]{2,1,0:T(8,128)(2,1)}, bf16[2,256,256]{2,1,0:T(8,128)(2,1)}, u32[]{:S(2)}, u32[]{:S(2)}) collective-permute-start(bf16[2,256,256]{2,1,0:T(8,128)(2,1)} %get-tuple-element.96), channel_id=1, source_target_pairs={{64,96},{96,128},{128,160},{160,192},{192,224},{224,0},{65,97},{97... | collective-permute-start | bytes 786440 | tf_op jit(solution)/shard_map/ppermute | solution.py:175
  48.7 83.7 %collective-permute-start.12 = (bf16[32,64,256]{2,1,0:T(8,128)(2,1)}, bf16[32,64,256]{2,1,0:T(8,128)(2,1)}, u32[]{:S(2)}, u32[]{:S(2)}) collective-permute-start(bf16[32,64,256]{2,1,0:T(8,128)(2,1)} %get-tuple-element.88), channel_id=1, source_target_pairs={{0,32},{32,0},{1,33},{33,1},{2,34},{34,2},{3,35},{35,3},{4,36},{36... | collective-permute-start | bytes 3145736 | tf_op jit(solution)/shard_map/ppermute | solution.py:168
  54.5 20.4 %all-to-all-start = ((bf16[32,64,128]{2,1,0:T(8,128)(2,1)}), bf16[32,64,128]{2,1,0:T(8,128)(2,1)S(1)}, u32[]{:S(2)}, u32[]{:S(2)}) async-start(bf16[32,64,128]{2,1,0:T(8,128)(2,1)} %broadcast_select_fusion.4), calls=%async_computation | async-start | bytes 1048576 | tf_op jit(solution)/shard_map/all_to_all | solution.py:107
  80.0 52.4 %all-to-all-start.1 = ((bf16[32,64,128]{2,1,0:T(8,128)(2,1)}), bf16[32,64,128]{2,1,0:T(8,128)(2,1)S(1)}, u32[]{:S(2)}, u32[]{:S(2)}) async-start(bf16[32,64,128]{2,1,0:T(8,128)(2,1)} %copy-done.3), calls=%async_computation.1 | async-start | bytes 1048576 | tf_op jit(solution)/shard_map/all_to_all | solution.py:107
  83.7 109.3 %all-gather.9.cloned.1.call-start = ((), (), s32[]{:S(2)}) async-start(), calls=%async_computation.18 | async-start | bytes 4866048 | tf_op jit(solution)/shard_map/all_gather | solution.py:200
  83.8 17.0 %collective-permute-start.6 = (bf16[2,256,256]{2,1,0:T(8,128)(2,1)}, bf16[2,256,256]{2,1,0:T(8,128)(2,1)S(1)}, u32[]{:S(2)}, u32[]{:S(2)}) collective-permute-start(bf16[2,256,256]{2,1,0:T(8,128)(2,1)} %get-tuple-element.95), channel_id=1, source_target_pairs={{64,128},{96,160},{128,192},{160,224},{192,0},{224,32},{65,129},{9... | collective-permute-start | bytes 786440 | tf_op jit(solution)/shard_map/ppermute | solution.py:175
  85.1 29.0 %collective-permute-start.7 = (bf16[2,256,256]{2,1,0:T(8,128)(2,1)}, bf16[2,256,256]{2,1,0:T(8,128)(2,1)S(1)}, u32[]{:S(2)}, u32[]{:S(2)}) collective-permute-start(bf16[2,256,256]{2,1,0:T(8,128)(2,1)} %get-tuple-element.94), channel_id=1, source_target_pairs={{64,160},{96,192},{128,224},{160,0},{192,32},{224,64},{65,161},{97... | collective-permute-start | bytes 786440 | tf_op jit(solution)/shard_map/ppermute | solution.py:175
  86.4 46.1 %collective-permute-start.8 = (bf16[2,256,256]{2,1,0:T(8,128)(2,1)}, bf16[2,256,256]{2,1,0:T(8,128)(2,1)S(1)}, u32[]{:S(2)}, u32[]{:S(2)}) collective-permute-start(bf16[2,256,256]{2,1,0:T(8,128)(2,1)} %get-tuple-element.93), channel_id=1, source_target_pairs={{64,192},{96,224},{128,0},{160,32},{192,64},{224,96},{65,193},{97,... | collective-permute-start | bytes 786440 | tf_op jit(solution)/shard_map/ppermute | solution.py:175
  87.7 44.8 %collective-permute-start.9 = (bf16[2,256,256]{2,1,0:T(8,128)(2,1)}, bf16[2,256,256]{2,1,0:T(8,128)(2,1)S(1)}, u32[]{:S(2)}, u32[]{:S(2)}) collective-permute-start(bf16[2,256,256]{2,1,0:T(8,128)(2,1)} %get-tuple-element.92), channel_id=1, source_target_pairs={{64,224},{96,0},{128,32},{160,64},{192,96},{224,128},{65,225},{97,... | collective-permute-start | bytes 786440 | tf_op jit(solution)/shard_map/ppermute | solution.py:175
  135.8 122.9 %all-gather.5.cloned.1.call-start = ((), (), s32[]{:S(2)}) async-start(), calls=%async_computation.16 | async-start | bytes 4718592 | tf_op jit(solution)/shard_map/all_gather | solution.py:200
  136.5 178.0 %all-gather.7.cloned.1.call-start = ((), (), s32[]{:S(2)}) async-start(), calls=%async_computation.17 | async-start | bytes 4718592 | tf_op jit(solution)/shard_map/all_gather | solution.py:200
  137.3 1.8 copy-start.5
  183.7 4.6 %collective-permute-start.13 = (bf16[32,16,128]{2,1,0:T(8,128)(2,1)S(1)}, bf16[32,16,128]{2,1,0:T(8,128)(2,1)S(1)}, u32[]{:S(2)}, u32[]{:S(2)}) collective-permute-start(bf16[32,16,128]{2,1,0:T(8,128)(2,1)S(1)} %get-tuple-element.99), channel_id=1, source_target_pairs={{0,64},{32,96},{1,65},{33,97},{2,66},{34,98},{3,67},{35,99},{4,68}... | collective-permute-start | bytes 393224 | tf_op jit(solution)/shard_map/ppermute | solution.py:207
  185.0 6.1 %collective-permute-start.14 = (bf16[32,16,128]{2,1,0:T(8,128)(2,1)S(1)}, bf16[32,16,128]{2,1,0:T(8,128)(2,1)S(1)}, u32[]{:S(2)}, u32[]{:S(2)}) collective-permute-start(bf16[32,16,128]{2,1,0:T(8,128)(2,1)S(1)} %get-tuple-element.98), channel_id=1, source_target_pairs={{0,128},{32,160},{1,129},{33,161},{2,130},{34,162},{3,131},{35,163... | collective-permute-start | bytes 393224 | tf_op jit(solution)/shard_map/ppermute | solution.py:207
  186.3 6.7 %collective-permute-start.15 = (bf16[32,16,128]{2,1,0:T(8,128)(2,1)S(1)}, bf16[32,16,128]{2,1,0:T(8,128)(2,1)S(1)}, u32[]{:S(2)}, u32[]{:S(2)}) collective-permute-start(bf16[32,16,128]{2,1,0:T(8,128)(2,1)S(1)} %get-tuple-element.100), channel_id=1, source_target_pairs={{0,192},{32,224},{1,193},{33,225},{2,194},{34,226},{3,195},{35,227... | collective-permute-start | bytes 393224 | tf_op jit(solution)/shard_map/ppermute | solution.py:207
  195.5 15.0 %all-to-all-start.4 = ((bf16[32,16,128]{2,1,0:T(8,128)(2,1)}), bf16[32,16,128]{2,1,0:T(8,128)(2,1)S(1)}, u32[]{:S(2)}, u32[]{:S(2)}) async-start(bf16[32,16,128]{2,1,0:T(8,128)(2,1)} %broadcast_select_fusion.5), calls=%async_computation.4 | async-start | bytes 262144 | tf_op jit(solution)/shard_map/all_to_all | solution.py:107
  210.5 2.3 copy-start
  254.7 11.7 %all-to-all-start.8 = ((bf16[32,16,128]{2,1,0:T(8,128)(2,1)}), bf16[32,16,128]{2,1,0:T(8,128)(2,1)S(1)}, u32[]{:S(2)}, u32[]{:S(2)}) async-start(bf16[32,16,128]{2,1,0:T(8,128)(2,1)} %get-tuple-element.66), calls=%async_computation.8 | async-start | bytes 262144 | tf_op jit(solution)/shard_map/all_to_all | solution.py:107
  266.4 2.2 copy-start.2
  310.6 11.7 %all-to-all-start.12 = ((bf16[32,16,128]{2,1,0:T(8,128)(2,1)}), bf16[32,16,128]{2,1,0:T(8,128)(2,1)S(1)}, u32[]{:S(2)}, u32[]{:S(2)}) async-start(bf16[32,16,128]{2,1,0:T(8,128)(2,1)} %get-tuple-element.74), calls=%async_computation.12 | async-start | bytes 262144 | tf_op jit(solution)/shard_map/all_to_all | solution.py:107
  322.3 2.2 copy-start.1
  (2 other events, 1.6 us)
Sparse Core Ops, SparseCore 0:
  135.9 55.9 all-gather.8
  193.6 55.2 all-gather.4
  250.7 53.3 all-gather.6

commit v5 on v4

--- a/solution.py
+++ b/solution.py
@@ -184,22 +184,18 @@
 
     cur = jnp.concatenate(shares, axis=1)
     send = jnp.take(cur, pair_words[0, words:], axis=0)
-    chunk = 4
+    edges = [early, 7, 11, 15, total]
     for layer in range(early):
         arrived = exchange(send)
         if layer == 1:
             arrived, pieces, partner[1] = lax.optimization_barrier((arrived, pieces, partner[1]))
             held = place(here, pieces).reshape(total * rows, width)
-            filled = {}
-            for c in range(early, total, chunk):
-                part = held[c * rows : (c + chunk) * rows]
-                if c == early:
-                    lines = table.reshape(-1, width)
-                    lines = jnp.pad(lines, ((0, -lines.shape[0] % 16), (0, 0)))
-                    part = jnp.concatenate([part, lines], axis=0)
-                filled[c] = lax.all_gather(part, "section", axis=0, tiled=False)
+            lines = table.reshape(-1, width)
+            lines = jnp.pad(lines, ((0, -lines.shape[0] % 16), (0, 0)))
+            part = jnp.concatenate([held[early * rows : edges[1] * rows], lines], axis=0)
+            filled = [lax.all_gather(part, "section", axis=0, tiled=False)]
         follow = layer + 1 if layer + 1 < early else None
-        cur, send = apply_layer(layer, 0, follow, 4, pair_words, cur, arrived, pair_bias, mine(layer))
+        cur, send = apply_layer(layer, 0, follow, 8, pair_words, cur, arrived, pair_bias, mine(layer))
 
     ready = cur.reshape(blocks, sections // 2, half, 2 * size)
     back = jnp.zeros_like(ready[:, 0])
@@ -207,14 +203,18 @@
         back = back + lax.ppermute(ready[:, k], "section", [(0, 2 * k), (1, 2 * k + 1)])
     cur = jnp.where(here < 2, ready[:, 0], back)
 
-    flat = filled[early][:, chunk * rows : chunk * rows + table.size // width].reshape(total, -1)
+    cur, held = lax.optimization_barrier((cur, held))
+    for first, end in zip(edges[1:], edges[2:]):
+        filled.append(lax.all_gather(held[first * rows : end * rows], "section", axis=0, tiled=False))
+    at = (edges[1] - early) * rows
+    flat = filled[0][:, at : at + table.size // width].reshape(total, -1)
     all_bias, table = split_table(flat, blocks, size, slots, parts)
     send = jnp.take(cur, table[early, words:], axis=0)
     for layer in range(early, total):
-        step = (layer - early) % chunk
+        chunk = sum(layer >= edge for edge in edges) - 1
         follow = layer + 1 if layer + 1 < total else None
         cur, send = apply_layer(
-            layer, step, follow, 16, table, cur, exchange(send), all_bias, filled[layer - step]
+            layer, layer - edges[chunk], follow, 16, table, cur, exchange(send), all_bias, filled[chunk]
         )
     out = cur.reshape(blocks, half, 2, size).transpose(2, 1, 0, 3)
     return out.reshape(images.shape)
@@ -228,6 +228,4 @@
         P("section", None, None),
         P("section", "dom"),
     )
-    return jax.shard_map(
-        shards, mesh=mesh, in_specs=placed, out_specs=P("section", None, "dom"), check_vma=False
-    )
+    return jax.shard_map(shards, mesh=mesh, in_specs=placed, out_specs=P("section", None, "dom"), check_vma=False)

time: 375 us -> 377 us (level)
  local copies, waits for them, and re-layouts: 19.6 us -> 32.5 us
  waiting for transfers between devices: 104 us -> 98.7 us
    unnamed x23 -> x49, local copies, waits for them, and re-layouts: 8.38 us -> 19.4 us
  transfers between devices with their start and end apart: 24 -> 25, of which waited for: 11 -> 11; matrix products, arithmetic and copies ran while one was open for 4% -> 5% of each run, Pallas kernels for 8% -> 9%
where the time goes in v5:
time: 377 us; the launch traced here: 375 us
  blocking collectives  135 us (36%)
  waiting for transfers between devices  98.7 us (26%)
  starting transfers between devices  52.4 us (14%)
  Pallas kernels  35.7 us (9%)
  local copies, waits for them, and re-layouts  32.5 us (9%)
  between operations  13.9 us (4%)
  other arithmetic  6.59 us (2%)
    all_to_all x11, blocking collectives, exchange(): return lax.all_to_all(send, 'dom', split_axis=0, concat_axis=0, tiled=True)  135 us
    ppermute x7, waiting for transfers between devices, shards(): pieces.append(lax.ppermute(piece, 'section', pairs))  42 us
    pallas_call x16, Pallas kernels, apply_layer(): pl.pallas_call(body, out_shape=[tile] * n_out, in_specs=[pl.BlockSpec(mem...  34.4 us
    all_to_all x5, waiting for transfers between devices, exchange(): return lax.all_to_all(send, 'dom', split_axis=0, concat_axis=0, tiled=True)  30.1 us
    all_to_all x5, starting transfers between devices, exchange(): return lax.all_to_all(send, 'dom', split_axis=0, concat_axis=0, tiled=True)  24.8 us
    ppermute x1, waiting for transfers between devices, shards(): other = lax.ppermute(table, 'section', pair)  19.8 us
    unnamed x49, local copies, waits for them, and re-layouts  19.4 us
    ppermute x7, starting transfers between devices, shards(): pieces.append(lax.ppermute(piece, 'section', pairs))  9.11 us
  transfers between devices with their start and end apart: 25, of which 11 were waited for; matrix products, arithmetic and copies ran while one was open for 5% of the time, Pallas kernels for 9%

profile of v5, /device:TPU:1, one launch (start us, length us, event | category | flops | bytes accessed | tf_op | source)
XLA Modules:
  0.0 375.1 jit_solution(16832311020213709668)
XLA Ops:
  12.8 2.7 slice_bitcast_fusion
  15.6 4.4 %collective-permute-start.4 = (bf16[32,64,256]{2,1,0:T(8,128)(2,1)S(1)}, bf16[32,64,256]{2,1,0:T(8,128)(2,1)}, u32[]{:S(2)}, u32[]{:S(2)}) collective-permute-start(bf16[32,64,256]{2,1,0:T(8,128)(2,1)S(1)} %get-tuple-element.92), channel_id=1, source_target_pairs={{0,32},{32,0},{1,33},{33,1},{2,34},{34,2},{3,35},{35,3},{4,36},{36... | collective-permute-start | bytes 3145736 | tf_op jit(solution)/shard_map/ppermute | solution.py:168
  24.9 19.8 %collective-permute-done = bf16[2,3072]{1,0:T(2,128)(2,1)S(1)} collective-permute-done((bf16[2,3072]{1,0:T(2,128)(2,1)S(1)}, bf16[2,3072]{1,0:T(2,128)(2,1)S(1)}, u32[]{:S(2)}, u32[]{:S(2)}) %collective-permute-start) | collective-permute-done | bytes 12320 | tf_op jit(solution)/shard_map/ppermute | solution.py:165
  50.6 4.2 %collective-permute-start.12 = (bf16[32,64,256]{2,1,0:T(8,128)(2,1)}, bf16[32,64,256]{2,1,0:T(8,128)(2,1)}, u32[]{:S(2)}, u32[]{:S(2)}) collective-permute-start(bf16[32,64,256]{2,1,0:T(8,128)(2,1)} %get-tuple-element.91), channel_id=1, source_target_pairs={{0,32},{32,0},{1,33},{33,1},{2,34},{34,2},{3,35},{35,3},{4,36},{36... | collective-permute-start | bytes 3145736 | tf_op jit(solution)/shard_map/ppermute | solution.py:168
  57.4 8.8 %all-to-all-start = ((bf16[32,64,128]{2,1,0:T(8,128)(2,1)}), bf16[32,64,128]{2,1,0:T(8,128)(2,1)S(1)}, u32[]{:S(2)}, u32[]{:S(2)}) async-start(bf16[32,64,128]{2,1,0:T(8,128)(2,1)} %broadcast_select_fusion.4), calls=%async_computation | async-start | bytes 1048576 | tf_op jit(solution)/shard_map/all_to_all | solution.py:107
  68.1 9.7 %all-to-all-done.refs_2_ = bf16[32,64,128]{2,1,0:T(8,128)(2,1)S(1)} async-done(((bf16[32,64,128]{2,1,0:T(8,128)(2,1)}), bf16[32,64,128]{2,1,0:T(8,128)(2,1)S(1)}, u32[]{:S(2)}, u32[]{:S(2)}) %all-to-all-start) | async-done | bytes 524320 | tf_op jit(solution)/shard_map/all_to_all | solution.py:107
  81.9 3.7 all-to-all-start.1
  90.9 11.7 %collective-permute-done.6.refs_2_ = bf16[2,256,256]{2,1,0:T(8,128)(2,1)S(1)} collective-permute-done((bf16[2,256,256]{2,1,0:T(8,128)(2,1)}, bf16[2,256,256]{2,1,0:T(8,128)(2,1)S(1)}, u32[]{:S(2)}, u32[]{:S(2)}) %collective-permute-start.6) | collective-permute-done | bytes 262176 | tf_op jit(solution)/shard_map/ppermute | solution.py:175
  103.3 12.6 %collective-permute-done.7.refs_3_ = bf16[2,256,256]{2,1,0:T(8,128)(2,1)S(1)} collective-permute-done((bf16[2,256,256]{2,1,0:T(8,128)(2,1)}, bf16[2,256,256]{2,1,0:T(8,128)(2,1)S(1)}, u32[]{:S(2)}, u32[]{:S(2)}) %collective-permute-start.7) | collective-permute-done | bytes 262176 | tf_op jit(solution)/shard_map/ppermute | solution.py:175
  116.6 17.7 %collective-permute-done.8.refs_4_ = bf16[2,256,256]{2,1,0:T(8,128)(2,1)S(1)} collective-permute-done((bf16[2,256,256]{2,1,0:T(8,128)(2,1)}, bf16[2,256,256]{2,1,0:T(8,128)(2,1)S(1)}, u32[]{:S(2)}, u32[]{:S(2)}) %collective-permute-start.8) | collective-permute-done | bytes 262176 | tf_op jit(solution)/shard_map/ppermute | solution.py:175
  144.4 2.6 layer.17
  147.1 19.1 %all_to_all.80.refs_2_ = bf16[32,64,128]{2,1,0:T(8,128)(2,1)S(1)} all-to-all(bf16[32,64,128]{2,1,0:T(8,128)(2,1)S(1)} %get-tuple-element.58), channel_id=1, replica_groups=mesh['section'=8,'dom'=32] {'dom'}, dimensions={0} | all-to-all | bytes 1048576 | tf_op jit(solution)/shard_map/all_to_all | solution.py:107
  166.1 2.6 layer.18
  168.7 15.0 %all_to_all.81.refs_2_ = bf16[32,64,128]{2,1,0:T(8,128)(2,1)S(1)} all-to-all(bf16[32,64,128]{2,1,0:T(8,128)(2,1)S(1)} %get-tuple-element.60), channel_id=1, replica_groups=mesh['section'=8,'dom'=32] {'dom'}, dimensions={0} | all-to-all | bytes 1048576 | tf_op jit(solution)/shard_map/all_to_all | solution.py:107
  183.8 2.6 layer.19
  191.0 2.8 collective-permute-done.14
  198.9 4.5 %all-to-all-start.4 = ((bf16[32,16,128]{2,1,0:T(8,128)(2,1)}), bf16[32,16,128]{2,1,0:T(8,128)(2,1)S(1)}, u32[]{:S(2)}, u32[]{:S(2)}) async-start(bf16[32,16,128]{2,1,0:T(8,128)(2,1)} %broadcast_select_fusion.5), calls=%async_computation.4 | async-start | bytes 262144 | tf_op jit(solution)/shard_map/all_to_all | solution.py:107
  203.7 7.4 %all-to-all-done.4.refs_2_ = bf16[32,16,128]{2,1,0:T(8,128)(2,1)S(1)} async-done(((bf16[32,16,128]{2,1,0:T(8,128)(2,1)}), bf16[32,16,128]{2,1,0:T(8,128)(2,1)S(1)}, u32[]{:S(2)}, u32[]{:S(2)}) %all-to-all-start.4) | async-done | bytes 131104 | tf_op jit(solution)/shard_map/all_to_all | solution.py:107
  214.9 11.2 %all_to_all.82.refs_2_ = bf16[32,16,128]{2,1,0:T(8,128)(2,1)S(1)} all-to-all(bf16[32,16,128]{2,1,0:T(8,128)(2,1)S(1)} %get-tuple-element.63), channel_id=1, replica_groups=mesh['section'=8,'dom'=32] {'dom'}, dimensions={0} | all-to-all | bytes 262144 | tf_op jit(solution)/shard_map/all_to_all | solution.py:107
  228.0 11.2 %all_to_all.83.refs_2_ = bf16[32,16,128]{2,1,0:T(8,128)(2,1)S(1)} all-to-all(bf16[32,16,128]{2,1,0:T(8,128)(2,1)S(1)} %get-tuple-element.65), channel_id=1, replica_groups=mesh['section'=8,'dom'=32] {'dom'}, dimensions={0} | all-to-all | bytes 262144 | tf_op jit(solution)/shard_map/all_to_all | solution.py:107
  241.1 11.2 %all_to_all.84.refs_2_ = bf16[32,16,128]{2,1,0:T(8,128)(2,1)S(1)} all-to-all(bf16[32,16,128]{2,1,0:T(8,128)(2,1)S(1)} %get-tuple-element.67), channel_id=1, replica_groups=mesh['section'=8,'dom'=32] {'dom'}, dimensions={0} | all-to-all | bytes 262144 | tf_op jit(solution)/shard_map/all_to_all | solution.py:107
  256.4 11.2 %all_to_all.85.refs_2_ = bf16[32,16,128]{2,1,0:T(8,128)(2,1)S(1)} all-to-all(bf16[32,16,128]{2,1,0:T(8,128)(2,1)S(1)} %get-tuple-element.70), channel_id=1, replica_groups=mesh['section'=8,'dom'=32] {'dom'}, dimensions={0} | all-to-all | bytes 262144 | tf_op jit(solution)/shard_map/all_to_all | solution.py:107
  269.6 11.2 %all_to_all.86.refs_2_ = bf16[32,16,128]{2,1,0:T(8,128)(2,1)S(1)} all-to-all(bf16[32,16,128]{2,1,0:T(8,128)(2,1)S(1)} %get-tuple-element.72), channel_id=1, replica_groups=mesh['section'=8,'dom'=32] {'dom'}, dimensions={0} | all-to-all | bytes 262144 | tf_op jit(solution)/shard_map/all_to_all | solution.py:107
  282.7 11.2 %all_to_all.87.refs_2_ = bf16[32,16,128]{2,1,0:T(8,128)(2,1)S(1)} all-to-all(bf16[32,16,128]{2,1,0:T(8,128)(2,1)S(1)} %get-tuple-element.74), channel_id=1, replica_groups=mesh['section'=8,'dom'=32] {'dom'}, dimensions={0} | all-to-all | bytes 262144 | tf_op jit(solution)/shard_map/all_to_all | solution.py:107
  294.0 2.6 layer.26
  296.6 3.9 %all-to-all-start.11 = ((bf16[32,16,128]{2,1,0:T(8,128)(2,1)}), bf16[32,16,128]{2,1,0:T(8,128)(2,1)S(1)}, u32[]{:S(2)}, u32[]{:S(2)}) async-start(bf16[32,16,128]{2,1,0:T(8,128)(2,1)} %get-tuple-element.76), calls=%async_computation.11 | async-start | bytes 262144 | tf_op jit(solution)/shard_map/all_to_all | solution.py:107
  303.0 5.3 %all-to-all-done.11.refs_2_ = bf16[32,16,128]{2,1,0:T(8,128)(2,1)S(1)} async-done(((bf16[32,16,128]{2,1,0:T(8,128)(2,1)}), bf16[32,16,128]{2,1,0:T(8,128)(2,1)S(1)}, u32[]{:S(2)}, u32[]{:S(2)}) %all-to-all-start.11) | async-done | bytes 131104 | tf_op jit(solution)/shard_map/all_to_all | solution.py:107
  312.4 11.2 %all_to_all.88.refs_2_ = bf16[32,16,128]{2,1,0:T(8,128)(2,1)S(1)} all-to-all(bf16[32,16,128]{2,1,0:T(8,128)(2,1)S(1)} %get-tuple-element.78), channel_id=1, replica_groups=mesh['section'=8,'dom'=32] {'dom'}, dimensions={0} | all-to-all | bytes 262144 | tf_op jit(solution)/shard_map/all_to_all | solution.py:107
  325.5 11.2 %all_to_all.89.refs_2_ = bf16[32,16,128]{2,1,0:T(8,128)(2,1)S(1)} all-to-all(bf16[32,16,128]{2,1,0:T(8,128)(2,1)S(1)} %get-tuple-element.80), channel_id=1, replica_groups=mesh['section'=8,'dom'=32] {'dom'}, dimensions={0} | all-to-all | bytes 262144 | tf_op jit(solution)/shard_map/all_to_all | solution.py:107
  338.7 11.2 %all_to_all.90.refs_2_ = bf16[32,16,128]{2,1,0:T(8,128)(2,1)S(1)} all-to-all(bf16[32,16,128]{2,1,0:T(8,128)(2,1)S(1)} %get-tuple-element.82), channel_id=1, replica_groups=mesh['section'=8,'dom'=32] {'dom'}, dimensions={0} | all-to-all | bytes 262144 | tf_op jit(solution)/shard_map/all_to_all | solution.py:107
  352.5 3.9 %all-to-all-start.15 = ((bf16[32,16,128]{2,1,0:T(8,128)(2,1)}), bf16[32,16,128]{2,1,0:T(8,128)(2,1)S(1)}, u32[]{:S(2)}, u32[]{:S(2)}) async-start(bf16[32,16,128]{2,1,0:T(8,128)(2,1)} %get-tuple-element.84), calls=%async_computation.15 | async-start | bytes 262144 | tf_op jit(solution)/shard_map/all_to_all | solution.py:107
  356.5 7.8 %all-to-all-done.15.refs_2_ = bf16[32,16,128]{2,1,0:T(8,128)(2,1)S(1)} async-done(((bf16[32,16,128]{2,1,0:T(8,128)(2,1)}), bf16[32,16,128]{2,1,0:T(8,128)(2,1)S(1)}, u32[]{:S(2)}, u32[]{:S(2)}) %all-to-all-start.15) | async-done | bytes 131104 | tf_op jit(solution)/shard_map/all_to_all | solution.py:107
  (146 shorter events, 84.8 us)
Async XLA Ops:
  8.8 11.1 %copy-start.20 = (s32[2,1024,4]{1,2,0:T(4,128)S(1)}, s32[2,1024,4]{1,2,0:T(4,128)}, u32[]{:S(2)}) copy-start(s32[2,1024,4]{1,2,0:T(4,128)} %param.8) | copy-start | bytes 98308
  8.8 11.3 %copy-start.22 = (s32[2,32]{1,0:T(2,128)S(1)}, s32[2,32]{1,0:T(2,128)}, u32[]{:S(2)}) copy-start(s32[2,32]{1,0:T(2,128)} %param.9) | copy-start | bytes 772
  8.8 11.8 %copy-start.21 = (bf16[2,2048]{1,0:T(2,128)(2,1)S(1)}, bf16[2,2048]{1,0:T(2,128)(2,1)}, u32[]{:S(2)}) copy-start(bf16[2,2048]{1,0:T(2,128)(2,1)} %param.7) | copy-start | bytes 24580
  8.8 13.9 %copy-start.19 = (bf16[2,32,64,256]{3,2,1,0:T(8,128)(2,1)S(1)}, bf16[2,32,64,256]{3,2,1,0:T(8,128)(2,1)}, u32[]{:S(2)}) copy-start(bf16[2,32,64,256]{3,2,1,0:T(8,128)(2,1)} %param.6) | copy-start | bytes 6291460
  8.8 37.3 %collective-permute-start.1 = (bf16[32,16,128]{2,1,0:T(8,128)(2,1)}, bf16[32,16,128]{2,1,0:T(8,128)(2,1)}, u32[]{:S(2)}, u32[]{:S(2)}) collective-permute-start(bf16[32,16,128]{2,1,0:T(8,128)(2,1)} %reshape.126), channel_id=1, source_target_pairs={{64,0},{96,32},{65,1},{97,33},{66,2},{98,34},{67,3},{99,35},{68,4}... | collective-permute-start | bytes 393224 | tf_op jit(solution)/shard_map/ppermute | solution.py:162
  10.2 38.2 %collective-permute-start.2 = (bf16[32,16,128]{2,1,0:T(8,128)(2,1)}, bf16[32,16,128]{2,1,0:T(8,128)(2,1)}, u32[]{:S(2)}, u32[]{:S(2)}) collective-permute-start(bf16[32,16,128]{2,1,0:T(8,128)(2,1)} %reshape.126), channel_id=1, source_target_pairs={{128,0},{160,32},{129,1},{161,33},{130,2},{162,34},{131,3},{163,35... | collective-permute-start | bytes 393224 | tf_op jit(solution)/shard_map/ppermute | solution.py:162
  11.5 39.1 %collective-permute-start.3 = (bf16[32,16,128]{2,1,0:T(8,128)(2,1)}, bf16[32,16,128]{2,1,0:T(8,128)(2,1)}, u32[]{:S(2)}, u32[]{:S(2)}) collective-permute-start(bf16[32,16,128]{2,1,0:T(8,128)(2,1)} %reshape.126), channel_id=1, source_target_pairs={{192,0},{224,32},{193,1},{225,33},{194,2},{226,34},{195,3},{227,35... | collective-permute-start | bytes 393224 | tf_op jit(solution)/shard_map/ppermute | solution.py:162
  15.6 50.8 %collective-permute-start.4 = (bf16[32,64,256]{2,1,0:T(8,128)(2,1)S(1)}, bf16[32,64,256]{2,1,0:T(8,128)(2,1)}, u32[]{:S(2)}, u32[]{:S(2)}) collective-permute-start(bf16[32,64,256]{2,1,0:T(8,128)(2,1)S(1)} %get-tuple-element.92), channel_id=1, source_target_pairs={{0,32},{32,0},{1,33},{33,1},{2,34},{34,2},{3,35},{35,3},{4,36},{36... | collective-permute-start | bytes 3145736 | tf_op jit(solution)/shard_map/ppermute | solution.py:168
  20.6 24.1 %collective-permute-start = (bf16[2,3072]{1,0:T(2,128)(2,1)S(1)}, bf16[2,3072]{1,0:T(2,128)(2,1)S(1)}, u32[]{:S(2)}, u32[]{:S(2)}) collective-permute-start(bf16[2,3072]{1,0:T(2,128)(2,1)S(1)} %fusion.11), channel_id=1, source_target_pairs={{0,32},{32,0},{1,33},{33,1},{2,34},{34,2},{3,35},{35,3},{4,36},{36... | collective-permute-start | bytes 36872 | tf_op jit(solution)/shard_map/ppermute | solution.py:165
  44.7 42.2 %collective-permute-start.10 = (bf16[2,256,256]{2,1,0:T(8,128)(2,1)}, bf16[2,256,256]{2,1,0:T(8,128)(2,1)}, u32[]{:S(2)}, u32[]{:S(2)}) collective-permute-start(bf16[2,256,256]{2,1,0:T(8,128)(2,1)} %get-tuple-element.94), channel_id=1, source_target_pairs={{64,0},{96,32},{128,64},{160,96},{192,128},{224,160},{65,1},{97,33... | collective-permute-start | bytes 786440 | tf_op jit(solution)/shard_map/ppermute | solution.py:175
  46.1 42.1 %collective-permute-start.11 = (bf16[2,256,256]{2,1,0:T(8,128)(2,1)}, bf16[2,256,256]{2,1,0:T(8,128)(2,1)}, u32[]{:S(2)}, u32[]{:S(2)}) collective-permute-start(bf16[2,256,256]{2,1,0:T(8,128)(2,1)} %get-tuple-element.93), channel_id=1, source_target_pairs={{64,32},{96,64},{128,96},{160,128},{192,160},{224,192},{65,33},{97... | collective-permute-start | bytes 786440 | tf_op jit(solution)/shard_map/ppermute | solution.py:175
  48.4 41.2 %collective-permute-start.5 = (bf16[2,256,256]{2,1,0:T(8,128)(2,1)}, bf16[2,256,256]{2,1,0:T(8,128)(2,1)}, u32[]{:S(2)}, u32[]{:S(2)}) collective-permute-start(bf16[2,256,256]{2,1,0:T(8,128)(2,1)} %get-tuple-element.99), channel_id=1, source_target_pairs={{64,96},{96,128},{128,160},{160,192},{192,224},{224,0},{65,97},{97... | collective-permute-start | bytes 786440 | tf_op jit(solution)/shard_map/ppermute | solution.py:175
  50.6 85.1 %collective-permute-start.12 = (bf16[32,64,256]{2,1,0:T(8,128)(2,1)}, bf16[32,64,256]{2,1,0:T(8,128)(2,1)}, u32[]{:S(2)}, u32[]{:S(2)}) collective-permute-start(bf16[32,64,256]{2,1,0:T(8,128)(2,1)} %get-tuple-element.91), channel_id=1, source_target_pairs={{0,32},{32,0},{1,33},{33,1},{2,34},{34,2},{3,35},{35,3},{4,36},{36... | collective-permute-start | bytes 3145736 | tf_op jit(solution)/shard_map/ppermute | solution.py:168
  57.4 20.4 %all-to-all-start = ((bf16[32,64,128]{2,1,0:T(8,128)(2,1)}), bf16[32,64,128]{2,1,0:T(8,128)(2,1)S(1)}, u32[]{:S(2)}, u32[]{:S(2)}) async-start(bf16[32,64,128]{2,1,0:T(8,128)(2,1)} %broadcast_select_fusion.4), calls=%async_computation | async-start | bytes 1048576 | tf_op jit(solution)/shard_map/all_to_all | solution.py:107
  81.9 53.9 %all-to-all-start.1 = ((bf16[32,64,128]{2,1,0:T(8,128)(2,1)}), bf16[32,64,128]{2,1,0:T(8,128)(2,1)S(1)}, u32[]{:S(2)}, u32[]{:S(2)}) async-start(bf16[32,64,128]{2,1,0:T(8,128)(2,1)} %copy-done.8), calls=%async_computation.1 | async-start | bytes 1048576 | tf_op jit(solution)/shard_map/all_to_all | solution.py:107
  85.6 110.8 %all-gather.9.cloned.1.call-start = ((), (), s32[]{:S(2)}) async-start(), calls=%async_computation.16 | async-start | bytes 3686400 | tf_op jit(solution)/shard_map/all_gather | solution.py:196
  85.6 17.0 %collective-permute-start.6 = (bf16[2,256,256]{2,1,0:T(8,128)(2,1)}, bf16[2,256,256]{2,1,0:T(8,128)(2,1)S(1)}, u32[]{:S(2)}, u32[]{:S(2)}) collective-permute-start(bf16[2,256,256]{2,1,0:T(8,128)(2,1)} %get-tuple-element.98), channel_id=1, source_target_pairs={{64,128},{96,160},{128,192},{160,224},{192,0},{224,32},{65,129},{9... | collective-permute-start | bytes 786440 | tf_op jit(solution)/shard_map/ppermute | solution.py:175
  87.0 29.0 %collective-permute-start.7 = (bf16[2,256,256]{2,1,0:T(8,128)(2,1)}, bf16[2,256,256]{2,1,0:T(8,128)(2,1)S(1)}, u32[]{:S(2)}, u32[]{:S(2)}) collective-permute-start(bf16[2,256,256]{2,1,0:T(8,128)(2,1)} %get-tuple-element.97), channel_id=1, source_target_pairs={{64,160},{96,192},{128,224},{160,0},{192,32},{224,64},{65,161},{97... | collective-permute-start | bytes 786440 | tf_op jit(solution)/shard_map/ppermute | solution.py:175
  88.3 46.1 %collective-permute-start.8 = (bf16[2,256,256]{2,1,0:T(8,128)(2,1)}, bf16[2,256,256]{2,1,0:T(8,128)(2,1)S(1)}, u32[]{:S(2)}, u32[]{:S(2)}) collective-permute-start(bf16[2,256,256]{2,1,0:T(8,128)(2,1)} %get-tuple-element.96), channel_id=1, source_target_pairs={{64,192},{96,224},{128,0},{160,32},{192,64},{224,96},{65,193},{97,... | collective-permute-start | bytes 786440 | tf_op jit(solution)/shard_map/ppermute | solution.py:175
  89.6 45.5 %collective-permute-start.9 = (bf16[2,256,256]{2,1,0:T(8,128)(2,1)}, bf16[2,256,256]{2,1,0:T(8,128)(2,1)S(1)}, u32[]{:S(2)}, u32[]{:S(2)}) collective-permute-start(bf16[2,256,256]{2,1,0:T(8,128)(2,1)} %get-tuple-element.95), channel_id=1, source_target_pairs={{64,224},{96,0},{128,32},{160,64},{192,96},{224,128},{65,225},{97,... | collective-permute-start | bytes 786440 | tf_op jit(solution)/shard_map/ppermute | solution.py:175
  142.5 109.8 %all-gather.11.cloned.1.call-start = ((), (), s32[]{:S(2)}) async-start(), calls=%async_computation.17 | async-start | bytes 4718592 | tf_op jit(solution)/shard_map/all_gather | solution.py:208
  186.4 4.6 %collective-permute-start.13 = (bf16[32,16,128]{2,1,0:T(8,128)(2,1)S(1)}, bf16[32,16,128]{2,1,0:T(8,128)(2,1)S(1)}, u32[]{:S(2)}, u32[]{:S(2)}) collective-permute-start(bf16[32,16,128]{2,1,0:T(8,128)(2,1)S(1)} %get-tuple-element.102), channel_id=1, source_target_pairs={{0,64},{32,96},{1,65},{33,97},{2,66},{34,98},{3,67},{35,99},{4,68}... | collective-permute-start | bytes 393224 | tf_op jit(solution)/shard_map/ppermute | solution.py:203
  187.7 6.1 %collective-permute-start.14 = (bf16[32,16,128]{2,1,0:T(8,128)(2,1)S(1)}, bf16[32,16,128]{2,1,0:T(8,128)(2,1)S(1)}, u32[]{:S(2)}, u32[]{:S(2)}) collective-permute-start(bf16[32,16,128]{2,1,0:T(8,128)(2,1)S(1)} %get-tuple-element.101), channel_id=1, source_target_pairs={{0,128},{32,160},{1,129},{33,161},{2,130},{34,162},{3,131},{35,163... | collective-permute-start | bytes 393224 | tf_op jit(solution)/shard_map/ppermute | solution.py:203
  189.0 4.8 %collective-permute-start.15 = (bf16[32,16,128]{2,1,0:T(8,128)(2,1)S(1)}, bf16[32,16,128]{2,1,0:T(8,128)(2,1)S(1)}, u32[]{:S(2)}, u32[]{:S(2)}) collective-permute-start(bf16[32,16,128]{2,1,0:T(8,128)(2,1)S(1)} %get-tuple-element.103), channel_id=1, source_target_pairs={{0,192},{32,224},{1,193},{33,225},{2,194},{34,226},{3,195},{35,227... | collective-permute-start | bytes 393224 | tf_op jit(solution)/shard_map/ppermute | solution.py:203
  194.9 108.1 %all-gather.13.cloned.1.call-start = ((), (), s32[]{:S(2)}) async-start(), calls=%async_computation.18 | async-start | bytes 4718592 | tf_op jit(solution)/shard_map/all_gather | solution.py:208
  195.7 160.8 %all-gather.15.cloned.1.call-start = ((), (), s32[]{:S(2)}) async-start(), calls=%async_computation.19 | async-start | bytes 1179648 | tf_op jit(solution)/shard_map/all_gather | solution.py:208
  198.9 12.2 %all-to-all-start.4 = ((bf16[32,16,128]{2,1,0:T(8,128)(2,1)}), bf16[32,16,128]{2,1,0:T(8,128)(2,1)S(1)}, u32[]{:S(2)}, u32[]{:S(2)}) async-start(bf16[32,16,128]{2,1,0:T(8,128)(2,1)} %broadcast_select_fusion.5), calls=%async_computation.4 | async-start | bytes 262144 | tf_op jit(solution)/shard_map/all_to_all | solution.py:107
  252.4 2.2 copy-start.2
  254.6 13.1 %copy-start.3 = (bf16[8192,256]{1,0:T(8,128)(2,1)S(1)}, bf16[8192,256]{1,0:T(8,128)(2,1)}, u32[]{:S(2)}) copy-start(bf16[8192,256]{1,0:T(8,128)(2,1)} %all-gather.11.cloned.1.call-done) | copy-start | bytes 12582916
  296.6 11.7 %all-to-all-start.11 = ((bf16[32,16,128]{2,1,0:T(8,128)(2,1)}), bf16[32,16,128]{2,1,0:T(8,128)(2,1)S(1)}, u32[]{:S(2)}, u32[]{:S(2)}) async-start(bf16[32,16,128]{2,1,0:T(8,128)(2,1)} %get-tuple-element.76), calls=%async_computation.11 | async-start | bytes 262144 | tf_op jit(solution)/shard_map/all_to_all | solution.py:107
  310.5 13.2 %copy-start.1 = (bf16[8192,256]{1,0:T(8,128)(2,1)S(1)}, bf16[8192,256]{1,0:T(8,128)(2,1)}, u32[]{:S(2)}) copy-start(bf16[8192,256]{1,0:T(8,128)(2,1)} %all-gather.13.cloned.1.call-done) | copy-start | bytes 12582916
  352.5 11.7 %all-to-all-start.15 = ((bf16[32,16,128]{2,1,0:T(8,128)(2,1)}), bf16[32,16,128]{2,1,0:T(8,128)(2,1)S(1)}, u32[]{:S(2)}, u32[]{:S(2)}) async-start(bf16[32,16,128]{2,1,0:T(8,128)(2,1)} %get-tuple-element.84), calls=%async_computation.15 | async-start | bytes 262144 | tf_op jit(solution)/shard_map/all_to_all | solution.py:107
  (16 other events, 18.1 us)
Sparse Core Ops, SparseCore 0:
  142.7 42.2 all-gather.8
  195.0 52.7 all-gather.10
  249.6 53.3 all-gather.12
  304.6 32.8 all-gather.14

commit v6 on v5

--- a/solution.py
+++ b/solution.py
@@ -194,6 +194,7 @@
             lines = jnp.pad(lines, ((0, -lines.shape[0] % 16), (0, 0)))
             part = jnp.concatenate([held[early * rows : edges[1] * rows], lines], axis=0)
             filled = [lax.all_gather(part, "section", axis=0, tiled=False)]
+            parted = [held[first * rows : end * rows] for first, end in zip(edges[1:], edges[2:])]
         follow = layer + 1 if layer + 1 < early else None
         cur, send = apply_layer(layer, 0, follow, 8, pair_words, cur, arrived, pair_bias, mine(layer))
 
@@ -203,9 +204,8 @@
         back = back + lax.ppermute(ready[:, k], "section", [(0, 2 * k), (1, 2 * k + 1)])
     cur = jnp.where(here < 2, ready[:, 0], back)
 
-    cur, held = lax.optimization_barrier((cur, held))
-    for first, end in zip(edges[1:], edges[2:]):
-        filled.append(lax.all_gather(held[first * rows : end * rows], "section", axis=0, tiled=False))
+    cur, parted = lax.optimization_barrier((cur, parted))
+    filled += [lax.all_gather(part, "section", axis=0, tiled=False) for part in parted]
     at = (edges[1] - early) * rows
     flat = filled[0][:, at : at + table.size // width].reshape(total, -1)
     all_bias, table = split_table(flat, blocks, size, slots, parts)

time: 377 us -> 380 us (level)
  blocking collectives: 135 us -> 120 us
  waiting for transfers between devices: 98.7 us -> 109 us
    all_to_all x11 -> x10, blocking collectives: 135 us -> 120 us  [exchange(): return lax.all_to_all(send, 'dom', split_axis=0, concat_axis=0, tiled=True)]
    all_to_all x5 -> x6, waiting for transfers between devices: 30.1 us -> 41 us  [exchange(): return lax.all_to_all(send, 'dom', split_axis=0, concat_axis=0, tiled=True)]
    unnamed x49 -> x57, local copies, waits for them, and re-layouts: 19.4 us -> 23.2 us
    all_to_all x5 -> x6, starting transfers between devices: 24.8 us -> 27.7 us  [exchange(): return lax.all_to_all(send, 'dom', split_axis=0, concat_axis=0, tiled=True)]
  transfers between devices with their start and end apart: 25 -> 26, of which waited for: 11 -> 11; matrix products, arithmetic and copies ran while one was open for 5% -> 5% of each run, Pallas kernels for 9% -> 9%
where the time goes in v6:
time: 380 us; the launch traced here: 378 us
  blocking collectives  120 us (32%)
  waiting for transfers between devices  109 us (29%)
  starting transfers between devices  55.4 us (15%)
  local copies, waits for them, and re-layouts  36.3 us (10%)
  Pallas kernels  35.7 us (9%)
  between operations  13.9 us (4%)
  other arithmetic  7.59 us (2%)
    all_to_all x10, blocking collectives, exchange(): return lax.all_to_all(send, 'dom', split_axis=0, concat_axis=0, tiled=True)  120 us
    ppermute x7, waiting for transfers between devices, shards(): pieces.append(lax.ppermute(piece, 'section', pairs))  42 us
    all_to_all x6, waiting for transfers between devices, exchange(): return lax.all_to_all(send, 'dom', split_axis=0, concat_axis=0, tiled=True)  41 us
    pallas_call x16, Pallas kernels, apply_layer(): pl.pallas_call(body, out_shape=[tile] * n_out, in_specs=[pl.BlockSpec(mem...  34.4 us
    all_to_all x6, starting transfers between devices, exchange(): return lax.all_to_all(send, 'dom', split_axis=0, concat_axis=0, tiled=True)  27.7 us
    unnamed x57, local copies, waits for them, and re-layouts  23.2 us
    ppermute x1, waiting for transfers between devices, shards(): other = lax.ppermute(table, 'section', pair)  19.8 us
    ppermute x7, starting transfers between devices, shards(): pieces.append(lax.ppermute(piece, 'section', pairs))  9.11 us
  transfers between devices with their start and end apart: 26, of which 11 were waited for; matrix products, arithmetic and copies ran while one was open for 5% of the time, Pallas kernels for 9%

profile of v6, /device:TPU:1, one launch (start us, length us, event | category | flops | bytes accessed | tf_op | source)
XLA Modules:
  0.0 378.3 jit_solution(18196288244681448826)
XLA Ops:
  12.8 2.7 slice_bitcast_fusion
  15.6 4.4 %collective-permute-start.4 = (bf16[32,64,256]{2,1,0:T(8,128)(2,1)S(1)}, bf16[32,64,256]{2,1,0:T(8,128)(2,1)}, u32[]{:S(2)}, u32[]{:S(2)}) collective-permute-start(bf16[32,64,256]{2,1,0:T(8,128)(2,1)S(1)} %get-tuple-element.96), channel_id=1, source_target_pairs={{0,32},{32,0},{1,33},{33,1},{2,34},{34,2},{3,35},{35,3},{4,36},{36... | collective-permute-start | bytes 3145736 | tf_op jit(solution)/shard_map/ppermute | solution.py:168
  24.9 19.8 %collective-permute-done = bf16[2,3072]{1,0:T(2,128)(2,1)S(1)} collective-permute-done((bf16[2,3072]{1,0:T(2,128)(2,1)S(1)}, bf16[2,3072]{1,0:T(2,128)(2,1)S(1)}, u32[]{:S(2)}, u32[]{:S(2)}) %collective-permute-start) | collective-permute-done | bytes 12320 | tf_op jit(solution)/shard_map/ppermute | solution.py:165
  50.6 4.2 %collective-permute-start.12 = (bf16[32,64,256]{2,1,0:T(8,128)(2,1)}, bf16[32,64,256]{2,1,0:T(8,128)(2,1)}, u32[]{:S(2)}, u32[]{:S(2)}) collective-permute-start(bf16[32,64,256]{2,1,0:T(8,128)(2,1)} %get-tuple-element.95), channel_id=1, source_target_pairs={{0,32},{32,0},{1,33},{33,1},{2,34},{34,2},{3,35},{35,3},{4,36},{36... | collective-permute-start | bytes 3145736 | tf_op jit(solution)/shard_map/ppermute | solution.py:168
  57.4 8.8 %all-to-all-start = ((bf16[32,64,128]{2,1,0:T(8,128)(2,1)}), bf16[32,64,128]{2,1,0:T(8,128)(2,1)S(1)}, u32[]{:S(2)}, u32[]{:S(2)}) async-start(bf16[32,64,128]{2,1,0:T(8,128)(2,1)} %broadcast_select_fusion.4), calls=%async_computation | async-start | bytes 1048576 | tf_op jit(solution)/shard_map/all_to_all | solution.py:107
  68.1 9.7 %all-to-all-done.refs_2_ = bf16[32,64,128]{2,1,0:T(8,128)(2,1)S(1)} async-done(((bf16[32,64,128]{2,1,0:T(8,128)(2,1)}), bf16[32,64,128]{2,1,0:T(8,128)(2,1)S(1)}, u32[]{:S(2)}, u32[]{:S(2)}) %all-to-all-start) | async-done | bytes 524320 | tf_op jit(solution)/shard_map/all_to_all | solution.py:107
  81.9 3.7 all-to-all-start.1
  90.9 11.7 %collective-permute-done.6.refs_2_ = bf16[2,256,256]{2,1,0:T(8,128)(2,1)S(1)} collective-permute-done((bf16[2,256,256]{2,1,0:T(8,128)(2,1)}, bf16[2,256,256]{2,1,0:T(8,128)(2,1)S(1)}, u32[]{:S(2)}, u32[]{:S(2)}) %collective-permute-start.6) | collective-permute-done | bytes 262176 | tf_op jit(solution)/shard_map/ppermute | solution.py:175
  103.3 12.6 %collective-permute-done.7.refs_3_ = bf16[2,256,256]{2,1,0:T(8,128)(2,1)S(1)} collective-permute-done((bf16[2,256,256]{2,1,0:T(8,128)(2,1)}, bf16[2,256,256]{2,1,0:T(8,128)(2,1)S(1)}, u32[]{:S(2)}, u32[]{:S(2)}) %collective-permute-start.7) | collective-permute-done | bytes 262176 | tf_op jit(solution)/shard_map/ppermute | solution.py:175
  116.6 17.7 %collective-permute-done.8.refs_4_ = bf16[2,256,256]{2,1,0:T(8,128)(2,1)S(1)} collective-permute-done((bf16[2,256,256]{2,1,0:T(8,128)(2,1)}, bf16[2,256,256]{2,1,0:T(8,128)(2,1)S(1)}, u32[]{:S(2)}, u32[]{:S(2)}) %collective-permute-start.8) | collective-permute-done | bytes 262176 | tf_op jit(solution)/shard_map/ppermute | solution.py:175
  142.5 2.8 broadcast_select_fusion
  145.3 2.6 layer.17
  147.9 19.1 %all_to_all.80.refs_2_ = bf16[32,64,128]{2,1,0:T(8,128)(2,1)S(1)} all-to-all(bf16[32,64,128]{2,1,0:T(8,128)(2,1)S(1)} %get-tuple-element.60), channel_id=1, replica_groups=mesh['section'=8,'dom'=32] {'dom'}, dimensions={0} | all-to-all | bytes 1048576 | tf_op jit(solution)/shard_map/all_to_all | solution.py:107
  167.0 2.6 layer.18
  171.3 3.7 all-to-all-start.3
  175.0 11.5 %all-to-all-done.3.refs_2_ = bf16[32,64,128]{2,1,0:T(8,128)(2,1)S(1)} async-done(((bf16[32,64,128]{2,1,0:T(8,128)(2,1)}), bf16[32,64,128]{2,1,0:T(8,128)(2,1)S(1)}, u32[]{:S(2)}, u32[]{:S(2)}) %all-to-all-start.3) | async-done | bytes 524320 | tf_op jit(solution)/shard_map/all_to_all | solution.py:107
  202.6 3.8 %all-to-all-start.4 = ((bf16[32,16,128]{2,1,0:T(8,128)(2,1)}), bf16[32,16,128]{2,1,0:T(8,128)(2,1)S(1)}, u32[]{:S(2)}, u32[]{:S(2)}) async-start(bf16[32,16,128]{2,1,0:T(8,128)(2,1)} %broadcast_select_fusion.5), calls=%async_computation.4 | async-start | bytes 262144 | tf_op jit(solution)/shard_map/all_to_all | solution.py:107
  206.7 7.4 %all-to-all-done.4.refs_2_ = bf16[32,16,128]{2,1,0:T(8,128)(2,1)S(1)} async-done(((bf16[32,16,128]{2,1,0:T(8,128)(2,1)}), bf16[32,16,128]{2,1,0:T(8,128)(2,1)S(1)}, u32[]{:S(2)}, u32[]{:S(2)}) %all-to-all-start.4) | async-done | bytes 131104 | tf_op jit(solution)/shard_map/all_to_all | solution.py:107
  217.9 11.2 %all_to_all.81.refs_2_ = bf16[32,16,128]{2,1,0:T(8,128)(2,1)S(1)} all-to-all(bf16[32,16,128]{2,1,0:T(8,128)(2,1)S(1)} %get-tuple-element.65), channel_id=1, replica_groups=mesh['section'=8,'dom'=32] {'dom'}, dimensions={0} | all-to-all | bytes 262144 | tf_op jit(solution)/shard_map/all_to_all | solution.py:107
  231.1 11.2 %all_to_all.82.refs_2_ = bf16[32,16,128]{2,1,0:T(8,128)(2,1)S(1)} all-to-all(bf16[32,16,128]{2,1,0:T(8,128)(2,1)S(1)} %get-tuple-element.67), channel_id=1, replica_groups=mesh['section'=8,'dom'=32] {'dom'}, dimensions={0} | all-to-all | bytes 262144 | tf_op jit(solution)/shard_map/all_to_all | solution.py:107
  244.2 11.2 %all_to_all.83.refs_2_ = bf16[32,16,128]{2,1,0:T(8,128)(2,1)S(1)} all-to-all(bf16[32,16,128]{2,1,0:T(8,128)(2,1)S(1)} %get-tuple-element.69), channel_id=1, replica_groups=mesh['section'=8,'dom'=32] {'dom'}, dimensions={0} | all-to-all | bytes 262144 | tf_op jit(solution)/shard_map/all_to_all | solution.py:107
  259.5 11.5 %all_to_all.84.refs_2_ = bf16[32,16,128]{2,1,0:T(8,128)(2,1)S(1)} all-to-all(bf16[32,16,128]{2,1,0:T(8,128)(2,1)S(1)} %get-tuple-element.72), channel_id=1, replica_groups=mesh['section'=8,'dom'=32] {'dom'}, dimensions={0} | all-to-all | bytes 262144 | tf_op jit(solution)/shard_map/all_to_all | solution.py:107
  272.9 11.2 %all_to_all.85.refs_2_ = bf16[32,16,128]{2,1,0:T(8,128)(2,1)S(1)} all-to-all(bf16[32,16,128]{2,1,0:T(8,128)(2,1)S(1)} %get-tuple-element.74), channel_id=1, replica_groups=mesh['section'=8,'dom'=32] {'dom'}, dimensions={0} | all-to-all | bytes 262144 | tf_op jit(solution)/shard_map/all_to_all | solution.py:107
  286.0 11.2 %all_to_all.86.refs_2_ = bf16[32,16,128]{2,1,0:T(8,128)(2,1)S(1)} all-to-all(bf16[32,16,128]{2,1,0:T(8,128)(2,1)S(1)} %get-tuple-element.76), channel_id=1, replica_groups=mesh['section'=8,'dom'=32] {'dom'}, dimensions={0} | all-to-all | bytes 262144 | tf_op jit(solution)/shard_map/all_to_all | solution.py:107
  299.9 3.9 %all-to-all-start.11 = ((bf16[32,16,128]{2,1,0:T(8,128)(2,1)}), bf16[32,16,128]{2,1,0:T(8,128)(2,1)S(1)}, u32[]{:S(2)}, u32[]{:S(2)}) async-start(bf16[32,16,128]{2,1,0:T(8,128)(2,1)} %get-tuple-element.78), calls=%async_computation.11 | async-start | bytes 262144 | tf_op jit(solution)/shard_map/all_to_all | solution.py:107
  303.8 3.1 all-gather.13.cloned.1.call-done
  306.9 4.6 %all-to-all-done.11.refs_2_ = bf16[32,16,128]{2,1,0:T(8,128)(2,1)S(1)} async-done(((bf16[32,16,128]{2,1,0:T(8,128)(2,1)}), bf16[32,16,128]{2,1,0:T(8,128)(2,1)S(1)}, u32[]{:S(2)}, u32[]{:S(2)}) %all-to-all-start.11) | async-done | bytes 131104 | tf_op jit(solution)/shard_map/all_to_all | solution.py:107
  315.7 11.2 %all_to_all.87.refs_2_ = bf16[32,16,128]{2,1,0:T(8,128)(2,1)S(1)} all-to-all(bf16[32,16,128]{2,1,0:T(8,128)(2,1)S(1)} %get-tuple-element.81), channel_id=1, replica_groups=mesh['section'=8,'dom'=32] {'dom'}, dimensions={0} | all-to-all | bytes 262144 | tf_op jit(solution)/shard_map/all_to_all | solution.py:107
  328.8 11.2 %all_to_all.88.refs_2_ = bf16[32,16,128]{2,1,0:T(8,128)(2,1)S(1)} all-to-all(bf16[32,16,128]{2,1,0:T(8,128)(2,1)S(1)} %get-tuple-element.83), channel_id=1, replica_groups=mesh['section'=8,'dom'=32] {'dom'}, dimensions={0} | all-to-all | bytes 262144 | tf_op jit(solution)/shard_map/all_to_all | solution.py:107
  342.0 11.2 %all_to_all.89.refs_2_ = bf16[32,16,128]{2,1,0:T(8,128)(2,1)S(1)} all-to-all(bf16[32,16,128]{2,1,0:T(8,128)(2,1)S(1)} %get-tuple-element.85), channel_id=1, replica_groups=mesh['section'=8,'dom'=32] {'dom'}, dimensions={0} | all-to-all | bytes 262144 | tf_op jit(solution)/shard_map/all_to_all | solution.py:107
  355.8 3.9 %all-to-all-start.15 = ((bf16[32,16,128]{2,1,0:T(8,128)(2,1)}), bf16[32,16,128]{2,1,0:T(8,128)(2,1)S(1)}, u32[]{:S(2)}, u32[]{:S(2)}) async-start(bf16[32,16,128]{2,1,0:T(8,128)(2,1)} %get-tuple-element.87), calls=%async_computation.15 | async-start | bytes 262144 | tf_op jit(solution)/shard_map/all_to_all | solution.py:107
  359.8 7.8 %all-to-all-done.15.refs_2_ = bf16[32,16,128]{2,1,0:T(8,128)(2,1)S(1)} async-done(((bf16[32,16,128]{2,1,0:T(8,128)(2,1)}), bf16[32,16,128]{2,1,0:T(8,128)(2,1)S(1)}, u32[]{:S(2)}, u32[]{:S(2)}) %all-to-all-start.15) | async-done | bytes 131104 | tf_op jit(solution)/shard_map/all_to_all | solution.py:107
  (155 shorter events, 91.0 us)
Async XLA Ops:
  8.8 11.1 %copy-start.24 = (s32[2,1024,4]{1,2,0:T(4,128)S(1)}, s32[2,1024,4]{1,2,0:T(4,128)}, u32[]{:S(2)}) copy-start(s32[2,1024,4]{1,2,0:T(4,128)} %param.8) | copy-start | bytes 98308
  8.8 11.3 %copy-start.26 = (s32[2,32]{1,0:T(2,128)S(1)}, s32[2,32]{1,0:T(2,128)}, u32[]{:S(2)}) copy-start(s32[2,32]{1,0:T(2,128)} %param.9) | copy-start | bytes 772
  8.8 11.8 %copy-start.25 = (bf16[2,2048]{1,0:T(2,128)(2,1)S(1)}, bf16[2,2048]{1,0:T(2,128)(2,1)}, u32[]{:S(2)}) copy-start(bf16[2,2048]{1,0:T(2,128)(2,1)} %param.7) | copy-start | bytes 24580
  8.8 13.9 %copy-start.23 = (bf16[2,32,64,256]{3,2,1,0:T(8,128)(2,1)S(1)}, bf16[2,32,64,256]{3,2,1,0:T(8,128)(2,1)}, u32[]{:S(2)}) copy-start(bf16[2,32,64,256]{3,2,1,0:T(8,128)(2,1)} %param.6) | copy-start | bytes 6291460
  8.8 37.3 %collective-permute-start.1 = (bf16[32,16,128]{2,1,0:T(8,128)(2,1)}, bf16[32,16,128]{2,1,0:T(8,128)(2,1)}, u32[]{:S(2)}, u32[]{:S(2)}) collective-permute-start(bf16[32,16,128]{2,1,0:T(8,128)(2,1)} %reshape.126), channel_id=1, source_target_pairs={{64,0},{96,32},{65,1},{97,33},{66,2},{98,34},{67,3},{99,35},{68,4}... | collective-permute-start | bytes 393224 | tf_op jit(solution)/shard_map/ppermute | solution.py:162
  10.2 38.2 %collective-permute-start.2 = (bf16[32,16,128]{2,1,0:T(8,128)(2,1)}, bf16[32,16,128]{2,1,0:T(8,128)(2,1)}, u32[]{:S(2)}, u32[]{:S(2)}) collective-permute-start(bf16[32,16,128]{2,1,0:T(8,128)(2,1)} %reshape.126), channel_id=1, source_target_pairs={{128,0},{160,32},{129,1},{161,33},{130,2},{162,34},{131,3},{163,35... | collective-permute-start | bytes 393224 | tf_op jit(solution)/shard_map/ppermute | solution.py:162
  11.5 39.1 %collective-permute-start.3 = (bf16[32,16,128]{2,1,0:T(8,128)(2,1)}, bf16[32,16,128]{2,1,0:T(8,128)(2,1)}, u32[]{:S(2)}, u32[]{:S(2)}) collective-permute-start(bf16[32,16,128]{2,1,0:T(8,128)(2,1)} %reshape.126), channel_id=1, source_target_pairs={{192,0},{224,32},{193,1},{225,33},{194,2},{226,34},{195,3},{227,35... | collective-permute-start | bytes 393224 | tf_op jit(solution)/shard_map/ppermute | solution.py:162
  15.6 50.9 %collective-permute-start.4 = (bf16[32,64,256]{2,1,0:T(8,128)(2,1)S(1)}, bf16[32,64,256]{2,1,0:T(8,128)(2,1)}, u32[]{:S(2)}, u32[]{:S(2)}) collective-permute-start(bf16[32,64,256]{2,1,0:T(8,128)(2,1)S(1)} %get-tuple-element.96), channel_id=1, source_target_pairs={{0,32},{32,0},{1,33},{33,1},{2,34},{34,2},{3,35},{35,3},{4,36},{36... | collective-permute-start | bytes 3145736 | tf_op jit(solution)/shard_map/ppermute | solution.py:168
  20.6 24.1 %collective-permute-start = (bf16[2,3072]{1,0:T(2,128)(2,1)S(1)}, bf16[2,3072]{1,0:T(2,128)(2,1)S(1)}, u32[]{:S(2)}, u32[]{:S(2)}) collective-permute-start(bf16[2,3072]{1,0:T(2,128)(2,1)S(1)} %fusion.11), channel_id=1, source_target_pairs={{0,32},{32,0},{1,33},{33,1},{2,34},{34,2},{3,35},{35,3},{4,36},{36... | collective-permute-start | bytes 36872 | tf_op jit(solution)/shard_map/ppermute | solution.py:165
  44.7 42.3 %collective-permute-start.10 = (bf16[2,256,256]{2,1,0:T(8,128)(2,1)}, bf16[2,256,256]{2,1,0:T(8,128)(2,1)}, u32[]{:S(2)}, u32[]{:S(2)}) collective-permute-start(bf16[2,256,256]{2,1,0:T(8,128)(2,1)} %get-tuple-element.98), channel_id=1, source_target_pairs={{64,0},{96,32},{128,64},{160,96},{192,128},{224,160},{65,1},{97,33... | collective-permute-start | bytes 786440 | tf_op jit(solution)/shard_map/ppermute | solution.py:175
  46.1 42.2 %collective-permute-start.11 = (bf16[2,256,256]{2,1,0:T(8,128)(2,1)}, bf16[2,256,256]{2,1,0:T(8,128)(2,1)}, u32[]{:S(2)}, u32[]{:S(2)}) collective-permute-start(bf16[2,256,256]{2,1,0:T(8,128)(2,1)} %get-tuple-element.97), channel_id=1, source_target_pairs={{64,32},{96,64},{128,96},{160,128},{192,160},{224,192},{65,33},{97... | collective-permute-start | bytes 786440 | tf_op jit(solution)/shard_map/ppermute | solution.py:175
  48.4 41.2 %collective-permute-start.5 = (bf16[2,256,256]{2,1,0:T(8,128)(2,1)}, bf16[2,256,256]{2,1,0:T(8,128)(2,1)}, u32[]{:S(2)}, u32[]{:S(2)}) collective-permute-start(bf16[2,256,256]{2,1,0:T(8,128)(2,1)} %get-tuple-element.103), channel_id=1, source_target_pairs={{64,96},{96,128},{128,160},{160,192},{192,224},{224,0},{65,97},{97... | collective-permute-start | bytes 786440 | tf_op jit(solution)/shard_map/ppermute | solution.py:175
  50.6 85.1 %collective-permute-start.12 = (bf16[32,64,256]{2,1,0:T(8,128)(2,1)}, bf16[32,64,256]{2,1,0:T(8,128)(2,1)}, u32[]{:S(2)}, u32[]{:S(2)}) collective-permute-start(bf16[32,64,256]{2,1,0:T(8,128)(2,1)} %get-tuple-element.95), channel_id=1, source_target_pairs={{0,32},{32,0},{1,33},{33,1},{2,34},{34,2},{3,35},{35,3},{4,36},{36... | collective-permute-start | bytes 3145736 | tf_op jit(solution)/shard_map/ppermute | solution.py:168
  57.4 20.4 %all-to-all-start = ((bf16[32,64,128]{2,1,0:T(8,128)(2,1)}), bf16[32,64,128]{2,1,0:T(8,128)(2,1)S(1)}, u32[]{:S(2)}, u32[]{:S(2)}) async-start(bf16[32,64,128]{2,1,0:T(8,128)(2,1)} %broadcast_select_fusion.4), calls=%async_computation | async-start | bytes 1048576 | tf_op jit(solution)/shard_map/all_to_all | solution.py:107
  81.9 53.8 %all-to-all-start.1 = ((bf16[32,64,128]{2,1,0:T(8,128)(2,1)}), bf16[32,64,128]{2,1,0:T(8,128)(2,1)S(1)}, u32[]{:S(2)}, u32[]{:S(2)}) async-start(bf16[32,64,128]{2,1,0:T(8,128)(2,1)} %copy-done.9), calls=%async_computation.1 | async-start | bytes 1048576 | tf_op jit(solution)/shard_map/all_to_all | solution.py:107
  85.6 114.5 %all-gather.9.cloned.1.call-start = ((), (), s32[]{:S(2)}) async-start(), calls=%async_computation.16 | async-start | bytes 3686400 | tf_op jit(solution)/shard_map/all_gather | solution.py:196
  85.7 16.9 %collective-permute-start.6 = (bf16[2,256,256]{2,1,0:T(8,128)(2,1)}, bf16[2,256,256]{2,1,0:T(8,128)(2,1)S(1)}, u32[]{:S(2)}, u32[]{:S(2)}) collective-permute-start(bf16[2,256,256]{2,1,0:T(8,128)(2,1)} %get-tuple-element.102), channel_id=1, source_target_pairs={{64,128},{96,160},{128,192},{160,224},{192,0},{224,32},{65,129},{9... | collective-permute-start | bytes 786440 | tf_op jit(solution)/shard_map/ppermute | solution.py:175
  87.0 28.9 %collective-permute-start.7 = (bf16[2,256,256]{2,1,0:T(8,128)(2,1)}, bf16[2,256,256]{2,1,0:T(8,128)(2,1)S(1)}, u32[]{:S(2)}, u32[]{:S(2)}) collective-permute-start(bf16[2,256,256]{2,1,0:T(8,128)(2,1)} %get-tuple-element.101), channel_id=1, source_target_pairs={{64,160},{96,192},{128,224},{160,0},{192,32},{224,64},{65,161},{97... | collective-permute-start | bytes 786440 | tf_op jit(solution)/shard_map/ppermute | solution.py:175
  88.3 46.0 %collective-permute-start.8 = (bf16[2,256,256]{2,1,0:T(8,128)(2,1)}, bf16[2,256,256]{2,1,0:T(8,128)(2,1)S(1)}, u32[]{:S(2)}, u32[]{:S(2)}) collective-permute-start(bf16[2,256,256]{2,1,0:T(8,128)(2,1)} %get-tuple-element.100), channel_id=1, source_target_pairs={{64,192},{96,224},{128,0},{160,32},{192,64},{224,96},{65,193},{97,... | collective-permute-start | bytes 786440 | tf_op jit(solution)/shard_map/ppermute | solution.py:175
  89.6 45.4 %collective-permute-start.9 = (bf16[2,256,256]{2,1,0:T(8,128)(2,1)}, bf16[2,256,256]{2,1,0:T(8,128)(2,1)S(1)}, u32[]{:S(2)}, u32[]{:S(2)}) collective-permute-start(bf16[2,256,256]{2,1,0:T(8,128)(2,1)} %get-tuple-element.99), channel_id=1, source_target_pairs={{64,224},{96,0},{128,32},{160,64},{192,96},{224,128},{65,225},{97,... | collective-permute-start | bytes 786440 | tf_op jit(solution)/shard_map/ppermute | solution.py:175
  171.3 15.2 %all-to-all-start.3 = ((bf16[32,64,128]{2,1,0:T(8,128)(2,1)}), bf16[32,64,128]{2,1,0:T(8,128)(2,1)S(1)}, u32[]{:S(2)}, u32[]{:S(2)}) async-start(bf16[32,64,128]{2,1,0:T(8,128)(2,1)} %copy-done.10), calls=%async_computation.3 | async-start | bytes 1048576 | tf_op jit(solution)/shard_map/all_to_all | solution.py:107
  174.9 80.5 %all-gather.11.cloned.1.call-start = ((), (), s32[]{:S(2)}) async-start(), calls=%async_computation.17 | async-start | bytes 4718592 | tf_op jit(solution)/shard_map/all_gather | solution.py:208
  191.4 5.6 %collective-permute-start.13 = (bf16[32,16,128]{2,1,0:T(8,128)(2,1)S(1)}, bf16[32,16,128]{2,1,0:T(8,128)(2,1)S(1)}, u32[]{:S(2)}, u32[]{:S(2)}) collective-permute-start(bf16[32,16,128]{2,1,0:T(8,128)(2,1)S(1)} %get-tuple-element.106), channel_id=1, source_target_pairs={{0,64},{32,96},{1,65},{33,97},{2,66},{34,98},{3,67},{35,99},{4,68}... | collective-permute-start | bytes 393224 | tf_op jit(solution)/shard_map/ppermute | solution.py:204
  192.7 6.1 %collective-permute-start.14 = (bf16[32,16,128]{2,1,0:T(8,128)(2,1)S(1)}, bf16[32,16,128]{2,1,0:T(8,128)(2,1)S(1)}, u32[]{:S(2)}, u32[]{:S(2)}) collective-permute-start(bf16[32,16,128]{2,1,0:T(8,128)(2,1)S(1)} %get-tuple-element.105), channel_id=1, source_target_pairs={{0,128},{32,160},{1,129},{33,161},{2,130},{34,162},{3,131},{35,163... | collective-permute-start | bytes 393224 | tf_op jit(solution)/shard_map/ppermute | solution.py:204
  194.0 4.8 %collective-permute-start.15 = (bf16[32,16,128]{2,1,0:T(8,128)(2,1)S(1)}, bf16[32,16,128]{2,1,0:T(8,128)(2,1)S(1)}, u32[]{:S(2)}, u32[]{:S(2)}) collective-permute-start(bf16[32,16,128]{2,1,0:T(8,128)(2,1)S(1)} %get-tuple-element.107), channel_id=1, source_target_pairs={{0,192},{32,224},{1,193},{33,225},{2,194},{34,226},{3,195},{35,227... | collective-permute-start | bytes 393224 | tf_op jit(solution)/shard_map/ppermute | solution.py:204
  198.8 108.1 %all-gather.13.cloned.1.call-start = ((), (), s32[]{:S(2)}) async-start(), calls=%async_computation.18 | async-start | bytes 4718592 | tf_op jit(solution)/shard_map/all_gather | solution.py:208
  199.5 160.2 %all-gather.15.cloned.1.call-start = ((), (), s32[]{:S(2)}) async-start(), calls=%async_computation.19 | async-start | bytes 1179648 | tf_op jit(solution)/shard_map/all_gather | solution.py:208
  202.6 11.5 %all-to-all-start.4 = ((bf16[32,16,128]{2,1,0:T(8,128)(2,1)}), bf16[32,16,128]{2,1,0:T(8,128)(2,1)S(1)}, u32[]{:S(2)}, u32[]{:S(2)}) async-start(bf16[32,16,128]{2,1,0:T(8,128)(2,1)} %broadcast_select_fusion.5), calls=%async_computation.4 | async-start | bytes 262144 | tf_op jit(solution)/shard_map/all_to_all | solution.py:107
  257.6 13.3 %copy-start.3 = (bf16[8192,256]{1,0:T(8,128)(2,1)S(1)}, bf16[8192,256]{1,0:T(8,128)(2,1)}, u32[]{:S(2)}) copy-start(bf16[8192,256]{1,0:T(8,128)(2,1)} %all-gather.11.cloned.1.call-done) | copy-start | bytes 12582916
  299.9 11.7 %all-to-all-start.11 = ((bf16[32,16,128]{2,1,0:T(8,128)(2,1)}), bf16[32,16,128]{2,1,0:T(8,128)(2,1)S(1)}, u32[]{:S(2)}, u32[]{:S(2)}) async-start(bf16[32,16,128]{2,1,0:T(8,128)(2,1)} %get-tuple-element.78), calls=%async_computation.11 | async-start | bytes 262144 | tf_op jit(solution)/shard_map/all_to_all | solution.py:107
  313.7 13.2 %copy-start.1 = (bf16[8192,256]{1,0:T(8,128)(2,1)S(1)}, bf16[8192,256]{1,0:T(8,128)(2,1)}, u32[]{:S(2)}) copy-start(bf16[8192,256]{1,0:T(8,128)(2,1)} %all-gather.13.cloned.1.call-done) | copy-start | bytes 12582916
  355.8 11.7 %all-to-all-start.15 = ((bf16[32,16,128]{2,1,0:T(8,128)(2,1)}), bf16[32,16,128]{2,1,0:T(8,128)(2,1)S(1)}, u32[]{:S(2)}, u32[]{:S(2)}) async-start(bf16[32,16,128]{2,1,0:T(8,128)(2,1)} %get-tuple-element.87), calls=%async_computation.15 | async-start | bytes 262144 | tf_op jit(solution)/shard_map/all_to_all | solution.py:107
  (21 other events, 26.0 us)
Sparse Core Ops, SparseCore 0:
  142.6 42.2 all-gather.8
  198.9 52.7 all-gather.10
  253.5 53.3 all-gather.12
  308.6 32.8 all-gather.14
